TPU v7x, 32 devices: a whole 2x2x4 slice. The times are simulated.
32 devices in a mesh: fault: 16 (over z, x, core), member: 2 (over y).
Axes of the slice: x: 2, y: 2, z: 4, core: 2. Of those that a mesh axis runs over, the one named last changes fastest.
Arguments:
- log_rate: float32 [8, 16384], P('member', 'fault'), may hold values from -2.5 to 2.5
- log_state: float32 [8, 16384], P('member', 'fault'), may hold values from -2.5 to 2.5
- direct_effect: float32 [8, 16384], P('member', 'fault'), may hold values from 0.01 to 0.03
- evolution_effect: float32 [8, 16384], P('member', 'fault'), may hold values from 0.01 to 0.04
- slip_distance: float32 [8, 16384], P('member', 'fault'), may hold values from 0.5 to 2
- normal_stress: float32 [16384], P('fault'), may hold values from 10 to 40
- near_blocks: bfloat16 [128, 24, 128, 128], P(('fault', 'member')), may hold values from -0.25 to 0.25
- near_columns: int32 [128, 24], P(('fault', 'member')), may hold values from 0 to 127, as said below
- near_count: int32 [128], P(('fault', 'member')), may hold values from 1 to 24, as said below
- far_clusters: int32 [128, 3], P(('fault', 'member')), may hold values from 0 to 3, as said below
- far_basis: bfloat16 [128, 3, 32, 128], P(('fault', 'member')), may hold values from -0.625 to 0.625
- column_basis: bfloat16 [32, 16384], P(None, ('fault', 'member')), may hold values from -0.09375 to 0.09375
Outputs:
- rate_next: float32 [8, 16384], P('member', 'fault')
- state_next: float32 [8, 16384], P('member', 'fault')
Inputs may be any that keep to these rules, and one draw needn't show every extreme that they name: `near_columns`: slot 0 of row p holds p; the slots of a row hold distinct block indices, all among the 8 block rows of p's index of fault and of the indices before and after it, counted periodically. `near_count`: slots at or beyond the count are ignored; every row of at least one index of fault has all 24 slots live. `far_clusters`: the clusters of one row are distinct.
All inputs are finite; a program needn't handle non-finite values.
Results may differ from a plain program's by a relative error of at most 0.0019.
Values may be sent and summed in bfloat16 or wider, within the bound.
No kernel may reach another device: no remote copies, remote signals or barrier semaphores. Data moves between devices by JAX's collectives and lax.ppermute only.
A program may use at most 64 MiB of HBM per device.

v0:
```python
import jax
import jax.numpy as jnp
from jax import lax
from jax.sharding import PartitionSpec as P

PANEL = 128
GROUP = 4


damping = 0.5
time_step = 0.25


def with_halo(cells, sides, width):
    for axis, dim in sides:
        count = lax.axis_size(axis)
        head = lax.slice_in_dim(cells, 0, width, axis=dim)
        tail = lax.slice_in_dim(cells, cells.shape[dim] - width, cells.shape[dim], axis=dim)
        cells = jnp.concatenate(
            [
                lax.ppermute(tail, axis, [(i, (i + 1) % count) for i in range(count)]),
                cells,
                lax.ppermute(head, axis, [((i + 1) % count, i) for i in range(count)]),
            ],
            axis=dim,
        )
    return cells


def swapped(block, axis, distance):
    count = lax.axis_size(axis)
    route = []
    for low in range(count):
        high = low | 1 << distance
        if high != low and high < count:
            route += [(low, high), (high, low)]
    return lax.ppermute(block, axis, route)


def per_device(
    log_rate,
    log_state,
    direct_effect,
    evolution_effect,
    slip_distance,
    normal_stress,
    near_blocks,
    near_columns,
    near_count,
    far_clusters,
    far_basis,
    column_basis,
):
    fault_count = lax.axis_size("fault")
    fault_pos = lax.axis_index("fault")
    member_pos = lax.axis_index("member")
    elements = log_rate.shape[1]
    own_panels = elements // PANEL
    total_panels = own_panels * fault_count
    row_count = near_blocks.shape[0]
    row_width = row_count * PANEL
    velocity = jnp.exp(log_rate)
    deficit = (1.0 - velocity).astype(jnp.bfloat16)
    rates_all = lax.all_gather(deficit, "member", axis=0, tiled=True)
    window = with_halo(rates_all, (("fault", 1),), elements)
    members = rates_all.shape[0]
    own_rows = lax.dynamic_slice_in_dim(rates_all, member_pos * row_width, row_width, 1)
    partial_value = lax.dot_general(
        column_basis, own_rows, (((1,), (1,)), ((), ())), preferred_element_type=jnp.float32
    )
    cluster_total = fault_count // GROUP
    rank_size = partial_value.shape[0]
    group_total = lax.psum(partial_value, "member")
    for bit in range(GROUP.bit_length() - 1):
        group_total = group_total + swapped(group_total, "fault", bit)
    group_rounded = group_total.astype(jnp.bfloat16)
    piece_rows = rank_size // GROUP
    own_piece = lax.dynamic_slice_in_dim(
        group_rounded, fault_pos % GROUP * piece_rows, piece_rows, 0
    )
    gathered = lax.all_gather(own_piece, "fault", axis=0, tiled=True)
    coeff_table = gathered.reshape(cluster_total, rank_size, members).astype(jnp.float32)
    local_cols = (near_columns - (fault_pos - 1) * own_panels) % total_panels
    panel_view = window.reshape(members, -1, PANEL)
    zero_value = jnp.zeros((), jnp.bfloat16)
    active = jnp.arange(near_columns.shape[1])[None, :] < near_count[:, None]
    picked = panel_view[:, local_cols, :]
    picked = jnp.where(active[None, :, :, None], picked, zero_value)
    near_field = jnp.einsum(
        "mrsj,rsje->mre", picked, near_blocks, preferred_element_type=jnp.float32
    )
    chooser = (far_clusters[:, :, None] == jnp.arange(cluster_total)[None, None, :]).astype(
        jnp.float32
    )
    chosen = jnp.einsum(
        "rkc,cqm->rkqm", chooser, coeff_table, precision=lax.Precision.HIGHEST
    ).astype(jnp.bfloat16)
    far_field = jnp.einsum("rkqm,rkqe->mre", chosen, far_basis, preferred_element_type=jnp.float32)
    stress_rate = (near_field + far_field).reshape(members, row_width)
    stress_own = lax.all_to_all(stress_rate, "member", split_axis=0, concat_axis=1, tiled=True)
    state_rate = (jnp.exp(-log_state) - velocity) / slip_distance
    rate_change = (stress_own - normal_stress[None, :] * evolution_effect * state_rate) / (
        normal_stress[None, :] * direct_effect + damping * velocity
    )
    return (log_rate + time_step * rate_change, log_state + time_step * state_rate)


def solution(mesh):
    return jax.shard_map(
        per_device,
        mesh=mesh,
        in_specs=(
            P("member", "fault"),
            P("member", "fault"),
            P("member", "fault"),
            P("member", "fault"),
            P("member", "fault"),
            P("fault"),
            P(("fault", "member"), None, None, None),
            P(("fault", "member"), None),
            P(("fault", "member")),
            P(("fault", "member"), None),
            P(("fault", "member"), None, None, None),
            P(None, ("fault", "member")),
        ),
        out_specs=(P("member", "fault"), P("member", "fault")),
        check_vma=False,
    )
```

profile of v0, /device:TPU:0, one launch (start us, length us, event | category | flops | bytes accessed | tf_op | source)
XLA Modules:
  0.0 52.7 jit_solution(961719658011298488)
XLA Ops:
  0.6 0.0 copy-start
  0.6 0.0 copy-start.1
  0.7 0.0 copy-start.2
  0.7 0.0 copy-start.4
  0.7 0.0 copy-start.5
  0.7 0.0 copy-start.3
  0.7 0.0 copy-start.6
  0.7 0.9 %fusion.7 = bf16[1,4,1024]{2,1,0:T(4,128)(2,1)S(1)} fusion(f32[4,1024]{1,0:T(4,128)} %param.12), kind=kLoop, calls=%fused_computation.18 | loop fusion | flops 8192 | bytes 24576
  1.6 5.4 %all-gather = bf16[2,4,1024]{2,1,0:T(4,128)(2,1)S(1)} all-gather(bf16[1,4,1024]{2,1,0:T(4,128)(2,1)S(1)} %fusion.7), channel_id=1, replica_groups=mesh['fault'=16,'member'=2] {'member'}, dimensions={0}, use_global_device_ids=true | all-gather | bytes 24576 | tf_op jit(solution)/shard_map/all_gather | solution.py:64
  7.0 0.1 collective-permute-start
  7.1 4.4 %collective-permute-start.1 = (bf16[8,1024]{1,0:T(8,128)(2,1)S(1)}, bf16[8,1024]{1,0:T(8,128)(2,1)S(1)}, u32[]{:S(2)}, u32[]{:S(2)}) collective-permute-start(bf16[8,1024]{1,0:T(8,128)(2,1)S(1)} %reshape.51), channel_id=1, source_target_pairs={{2,0},{4,2},{6,4},{8,6},{10,8},{12,10},{14,12},{16,14},{18,16},{20... | collective-permute-start | bytes 49160 | tf_op jit(solution)/shard_map/ppermute | solution.py:23
  11.5 0.9 %convolution_bitcast_fusion.2 = f32[32,8]{0,1:T(8,128)S(1)} fusion(bf16[32,512]{1,0:T(8,128)(2,1)} %param.23, bf16[8,1024]{1,0:T(8,128)(2,1)S(1)} %reshape.51, s32[]{:T(128)S(6)} %select_n.29), kind=kOutput, calls=%fused_computation.6 | convolution fusion | flops 262144 | bytes 41988 | tf_op jit(solution)/shard_map/dot_general | solution.py:68
  12.4 4.9 %psum.7 = f32[32,8]{0,1:T(8,128)S(1)} all-reduce(f32[32,8]{0,1:T(8,128)S(1)} %convolution_bitcast_fusion.2), channel_id=1, replica_groups=mesh['fault'=16,'member'=2] {'member'}, use_global_device_ids=true, to_apply=%region_0.0 | all-reduce | flops 256 | bytes 2048 | tf_op jit(solution)/shard_map/psum | solution.py:73
  17.3 0.0 collective-permute-start.2
  17.3 0.7 %compare_select_fusion = s32[4,24]{1,0:T(4,128)S(1)} fusion(s32[4,24]{1,0:T(4,128)} %param.19, s32[]{:T(128)S(6)} %mul.38), kind=kLoop, calls=%fused_computation.23 | loop fusion | flops 1440 | bytes 772 | tf_op jit(solution)/shard_map/select_n | solution.py:87
  18.0 0.7 %iota_compare_fusion.1 = pred[4,24]{1,0:T(4,128)(4,1)S(1)} fusion(s32[4]{0:T(128)} %param.20), kind=kLoop, calls=%fused_computation.31 | loop fusion | flops 96 | bytes 112 | tf_op jit(solution)/shard_map/lt | solution.py:86
  18.7 0.1 reshape.42
  18.8 0.0 collective-permute-done.2
  18.8 0.1 collective-permute-start.3
  18.9 3.6 %collective-permute-done.3 = f32[32,8]{0,1:T(8,128)S(1)} collective-permute-done((f32[32,8]{0,1:T(8,128)S(1)}, f32[32,8]{0,1:T(8,128)S(1)}, u32[]{:S(2)}, u32[]{:S(2)}) %collective-permute-start.3) | collective-permute-done | bytes 1056 | tf_op jit(solution)/shard_map/ppermute | solution.py:37
  22.5 0.1 constant_dynamic-slice_fusion
  22.6 0.1 copy.15
  22.7 19.5 %all_gather.7 = bf16[128,8]{1,0:T(8,128)(2,1)S(1)} all-gather(bf16[8,8]{1,0:T(8,128)(2,1)S(1)} %copy.15), channel_id=1, replica_groups=mesh['fault'=16,'member'=2] {'fault'}, dimensions={0}, use_global_device_ids=true | all-gather | bytes 2176 | tf_op jit(solution)/shard_map/all_gather | solution.py:81
  42.2 0.1 copy.22
  42.3 0.9 %convolution_convert_fusion = bf16[4,3,32,8]{2,1,3,0:T(4,128)(2,1)S(1)} fusion(bf16[4,32,8]{1,0,2:T(4,128)(2,1)S(1)} %copy.22, s32[4,3]{1,0:T(4,128)} %param.21), kind=kOutput, calls=%fused_computation.1 | convolution fusion | flops 27696 | bytes 8240 | tf_op jit(solution)/shard_map/rkc,cqm->rkqm/dot_general | solution.py:95
  43.2 1.1 %convolution_bitcast_fusion.1 = f32[4,8,128]{2,1,0:T(8,128)S(1)} fusion(bf16[4,3,32,128]{3,2,1,0:T(8,128)(2,1)} %param.22, bf16[4,3,32,8]{2,1,3,0:T(4,128)(2,1)S(1)} %convolution_convert_fusion), kind=kOutput, calls=%fused_computation.5 | convolution fusion | flops 786432 | bytes 120832 | tf_op jit(solution)/shard_map/rkqm,rkqe->mre/dot_general | solution.py:98
  44.2 0.0 collective-permute-done
  44.2 0.0 collective-permute-done.1
  44.3 0.7 %gather_fusion = bf16[96,8,128]{2,1,0:T(8,128)(2,1)S(1)} fusion(bf16[8,24,128]{2,0,1:T(8,128)(2,1)S(1)} %maximum_bitcast_fusion, s32[1024]{0:T(1024)S(1)} %pad_clamp_fusion), kind=kCustom, calls=%fused_computation | custom fusion | bytes 393600 | tf_op jit(solution)/shard_map/gather | solution.py:87
  44.9 0.0 copy-done
  44.9 0.6 %fusion.1 = f32[8,4,128]{2,0,1:T(8,128)S(1)} fusion(f32[4,8,128]{2,1,0:T(8,128)S(1)} %convolution_bitcast_fusion.1, bf16[4,24,128,128]{3,2,1,0:T(8,128)(2,1)S(1)} %copy-done, bf16[4,24,8,128]{3,2,1,0:T(8,128)(2,1)S(1)} %bitcast.37, pred[4,24]{1,0:T(4,128)(4,1)S(1)} %iota_compare_fusion.1), kind=kOutput, calls=%fused_computation.4 | convolution fusion | flops 25268224 | bytes 3375200 | tf_op jit(solution)/shard_map/mrsj,rsje->mre/dot_general | solution.py:89
  45.6 6.5 %all_to_all.19 = f32[2,4,512]{2,1,0:T(4,128)S(1)} all-to-all(f32[2,4,512]{2,1,0:T(4,128)S(1)} %all_to_all.14), channel_id=1, replica_groups=mesh['fault'=16,'member'=2] {'member'}, dimensions={0} | all-to-all | bytes 32768 | tf_op jit(solution)/shard_map/all_to_all | solution.py:100
  52.0 0.0 copy-done.1
  52.0 0.0 copy-done.2
  52.0 0.0 copy-done.4
  52.0 0.0 copy-done.5
  52.0 0.0 copy-done.3
  52.0 0.0 copy-done.6
  52.0 0.6 %multiply_add_fusion = (f32[4,1024]{1,0:T(4,128)}, f32[4,1024]{1,0:T(4,128)}) fusion(f32[4,1024]{1,0:T(4,128)S(1)} %copy-done.2, f32[4,1024]{1,0:T(4,128)S(1)} %copy-done.3, f32[4,1024]{1,0:T(4,128)S(1)} %copy-done.1, f32[4,1024]{1,0:T(4,128)S(1)} %copy-done.4, f32[4,1024]{1,0:T(4,128)S(1)} %bitcast.39, f32[4,1024]{1,0:T(4,128)S(1)} %copy-done.5, ...), kind=kLoop, calls=%fused_computation.13 | loop fusion | flops 57344 | bytes 135168 | tf_op jit(solution)/shard_map/add | solution.py:105
  (7 shorter events, 0.1 us)
Async XLA Ops:
  0.6 44.3 %copy-start = (bf16[4,24,128,128]{3,2,1,0:T(8,128)(2,1)S(1)}, bf16[4,24,128,128]{3,2,1,0:T(8,128)(2,1)}, u32[]{:S(2)}) copy-start(bf16[4,24,128,128]{3,2,1,0:T(8,128)(2,1)} %param.18) | copy-start | bytes 9437188
  0.6 51.4 %copy-start.1 = (f32[4,1024]{1,0:T(4,128)S(1)}, f32[4,1024]{1,0:T(4,128)}, u32[]{:S(2)}) copy-start(f32[4,1024]{1,0:T(4,128)} %param.12) | copy-start | bytes 49156
  0.7 51.4 %copy-start.2 = (f32[4,1024]{1,0:T(4,128)S(1)}, f32[4,1024]{1,0:T(4,128)}, u32[]{:S(2)}) copy-start(f32[4,1024]{1,0:T(4,128)} %param.13) | copy-start | bytes 49156
  0.7 51.3 %copy-start.4 = (f32[4,1024]{1,0:T(4,128)S(1)}, f32[4,1024]{1,0:T(4,128)}, u32[]{:S(2)}) copy-start(f32[4,1024]{1,0:T(4,128)} %param.14) | copy-start | bytes 49156
  0.7 51.3 %copy-start.5 = (f32[4,1024]{1,0:T(4,128)S(1)}, f32[4,1024]{1,0:T(4,128)}, u32[]{:S(2)}) copy-start(f32[4,1024]{1,0:T(4,128)} %param.15) | copy-start | bytes 49156
  0.7 51.3 %copy-start.3 = (f32[4,1024]{1,0:T(4,128)S(1)}, f32[4,1024]{1,0:T(4,128)}, u32[]{:S(2)}) copy-start(f32[4,1024]{1,0:T(4,128)} %param.16) | copy-start | bytes 49156
  0.7 51.3 %copy-start.6 = (f32[1024]{0:T(1024)S(1)}, f32[1024]{0:T(1024)}, u32[]{:S(2)}) copy-start(f32[1024]{0:T(1024)} %param.17) | copy-start | bytes 12292
  7.0 37.2 %collective-permute-start = (bf16[8,1024]{1,0:T(8,128)(2,1)S(1)}, bf16[8,1024]{1,0:T(8,128)(2,1)S(1)}, u32[]{:S(2)}, u32[]{:S(2)}) collective-permute-start(bf16[8,1024]{1,0:T(8,128)(2,1)S(1)} %reshape.51), channel_id=1, source_target_pairs={{0,2},{2,4},{4,6},{6,8},{8,10},{10,12},{12,14},{14,16},{16,18},{18... | collective-permute-start | bytes 49160 | tf_op jit(solution)/shard_map/ppermute | solution.py:21
  7.1 37.2 %collective-permute-start.1 = (bf16[8,1024]{1,0:T(8,128)(2,1)S(1)}, bf16[8,1024]{1,0:T(8,128)(2,1)S(1)}, u32[]{:S(2)}, u32[]{:S(2)}) collective-permute-start(bf16[8,1024]{1,0:T(8,128)(2,1)S(1)} %reshape.51), channel_id=1, source_target_pairs={{2,0},{4,2},{6,4},{8,6},{10,8},{12,10},{14,12},{16,14},{18,16},{20... | collective-permute-start | bytes 49160 | tf_op jit(solution)/shard_map/ppermute | solution.py:23
  17.3 1.5 %collective-permute-start.2 = (f32[32,8]{0,1:T(8,128)S(1)}, f32[32,8]{0,1:T(8,128)S(1)}, u32[]{:S(2)}, u32[]{:S(2)}) collective-permute-start(f32[32,8]{0,1:T(8,128)S(1)} %psum.7), channel_id=1, source_target_pairs={{0,2},{2,0},{4,6},{6,4},{8,10},{10,8},{12,14},{14,12},{16,18},{18,... | collective-permute-start | bytes 3080 | tf_op jit(solution)/shard_map/ppermute | solution.py:37
  18.8 3.7 %collective-permute-start.3 = (f32[32,8]{0,1:T(8,128)S(1)}, f32[32,8]{0,1:T(8,128)S(1)}, u32[]{:S(2)}, u32[]{:S(2)}) collective-permute-start(f32[32,8]{0,1:T(8,128)S(1)} %add.50), channel_id=1, source_target_pairs={{0,4},{4,0},{2,6},{6,2},{8,12},{12,8},{10,14},{14,10},{16,20},{20,... | collective-permute-start | bytes 3080 | tf_op jit(solution)/shard_map/ppermute | solution.py:37
where the time goes:
time: 53.1 us; the launch traced here: 52.7 us
  blocking collectives  36.3 us (68%)
  starting transfers between devices  4.56 us (9%)
  waiting for transfers between devices  3.57 us (7%)
  matrix products  3.42 us (6%)
  other arithmetic  2.97 us (6%)
  local copies, waits for them, and re-layouts  1.08 us (2%)
  between operations  0.8 us (2%)
    all_gather x1, blocking collectives, per_device(): gathered = lax.all_gather(own_piece, 'fault', axis=0, tiled=True)  19.5 us
    all_to_all x1, blocking collectives, per_device(): lax.all_to_all(stress_rate, 'member', split_axis=0, concat_axis=1, tiled=...  6.45 us
    all_gather x1, blocking collectives, per_device(): rates_all = lax.all_gather(deficit, 'member', axis=0, tiled=True)  5.41 us
    psum x1, blocking collectives, per_device(): group_total = lax.psum(partial_value, 'member')  4.93 us
    ppermute x1, starting transfers between devices, with_halo(): lax.ppermute(head, axis, [((i + 1) % count, i) for i in range(count)])  4.43 us
    ppermute x2, waiting for transfers between devices, swapped(): return lax.ppermute(block, axis, route)  3.57 us
    dot_general x1, matrix products, per_device(): jnp.einsum('rkqm,rkqe->mre', chosen, far_basis, preferred_element_type=jn...  1.09 us
  transfers between devices with their start and end apart: 4, of which 1 were waited for; matrix products, arithmetic and copies ran while one was open for 9% of the time, Pallas kernels for 0%

commit v1 on v0

v1 whole, which is shorter than its diff:
```python
import jax
import jax.numpy as jnp
from jax import lax
from jax.sharding import PartitionSpec as P

PANEL = 128
GROUP = 4


damping = 0.5
time_step = 0.25


def swapped(block, axis, partner):
    count = lax.axis_size(axis)
    return lax.ppermute(block, axis, [(i, partner(i) % count) for i in range(count)])


def per_device(
    log_rate,
    log_state,
    direct_effect,
    evolution_effect,
    slip_distance,
    normal_stress,
    near_blocks,
    near_columns,
    near_count,
    far_clusters,
    far_basis,
    column_basis,
):
    fault_count = lax.axis_size("fault")
    member_count = lax.axis_size("member")
    fault_pos = lax.axis_index("fault")
    member_pos = lax.axis_index("member")
    local_members, elements = log_rate.shape
    own_panels = elements // PANEL
    total_panels = own_panels * fault_count
    row_count, slots = near_columns.shape
    row_width = row_count * PANEL
    rank_size = column_basis.shape[0]
    cluster_total = fault_count // GROUP
    bf16, f32 = jnp.bfloat16, jnp.float32
    pair = member_count == 2

    def gathered(block):
        if pair:
            return jnp.stack([block, swapped(block, "member", lambda i: i ^ 1)])
        return lax.all_gather(block, "member", axis=0)

    def in_order(stacked):
        if pair:
            flip = member_pos == 1
            return jnp.where(flip, stacked[::-1], stacked)
        return stacked

    log_rate_all = gathered(log_rate)
    column_all = gathered(column_basis)
    far_by_cluster = jnp.zeros((row_count, cluster_total, rank_size, PANEL), bf16)
    for k in range(far_clusters.shape[1]):
        mine = far_clusters[:, k, None] == jnp.arange(cluster_total)[None, :]
        far_by_cluster = jnp.where(mine[:, :, None, None], far_basis[:, k, None], far_by_cluster)
    far_all = gathered(far_by_cluster.reshape(row_count, cluster_total * rank_size, PANEL))

    velocity = jnp.exp(log_rate)
    deficit = (1.0 - velocity).astype(bf16)
    deficit_all = (1.0 - jnp.exp(log_rate_all)).astype(bf16)
    members = member_count * local_members
    deficit_all = deficit_all.reshape(members, elements)
    columns = jnp.moveaxis(in_order(column_all), 0, 1).reshape(rank_size, elements)
    partial_value = lax.dot_general(
        deficit, columns, (((1,), (1,)), ((), ())), preferred_element_type=f32
    )

    near_side = swapped(deficit_all, "fault", lambda i: i ^ 1)
    total = partial_value + swapped(partial_value, "fault", lambda i: i ^ 1)
    far_side = swapped(deficit_all, "fault", lambda i: i + 1 if i % 2 else i - 1)
    bit = 2
    while bit < GROUP:
        total = total + swapped(total, "fault", lambda i: i ^ bit)
        bit *= 2
    table = total.astype(bf16)[None]
    while bit < fault_count:
        other = swapped(table, "fault", lambda i: i ^ bit)
        upper = (fault_pos // bit) % 2 == 1
        table = jnp.where(upper, jnp.concatenate([other, table]), jnp.concatenate([table, other]))
        bit *= 2

    offset = (near_columns - (fault_pos - 1) * own_panels) % total_panels
    side = offset // own_panels
    odd = fault_pos % 2
    place = jnp.where(side == 1, 0, jnp.where((side == 0) == (odd == 1), 1, 2))
    local_cols = place * own_panels + offset % own_panels
    window = jnp.concatenate([deficit_all, near_side, far_side], axis=1)
    panel_view = window.reshape(members, -1, PANEL)
    active = jnp.arange(slots)[None, :] < near_count[:, None]
    picked = panel_view[:, local_cols, :]
    picked = jnp.where(active[None, :, :, None], picked, jnp.zeros((), bf16))
    near_field = jnp.einsum("mrsj,rsje->mre", picked, near_blocks, preferred_element_type=f32)
    near_field = near_field.reshape(member_count, local_members, row_width)
    if pair:
        near_other = swapped(near_field[1], "member", lambda i: i ^ 1)
        near_rows = jnp.stack([near_field[0], near_other])
    else:
        near_rows = lax.all_to_all(near_field, "member", 0, 0)

    chosen = jnp.moveaxis(table, 1, 0).reshape(local_members, cluster_total * rank_size)
    far_rows = jnp.einsum("mk,hrke->hmre", chosen, far_all, preferred_element_type=f32)
    stress = near_rows + far_rows.reshape(member_count, local_members, row_width)
    stress = jnp.moveaxis(in_order(stress), 0, 1).reshape(local_members, elements)
    state_rate = (jnp.exp(-log_state) - velocity) / slip_distance
    rate_change = (stress - normal_stress[None, :] * evolution_effect * state_rate) / (
        normal_stress[None, :] * direct_effect + damping * velocity
    )
    return (log_rate + time_step * rate_change, log_state + time_step * state_rate)


def solution(mesh):
    return jax.shard_map(
        per_device,
        mesh=mesh,
        in_specs=(
            P("member", "fault"),
            P("member", "fault"),
            P("member", "fault"),
            P("member", "fault"),
            P("member", "fault"),
            P("fault"),
            P(("fault", "member"), None, None, None),
            P(("fault", "member"), None),
            P(("fault", "member")),
            P(("fault", "member"), None),
            P(("fault", "member"), None, None, None),
            P(None, ("fault", "member")),
        ),
        out_specs=(P("member", "fault"), P("member", "fault")),
        check_vma=False,
    )
```

time: 53.1 us -> 36.9 us (0.69)
  blocking collectives: 36.3 us -> 0 us
  waiting for transfers between devices: 3.57 us -> 10.4 us
  starting transfers between devices: 4.56 us -> 10.4 us
  other arithmetic: 2.97 us -> 8.15 us
  local copies, waits for them, and re-layouts: 1.08 us -> 3.41 us
    all_gather x2 -> x0, blocking collectives: 24.9 us -> none  [the longest x1 19.5 us: per_device(): gathered = lax.all_gather(own_piece, 'fault', axis=0, tiled=True)]
    ppermute x4 -> x10, waiting for transfers between devices: 3.57 us -> 10.4 us  [swapped(): lax.ppermute(block, axis, [(i, partner(i) % count) for i in range(count)])]
    all_to_all x1 -> x0, blocking collectives: 6.45 us -> none  [per_device(): lax.all_to_all(stress_rate, 'member', split_axis=0, concat_axis=1, tiled=...]
    ppermute x4 -> x10, starting transfers between devices: 4.56 us -> 10.4 us  [swapped(): lax.ppermute(block, axis, [(i, partner(i) % count) for i in range(count)])]
    psum x1 -> x0, blocking collectives: 4.93 us -> none  [per_device(): group_total = lax.psum(partial_value, 'member')]
    broadcast_in_dim x0 -> x10, local copies, waits for them, and re-layouts: none -> 1.37 us  [per_device(): jnp.where(mine[:, :, None, None], far_basis[:, k, None], far_by_cluster)]
    select_n x0 -> x4, other arithmetic: none -> 1.2 us  [the longest x2 1.19 us: per_device(): jnp.where(mine[:, :, None, None], far_basis[:, k, None], far_by_cluster)]
    slice x0 -> x2, local copies, waits for them, and re-layouts: none -> 1.01 us  [the longest x1 1.01 us: per_device(): mine = far_clusters[:, k, None] == jnp.arange(cluster_total)[None, :]]
  transfers between devices with their start and end apart: 4 -> 10, of which waited for: 1 -> 4; matrix products, arithmetic and copies ran while one was open for 9% -> 34% of each run, Pallas kernels for 0% -> 0%
where the time goes in v1:
time: 36.9 us; the launch traced here: 36.3 us
  starting transfers between devices  10.4 us (28%)
  waiting for transfers between devices  10.4 us (28%)
  other arithmetic  8.15 us (22%)
  local copies, waits for them, and re-layouts  3.41 us (9%)
  matrix products  3.15 us (9%)
  between operations  0.81 us (2%)
    ppermute x10, starting transfers between devices, swapped(): lax.ppermute(block, axis, [(i, partner(i) % count) for i in range(count)])  10.4 us
    ppermute x10, waiting for transfers between devices, swapped(): lax.ppermute(block, axis, [(i, partner(i) % count) for i in range(count)])  10.4 us
    broadcast_in_dim x10, local copies, waits for them, and re-layouts, per_device(): jnp.where(mine[:, :, None, None], far_basis[:, k, None], far_by_cluster)  1.37 us
    add x1, other arithmetic, per_device(): log_state + time_step * state_rate  1.36 us
    lt x1, other arithmetic, per_device(): active = jnp.arange(slots)[None, :] < near_count[:, None]  1.32 us
    dot_general x1, matrix products, per_device(): jnp.einsum('mrsj,rsje->mre', picked, near_blocks, preferred_element_type=...  1.24 us
    select_n x2, other arithmetic, per_device(): jnp.where(mine[:, :, None, None], far_basis[:, k, None], far_by_cluster)  1.19 us
    dot_general x1, matrix products, per_device(): jnp.einsum('mk,hrke->hmre', chosen, far_all, preferred_element_type=f32)  1.05 us
  transfers between devices with their start and end apart: 10, of which 4 were waited for; matrix products, arithmetic and copies ran while one was open for 34% of the time, Pallas kernels for 0%

profile of v1, /device:TPU:0, one launch (start us, length us, event | category | flops | bytes accessed | tf_op | source)
XLA Modules:
  0.0 36.3 jit_solution(17896169094291125904)
XLA Ops:
  0.6 0.0 copy-start
  0.6 3.0 %collective-permute-start.5 = (bf16[32,512]{1,0:T(8,128)(2,1)}, bf16[32,512]{1,0:T(8,128)(2,1)S(1)}, u32[]{:S(2)}, u32[]{:S(2)}) collective-permute-start(bf16[32,512]{1,0:T(8,128)(2,1)} %param.23), channel_id=1, source_target_pairs={{0,1},{1,0},{2,3},{3,2},{4,5},{5,4},{6,7},{7,6},{8,9},{9,8},{10,11... | collective-permute-start | bytes 98312 | tf_op jit(solution)/shard_map/ppermute | solution.py:16
  3.7 0.1 collective-permute-start
  3.8 1.0 %slice_reduce_fusion.2 = (s32[4]{0:T(128)S(1)}, s32[4]{0:T(128)S(1)}, s32[4]{0:T(128)S(1)}) fusion(s32[4,3]{1,0:T(4,128)} %param.21), kind=kLoop, calls=%fused_computation.56 | loop fusion | bytes 96 | tf_op jit(solution)/shard_map/slice | solution.py:62
  4.8 0.1 iota_compare_fusion
  4.8 0.1 broadcast_in_dim.124
  4.9 0.1 broadcast_in_dim.125
  5.0 0.1 broadcast_in_dim.130
  5.1 0.1 broadcast_in_dim.131
  5.2 0.8 %slice_bitcast_fusion.2 = (bf16[4,32,128]{2,1,0:T(8,128)(2,1)S(1)}, bf16[4,32,128]{2,1,0:T(8,128)(2,1)S(1)}, bf16[4,32,128]{2,1,0:T(8,128)(2,1)S(1)}) fusion(bf16[4,3,32,128]{3,2,1,0:T(8,128)(2,1)} %param.22), kind=kLoop, calls=%fused_computation.23 | loop fusion | bytes 196608 | tf_op jit(solution)/shard_map/jit(_where)/broadcast_in_dim | solution.py:63
  6.0 0.1 iota_compare_fusion.2
  6.1 0.1 broadcast_in_dim.118
  6.1 0.1 broadcast_in_dim.119
  6.2 0.9 %fusion.7 = bf16[4,128,128]{2,1,0:T(8,128)(2,1)} fusion(pred[4,128]{1,0:T(4,128)(4,1)S(1)} %broadcast_in_dim.131, pred[4,128]{1,0:T(4,128)(4,1)S(1)} %broadcast_in_dim.125, pred[4,128]{1,0:T(4,128)(4,1)S(1)} %broadcast_in_dim.119, bf16[4,32,128]{2,1,0:T(8,128)(2,1)S(1)} %get-tuple-element.6, bf16[4,32,128]{2,1,0:T(8,128)(2,1)S(1)} %get-tuple-element.7, ...), kind=kLoop, calls=%fused_computation.11 | loop fusion | flops 196608 | bytes 230912 | tf_op jit(solution)/shard_map/jit(_where)/select_n | solution.py:63
  7.1 1.9 %collective-permute-start.4 = (bf16[4,128,128]{2,1,0:T(8,128)(2,1)}, bf16[4,128,128]{2,1,0:T(8,128)(2,1)}, u32[]{:S(2)}, u32[]{:S(2)}) collective-permute-start(bf16[4,128,128]{2,1,0:T(8,128)(2,1)} %fusion.7), channel_id=1, source_target_pairs={{0,1},{1,0},{2,3},{3,2},{4,5},{5,4},{6,7},{7,6},{8,9},{9,8},{10,11... | collective-permute-start | bytes 393224 | tf_op jit(solution)/shard_map/ppermute | solution.py:16
  9.1 0.7 %compare_select_fusion = s32[4,24]{1,0:T(4,128)S(1)} fusion(s32[4,24]{1,0:T(4,128)} %param.19, s32[]{:T(128)S(6)} %mul.36, pred[]{:T(512)S(6)} %eq.87), kind=kLoop, calls=%fused_computation.35 | loop fusion | flops 3936 | bytes 773 | tf_op jit(solution)/shard_map/select_n | solution.py:98
  9.8 0.1 reshape.175
  9.9 1.3 %iota_compare_fusion.3 = pred[4,24]{1,0:T(4,128)(4,1)} fusion(s32[4]{0:T(128)} %param.20), kind=kLoop, calls=%fused_computation.58 | loop fusion | flops 96 | bytes 112 | tf_op jit(solution)/shard_map/lt | solution.py:97
  11.3 0.3 select_select_fusion
  11.6 0.6 %pad_clamp_fusion = s32[1024]{0:T(1024)} fusion(s32[96]{0:T(128)S(1)} %reshape.175), kind=kLoop, calls=%fused_computation.36 | loop fusion | flops 1024 | bytes 4480 | tf_op jit(solution)/shard_map/gather | solution.py:98
  12.2 0.0 collective-permute-done
  12.2 0.7 %fusion.11 = bf16[2,4,1024]{2,1,0:T(4,128)(2,1)S(1)} fusion(f32[1,4,1024]{2,1,0:T(4,128)S(1)} %bitcast.73, f32[1,4,1024]{2,1,0:T(4,128)} %bitcast.69), kind=kLoop, calls=%fused_computation.20 | loop fusion | flops 24576 | bytes 49152 | tf_op jit(solution)/shard_map/convert_element_type | solution.py:68
  12.9 0.1 collective-permute-start.1
  13.0 4.6 %collective-permute-start.2 = (bf16[8,1024]{1,0:T(8,128)(2,1)S(1)}, bf16[8,1024]{1,0:T(8,128)(2,1)S(1)}, u32[]{:S(2)}, u32[]{:S(2)}) collective-permute-start(bf16[8,1024]{1,0:T(8,128)(2,1)S(1)} %convert_element_type.19), channel_id=1, source_target_pairs={{0,30},{2,4},{4,2},{6,8},{8,6},{10,12},{12,10},{14,16},{16,14},{18... | collective-permute-start | bytes 49160 | tf_op jit(solution)/shard_map/ppermute | solution.py:16
  17.6 0.0 collective-permute-done.5
  17.6 0.8 %pad_maximum_fusion = bf16[2,32,512]{2,1,0:T(8,128)(2,1)S(1)} fusion(bf16[1,32,512]{2,1,0:T(8,128)(2,1)S(1)} %bitcast.72, bf16[1,32,512]{2,1,0:T(8,128)(2,1)} %bitcast.71), kind=kLoop, calls=%fused_computation.16 | loop fusion | flops 32768 | bytes 131072 | tf_op jit(solution)/shard_map/stack | solution.py:49
  18.4 0.9 %fusion.12 = f32[4,32]{1,0:T(4,128)S(1)} fusion(bf16[32,1024]{1,0:T(8,128)(2,1)S(1)} %bitcast.68, f32[4,1024]{1,0:T(4,128)} %param.12), kind=kOutput, calls=%fused_computation.31 | convolution fusion | flops 270336 | bytes 82432 | tf_op jit(solution)/shard_map/dot_general | solution.py:72
  19.3 0.0 collective-permute-start.6
  19.3 1.1 %collective-permute-done.6 = f32[4,32]{1,0:T(4,128)S(1)} collective-permute-done((f32[4,32]{1,0:T(4,128)S(1)}, f32[4,32]{1,0:T(4,128)S(1)}, u32[]{:S(2)}, u32[]{:S(2)}) %collective-permute-start.6) | collective-permute-done | bytes 544 | tf_op jit(solution)/shard_map/ppermute | solution.py:16
  20.4 0.6 %add.59 = f32[4,32]{1,0:T(4,128)} add(f32[4,32]{1,0:T(4,128)S(1)} %fusion.12, f32[4,32]{1,0:T(4,128)S(1)} %collective-permute-done.6) | non-fusion elementwise | flops 128 | bytes 1536 | tf_op jit(solution)/shard_map/add | solution.py:77
  21.0 0.0 collective-permute-start.7
  21.0 0.0 collective-permute-done.1
  21.0 0.0 collective-permute-done.2
  21.1 0.8 %gather_fusion = bf16[96,8,128]{2,1,0:T(8,128)(2,1)S(1)} fusion(bf16[8,24,128]{2,0,1:T(8,128)(2,1)S(1)} %pad_maximum_fusion.1, s32[1024]{0:T(1024)} %pad_clamp_fusion), kind=kCustom, calls=%fused_computation | custom fusion | bytes 393600 | tf_op jit(solution)/shard_map/gather | solution.py:98
  21.8 0.0 copy-start.3
  21.9 0.0 copy-start.4
  21.9 3.1 %collective-permute-done.7 = f32[4,32]{1,0:T(4,128)} collective-permute-done((f32[4,32]{1,0:T(4,128)}, f32[4,32]{1,0:T(4,128)}, u32[]{:S(2)}, u32[]{:S(2)}) %collective-permute-start.7) | collective-permute-done | bytes 544 | tf_op jit(solution)/shard_map/ppermute | solution.py:16
  24.9 0.7 %fusion.18 = bf16[1,4,32]{2,1,0:T(4,128)(2,1)S(1)} fusion(f32[4,32]{1,0:T(4,128)} %add.59, f32[4,32]{1,0:T(4,128)} %collective-permute-done.7), kind=kLoop, calls=%fused_computation.60 | loop fusion | flops 256 | bytes 1280 | tf_op jit(solution)/shard_map/broadcast_in_dim | solution.py:83
  25.6 0.0 collective-permute-start.8
  25.6 1.2 %convolution_bitcast_fusion = f32[8,4,128]{2,0,1:T(8,128)S(1)} fusion(bf16[4,24,128,128]{3,2,1,0:T(8,128)(2,1)S(1)} %copy-done, bf16[4,24,8,128]{3,2,1,0:T(8,128)(2,1)S(1)} %bitcast.64, pred[4,24]{1,0:T(4,128)(4,1)} %iota_compare_fusion.3), kind=kOutput, calls=%fused_computation.1 | convolution fusion | flops 25264128 | bytes 3358816 | tf_op jit(solution)/shard_map/mrsj,rsje->mre/dot_general | solution.py:100
  26.9 2.3 %collective-permute-done.8 = bf16[1,4,32]{2,1,0:T(4,128)(2,1)S(1)} collective-permute-done((bf16[1,4,32]{2,1,0:T(4,128)(2,1)S(1)}, bf16[1,4,32]{2,1,0:T(4,128)(2,1)S(1)}, u32[]{:S(2)}, u32[]{:S(2)}) %collective-permute-start.8) | collective-permute-done | bytes 288 | tf_op jit(solution)/shard_map/ppermute | solution.py:16
  29.2 0.1 collective-permute-start.9
  29.3 0.6 %collective-permute-start.3 = (f32[4,512]{1,0:T(4,128)S(1)}, f32[4,512]{1,0:T(4,128)S(1)}, u32[]{:S(2)}, u32[]{:S(2)}) collective-permute-start(f32[4,512]{1,0:T(4,128)S(1)} %get-tuple-element.11), channel_id=1, source_target_pairs={{0,1},{1,0},{2,3},{3,2},{4,5},{5,4},{6,7},{7,6},{8,9},{9,8},{10,11... | collective-permute-start | bytes 24584 | tf_op jit(solution)/shard_map/ppermute | solution.py:16
  29.9 3.9 %collective-permute-done.9 = bf16[2,4,32]{2,1,0:T(4,128)(2,1)S(1)} collective-permute-done((bf16[2,4,32]{2,1,0:T(4,128)(2,1)S(1)}, bf16[2,4,32]{2,1,0:T(4,128)(2,1)S(1)}, u32[]{:S(2)}, u32[]{:S(2)}) %collective-permute-start.9) | collective-permute-done | bytes 544 | tf_op jit(solution)/shard_map/ppermute | solution.py:16
  33.8 0.1 reshape.184
  33.9 0.0 collective-permute-done.3
  33.9 1.1 %maximum_add_fusion = f32[2,4,512]{2,1,0:T(4,128)S(1)} fusion(f32[1,4,512]{2,1,0:T(4,128)S(1)} %bitcast.76, f32[1,4,512]{2,1,0:T(4,128)S(1)} %get-tuple-element.10, bf16[4,128,1,1]{1,0,2,3:T(4,128)(2,1)S(1)} %reshape.184, bf16[1,4,128,128]{3,2,1,0:T(8,128)(2,1)} %bitcast.22, bf16[1,4,128,128]{3,2,1,0:T(8,128)(2,1)S(1)} %select_select_fusion), kind=kOutput, calls=%fused_computation.25 | convolution fusion | flops 1187840 | bytes 295936 | tf_op jit(solution)/shard_map/mk,hrke->hmre/dot_general | solution.py:109
  35.0 1.4 %multiply_add_fusion = (f32[4,1024]{1,0:T(4,128)}, f32[4,1024]{1,0:T(4,128)}) fusion(f32[4,1024]{1,0:T(4,128)S(1)} %copy-done.2, f32[4,1024]{1,0:T(4,128)S(1)} %copy-done.3, f32[4,1024]{1,0:T(4,128)S(1)} %copy-done.1, f32[4,1024]{1,0:T(4,128)S(1)} %copy-done.4, f32[4,1024]{1,0:T(4,128)S(1)} %bitcast.70, f32[4,1024]{1,0:T(4,128)} %param.15, f32[1024]{0:T(1024)} %param.17), kind=kLoop, calls=%fused_computation.26 | loop fusion | flops 57344 | bytes 135168 | tf_op jit(solution)/shard_map/add | solution.py:116
  (22 shorter events, 0.2 us)
Async XLA Ops:
  0.6 25.0 %copy-start = (bf16[4,24,128,128]{3,2,1,0:T(8,128)(2,1)S(1)}, bf16[4,24,128,128]{3,2,1,0:T(8,128)(2,1)}, u32[]{:S(2)}) copy-start(bf16[4,24,128,128]{3,2,1,0:T(8,128)(2,1)} %param.18) | copy-start | bytes 9437188
  0.6 17.0 %collective-permute-start.5 = (bf16[32,512]{1,0:T(8,128)(2,1)}, bf16[32,512]{1,0:T(8,128)(2,1)S(1)}, u32[]{:S(2)}, u32[]{:S(2)}) collective-permute-start(bf16[32,512]{1,0:T(8,128)(2,1)} %param.23), channel_id=1, source_target_pairs={{0,1},{1,0},{2,3},{3,2},{4,5},{5,4},{6,7},{7,6},{8,9},{9,8},{10,11... | collective-permute-start | bytes 98312 | tf_op jit(solution)/shard_map/ppermute | solution.py:16
  3.7 8.5 %collective-permute-start = (f32[4,1024]{1,0:T(4,128)}, f32[4,1024]{1,0:T(4,128)S(1)}, u32[]{:S(2)}, u32[]{:S(2)}) collective-permute-start(f32[4,1024]{1,0:T(4,128)} %param.12), channel_id=1, source_target_pairs={{0,1},{1,0},{2,3},{3,2},{4,5},{5,4},{6,7},{7,6},{8,9},{9,8},{10,11... | collective-permute-start | bytes 49160 | tf_op jit(solution)/shard_map/ppermute | solution.py:16
  7.1 27.8 %copy-start.1 = (f32[4,1024]{1,0:T(4,128)S(1)}, f32[4,1024]{1,0:T(4,128)}, u32[]{:S(2)}) copy-start(f32[4,1024]{1,0:T(4,128)} %param.12) | copy-start | bytes 49156
  7.1 27.8 %copy-start.2 = (f32[4,1024]{1,0:T(4,128)S(1)}, f32[4,1024]{1,0:T(4,128)}, u32[]{:S(2)}) copy-start(f32[4,1024]{1,0:T(4,128)} %param.13) | copy-start | bytes 49156
  7.1 26.7 %collective-permute-start.4 = (bf16[4,128,128]{2,1,0:T(8,128)(2,1)}, bf16[4,128,128]{2,1,0:T(8,128)(2,1)}, u32[]{:S(2)}, u32[]{:S(2)}) collective-permute-start(bf16[4,128,128]{2,1,0:T(8,128)(2,1)} %fusion.7), channel_id=1, source_target_pairs={{0,1},{1,0},{2,3},{3,2},{4,5},{5,4},{6,7},{7,6},{8,9},{9,8},{10,11... | collective-permute-start | bytes 393224 | tf_op jit(solution)/shard_map/ppermute | solution.py:16
  12.9 8.1 %collective-permute-start.1 = (bf16[8,1024]{1,0:T(8,128)(2,1)S(1)}, bf16[8,1024]{1,0:T(8,128)(2,1)S(1)}, u32[]{:S(2)}, u32[]{:S(2)}) collective-permute-start(bf16[8,1024]{1,0:T(8,128)(2,1)S(1)} %convert_element_type.19), channel_id=1, source_target_pairs={{0,2},{2,0},{4,6},{6,4},{8,10},{10,8},{12,14},{14,12},{16,18},{18,... | collective-permute-start | bytes 49160 | tf_op jit(solution)/shard_map/ppermute | solution.py:16
  13.0 8.0 %collective-permute-start.2 = (bf16[8,1024]{1,0:T(8,128)(2,1)S(1)}, bf16[8,1024]{1,0:T(8,128)(2,1)S(1)}, u32[]{:S(2)}, u32[]{:S(2)}) collective-permute-start(bf16[8,1024]{1,0:T(8,128)(2,1)S(1)} %convert_element_type.19), channel_id=1, source_target_pairs={{0,30},{2,4},{4,2},{6,8},{8,6},{10,12},{12,10},{14,16},{16,14},{18... | collective-permute-start | bytes 49160 | tf_op jit(solution)/shard_map/ppermute | solution.py:16
  19.3 1.2 %collective-permute-start.6 = (f32[4,32]{1,0:T(4,128)S(1)}, f32[4,32]{1,0:T(4,128)S(1)}, u32[]{:S(2)}, u32[]{:S(2)}) collective-permute-start(f32[4,32]{1,0:T(4,128)S(1)} %fusion.12), channel_id=1, source_target_pairs={{0,2},{2,0},{4,6},{6,4},{8,10},{10,8},{12,14},{14,12},{16,18},{18,... | collective-permute-start | bytes 1544 | tf_op jit(solution)/shard_map/ppermute | solution.py:16
  21.0 3.9 %collective-permute-start.7 = (f32[4,32]{1,0:T(4,128)}, f32[4,32]{1,0:T(4,128)}, u32[]{:S(2)}, u32[]{:S(2)}) collective-permute-start(f32[4,32]{1,0:T(4,128)} %add.59), channel_id=1, source_target_pairs={{0,4},{2,6},{4,0},{6,2},{8,12},{10,14},{12,8},{14,10},{16,20},{18,... | collective-permute-start | bytes 1544 | tf_op jit(solution)/shard_map/ppermute | solution.py:16
  21.8 13.1 %copy-start.3 = (f32[4,1024]{1,0:T(4,128)S(1)}, f32[4,1024]{1,0:T(4,128)}, u32[]{:S(2)}) copy-start(f32[4,1024]{1,0:T(4,128)} %param.16) | copy-start | bytes 49156
  21.9 13.1 %copy-start.4 = (f32[4,1024]{1,0:T(4,128)S(1)}, f32[4,1024]{1,0:T(4,128)}, u32[]{:S(2)}) copy-start(f32[4,1024]{1,0:T(4,128)} %param.14) | copy-start | bytes 49156
  25.6 3.6 %collective-permute-start.8 = (bf16[1,4,32]{2,1,0:T(4,128)(2,1)S(1)}, bf16[1,4,32]{2,1,0:T(4,128)(2,1)S(1)}, u32[]{:S(2)}, u32[]{:S(2)}) collective-permute-start(bf16[1,4,32]{2,1,0:T(4,128)(2,1)S(1)} %fusion.18), channel_id=1, source_target_pairs={{0,8},{2,10},{4,12},{6,14},{8,0},{10,2},{12,4},{14,6},{16,24},{18,... | collective-permute-start | bytes 776 | tf_op jit(solution)/shard_map/ppermute | solution.py:16
  29.2 4.5 %collective-permute-start.9 = (bf16[2,4,32]{2,1,0:T(4,128)(2,1)S(1)}, bf16[2,4,32]{2,1,0:T(4,128)(2,1)S(1)}, u32[]{:S(2)}, u32[]{:S(2)}) collective-permute-start(bf16[2,4,32]{2,1,0:T(4,128)(2,1)S(1)} %maximum_select_fusion.1), channel_id=1, source_target_pairs={{0,16},{2,18},{4,20},{6,22},{8,24},{10,26},{12,28},{14,30},{16,0},... | collective-permute-start | bytes 1544 | tf_op jit(solution)/shard_map/ppermute | solution.py:16
  29.3 4.6 %collective-permute-start.3 = (f32[4,512]{1,0:T(4,128)S(1)}, f32[4,512]{1,0:T(4,128)S(1)}, u32[]{:S(2)}, u32[]{:S(2)}) collective-permute-start(f32[4,512]{1,0:T(4,128)S(1)} %get-tuple-element.11), channel_id=1, source_target_pairs={{0,1},{1,0},{2,3},{3,2},{4,5},{5,4},{6,7},{7,6},{8,9},{9,8},{10,11... | collective-permute-start | bytes 24584 | tf_op jit(solution)/shard_map/ppermute | solution.py:16

commit v2 on v1

v2 whole, which is shorter than its diff:
```python
import functools

import jax
import jax.numpy as jnp
from jax import lax
from jax.experimental import pallas as pl
from jax.experimental.pallas import tpu as pltpu
from jax.sharding import PartitionSpec as P

PANEL = 128
GROUP = 4
COST = 10**9


damping = 0.5
time_step = 0.25

IN_SMEM = pl.BlockSpec(memory_space=pltpu.SMEM)
IN_VMEM = pl.BlockSpec(memory_space=pltpu.VMEM)
f32 = jnp.float32
bf16 = jnp.bfloat16


def swapped(block, axis, partner):
    count = lax.axis_size(axis)
    return lax.ppermute(block, axis, [(i, partner(i) % count) for i in range(count)])


def place_of(parts, pos, h):
    return pos ^ h if parts == 2 else h


def span(start, width):
    return pl.ds(pl.multiple_of(start, PANEL), width)


def deficit_kernel(rate_ref, out_ref):
    out_ref[...] = (1.0 - jnp.exp(rate_ref[...])).astype(bf16)


def partial_kernel(parts, pos_ref, deficit_ref, *refs):
    column_refs, out_ref = refs[:parts], refs[parts]
    total = None
    for h in range(parts):
        width = column_refs[h].shape[1]
        piece = lax.dot_general(
            deficit_ref[:, span(place_of(parts, pos_ref[0], h) * width, width)],
            column_refs[h][...],
            (((1,), (1,)), ((), ())),
            preferred_element_type=f32,
        )
        total = piece if total is None else total + piece
    out_ref[...] = total


def far_kernel(cluster_ref, own_cluster_ref, basis_ref, out_ref):
    rows, slots, rank, panel = basis_ref.shape
    clusters = out_ref.shape[0] // rank
    for r in range(rows):
        for j in range(clusters):
            wanted = own_cluster_ref[0] ^ j
            block = jnp.zeros((rank, panel), f32)
            for k in range(slots):
                live = cluster_ref[r, k] == wanted
                block = jnp.where(live, basis_ref[r, k].astype(f32), block)
            out_ref[j * rank : (j + 1) * rank, r * panel : (r + 1) * panel] = block.astype(bf16)


def near_kernel(own_panels, total_panels, column_ref, count_ref, pos_ref, own_ref, near_ref, far_ref, blocks_ref, out_ref, window, picked):
    rows, slots = column_ref.shape
    members = own_ref.shape[0]
    odd = pos_ref[0] % 2
    for side, start in ((own_ref, own_panels), (near_ref, (1 - odd) * 2 * own_panels), (far_ref, odd * 2 * own_panels)):
        for j in range(own_panels):
            window[start + j] = side[:, j * PANEL : (j + 1) * PANEL].astype(f32)
    window[3 * own_panels] = jnp.zeros((members, PANEL), f32)
    base = (pos_ref[0] - 1) * own_panels
    for r in range(rows):
        for s in range(slots):
            place = lax.rem(column_ref[r, s] - base + total_panels, total_panels)
            place = jnp.where(s < count_ref[r], place, 3 * own_panels)
            picked[r, :, s * PANEL : (s + 1) * PANEL] = window[place].astype(bf16)
        out_ref[:, r * PANEL : (r + 1) * PANEL] = jnp.dot(
            picked[r], blocks_ref[r].reshape(slots * PANEL, PANEL), preferred_element_type=f32
        )


def last_kernel(parts, pos_ref, low_ref, high_ref, *refs):
    far_refs, near_refs = refs[:parts], refs[parts : 2 * parts]
    base_ref, scale_ref, out_ref = refs[2 * parts :]
    depth = low_ref.shape[1]
    for h in range(parts):
        width = near_refs[h].shape[1]
        lanes = span(place_of(parts, pos_ref[0], h) * width, width)
        stress = (
            near_refs[h][...]
            + jnp.dot(low_ref[...], far_refs[h][:depth], preferred_element_type=f32)
            + jnp.dot(high_ref[...], far_refs[h][depth:], preferred_element_type=f32)
        )
        out_ref[:, lanes] = base_ref[:, lanes] + scale_ref[:, lanes] * stress


def per_device(
    log_rate,
    log_state,
    direct_effect,
    evolution_effect,
    slip_distance,
    normal_stress,
    near_blocks,
    near_columns,
    near_count,
    far_clusters,
    far_basis,
    column_basis,
):
    fault_count = lax.axis_size("fault")
    parts = lax.axis_size("member")
    fault_pos = lax.axis_index("fault")
    member_pos = lax.axis_index("member")
    local_members, elements = log_rate.shape
    own_panels = elements // PANEL
    total_panels = own_panels * fault_count
    row_count, slots = near_columns.shape
    row_width = row_count * PANEL
    rank_size = column_basis.shape[0]
    cluster_total = fault_count // GROUP
    members = parts * local_members
    def gathered(block):
        if parts == 2:
            return [block, swapped(block, "member", lambda i: i ^ 1)]
        every = lax.all_gather(block, "member", axis=0)
        return [every[h] for h in range(parts)]

    def call(body, name, out_shape, specs, mib=2, flops=10**6, scratch=()):
        return pl.pallas_call(
            body,
            out_shape=jax.ShapeDtypeStruct(*out_shape),
            in_specs=specs,
            out_specs=IN_VMEM,
            scratch_shapes=scratch,
            compiler_params=pltpu.CompilerParams(vmem_limit_bytes=mib << 20),
            cost_estimate=pl.CostEstimate(flops=flops, bytes_accessed=1, transcendentals=0),
            name=name,
        )

    columns = gathered(column_basis)
    deficit = call(deficit_kernel, "deficit", ((local_members, elements), bf16), [IN_VMEM], flops=COST)(log_rate)
    deficits = gathered(deficit)
    far_by_cluster = call(
        far_kernel, "far_by_cluster", ((cluster_total * rank_size, row_width), bf16), [IN_SMEM, IN_SMEM, IN_VMEM], flops=COST
    )(far_clusters, (fault_pos // GROUP)[None], far_basis)
    far_all = gathered(far_by_cluster)
    deficit, far_by_cluster = lax.optimization_barrier((deficit, far_by_cluster))
    partial_value = call(
        functools.partial(partial_kernel, parts), "partial", ((local_members, rank_size), f32), [IN_SMEM] + [IN_VMEM] * (1 + parts), flops=COST
    )(member_pos[None], deficit, *columns)
    deficit_all = jnp.concatenate(deficits, axis=0)

    total = partial_value + swapped(partial_value, "fault", lambda i: i ^ 1)
    near_side = swapped(deficit_all, "fault", lambda i: i ^ 1)
    far_side = swapped(deficit_all, "fault", lambda i: i + 1 if i % 2 else i - 1)
    bit = 2
    while bit < GROUP:
        total = total + swapped(total, "fault", lambda i: i ^ bit)
        bit *= 2
    low, far_side, near_side = lax.optimization_barrier((total.astype(bf16), far_side, near_side))

    near_field = call(
        functools.partial(near_kernel, own_panels, total_panels),
        "near",
        ((members, row_width), f32),
        [IN_SMEM] * 3 + [IN_VMEM] * 4,
        mib=8,
        flops=COST,
        scratch=[
            pltpu.VMEM((3 * own_panels + 1, members, PANEL), f32),
            pltpu.VMEM((row_count, members, slots * PANEL), bf16),
        ],
    )(near_columns, near_count, fault_pos[None], deficit_all, near_side, far_side, near_blocks)

    high = None
    while bit < fault_count:
        if high is not None:
            low = jnp.concatenate([low, high], axis=1)
        if 2 * bit == fault_count:
            low, near_field = lax.optimization_barrier((low, near_field))
        high = swapped(low, "fault", lambda i: i ^ bit)
        bit *= 2

    near_field = near_field.reshape(parts, local_members, row_width)
    if parts == 2:
        near_rows = [near_field[0], swapped(near_field[1], "member", lambda i: i ^ 1)]
    else:
        exchanged = lax.all_to_all(near_field, "member", 0, 0)
        near_rows = [exchanged[h] for h in range(parts)]

    velocity = jnp.exp(log_rate)
    state_rate = (jnp.exp(-log_state) - velocity) / slip_distance
    resistance = normal_stress[None, :] * direct_effect + damping * velocity
    scale = time_step / resistance
    base = log_rate - scale * (normal_stress[None, :] * evolution_effect * state_rate)
    state_next = log_state + time_step * state_rate
    rate_next = call(
        functools.partial(last_kernel, parts),
        "last",
        ((local_members, elements), f32),
        [IN_SMEM] + [IN_VMEM] * (4 + 2 * parts),
        flops=COST,
    )(member_pos[None], low, high, *far_all, *near_rows, base, scale)
    return rate_next, state_next


def solution(mesh):
    return jax.shard_map(
        per_device,
        mesh=mesh,
        in_specs=(
            P("member", "fault"),
            P("member", "fault"),
            P("member", "fault"),
            P("member", "fault"),
            P("member", "fault"),
            P("fault"),
            P(("fault", "member"), None, None, None),
            P(("fault", "member"), None),
            P(("fault", "member")),
            P(("fault", "member"), None),
            P(("fault", "member"), None, None, None),
            P(None, ("fault", "member")),
        ),
        out_specs=(P("member", "fault"), P("member", "fault")),
        check_vma=False,
    )
```

time: 36.9 us -> 26.3 us (0.71)
  other arithmetic: 8.15 us -> 0.73 us
  matrix products: 3.15 us -> 0 us
  Pallas kernels: 0 us -> 2.7 us
  local copies, waits for them, and re-layouts: 3.41 us -> 0.77 us
  starting transfers between devices: 10.4 us -> 11.4 us
  waiting for transfers between devices: 10.4 us -> 9.77 us
    dot_general x3 -> x0, matrix products: 3.15 us -> none  [the longest x1 1.24 us: per_device(): jnp.einsum('mrsj,rsje->mre', picked, near_blocks, preferred_element_type=...]
    pallas_call x0 -> x5, Pallas kernels: none -> 2.7 us  [the longest x1 1.17 us: per_device(): call(functools.partial(near_kernel, own_panels, total_panels), 'near', ((...]
    select_n x5 -> x0, other arithmetic: 1.91 us -> none  [the longest x2 1.19 us: per_device(): jnp.where(mine[:, :, None, None], far_basis[:, k, None], far_by_cluster)]
    broadcast_in_dim x11 -> x0, local copies, waits for them, and re-layouts: 1.45 us -> none  [the longest x10 1.37 us: per_device(): jnp.where(mine[:, :, None, None], far_basis[:, k, None], far_by_cluster)]
    lt x1 -> x0, other arithmetic: 1.32 us -> none  [per_device(): active = jnp.arange(slots)[None, :] < near_count[:, None]]
    slice x2 -> x1, local copies, waits for them, and re-layouts: 1.01 us -> 0.01 us  [per_device(): near_field[1]]
    ppermute x10, starting transfers between devices: 10.4 us -> 11.4 us  [swapped(): lax.ppermute(block, axis, [(i, partner(i) % count) for i in range(count)])]
    gather x1 -> x0, local copies, waits for them, and re-layouts: 0.79 us -> none  [per_device(): picked = panel_view[:, local_cols, :]]
  transfers between devices with their start and end apart: 10 -> 10, of which waited for: 4 -> 5; matrix products, arithmetic and copies ran while one was open for 34% -> 3% of each run, Pallas kernels for 0% -> 7%
where the time goes in v2:
time: 26.3 us; the launch traced here: 26.1 us
  starting transfers between devices  11.4 us (43%)
  waiting for transfers between devices  9.77 us (37%)
  Pallas kernels  2.7 us (10%)
  local copies, waits for them, and re-layouts  0.77 us (3%)
  between operations  0.75 us (3%)
  other arithmetic  0.73 us (3%)
    ppermute x10, starting transfers between devices, swapped(): lax.ppermute(block, axis, [(i, partner(i) % count) for i in range(count)])  11.4 us
    ppermute x10, waiting for transfers between devices, swapped(): lax.ppermute(block, axis, [(i, partner(i) % count) for i in range(count)])  9.77 us
    pallas_call x1, Pallas kernels, per_device(): call(functools.partial(near_kernel, own_panels, total_panels), 'near', ((...  1.17 us
    pallas_call x1, Pallas kernels, per_device(): call(functools.partial(last_kernel, parts), 'last', ((local_members, elem...  0.77 us
    unnamed x26, local copies, waits for them, and re-layouts  0.76 us
    add x1, other arithmetic, per_device(): state_next = log_state + time_step * state_rate  0.63 us
    pallas_call x1, Pallas kernels, per_device(): call(far_kernel, 'far_by_cluster', ((cluster_total * rank_size, row_width...  0.62 us
  transfers between devices with their start and end apart: 10, of which 5 were waited for; matrix products, arithmetic and copies ran while one was open for 3% of the time, Pallas kernels for 7%

profile of v2, /device:TPU:0, one launch (start us, length us, event | category | flops | bytes accessed | tf_op | source)
XLA Modules:
  0.0 26.1 jit_solution(346974246309004354)
XLA Ops:
  0.6 0.0 copy-start
  0.6 0.7 %copy-done = f32[4,1024]{1,0:T(4,128)S(1)} copy-done((f32[4,1024]{1,0:T(4,128)S(1)}, f32[4,1024]{1,0:T(4,128)}, u32[]{:S(2)}) %copy-start) | copy-done | bytes 16408
  1.4 0.0 copy-start.4
  1.4 0.0 copy-start.3
  1.4 0.0 copy-start.5
  1.4 3.0 %collective-permute-start.3 = (bf16[4,1024]{1,0:T(4,128)(2,1)S(1)}, bf16[4,1024]{1,0:T(4,128)(2,1)S(1)}, u32[]{:S(2)}, u32[]{:S(2)}) collective-permute-start(bf16[4,1024]{1,0:T(4,128)(2,1)S(1)} %deficit.1.deficit_ref), channel_id=1, source_target_pairs={{0,1},{1,0},{2,3},{3,2},{4,5},{5,4},{6,7},{7,6},{8,9},{9,8},{10,11... | collective-permute-start | bytes 24584 | tf_op jit(solution)/shard_map/ppermute | solution.py:26
  4.4 0.0 copy-done.4
  4.4 0.7 %collective-permute-start = (bf16[32,512]{1,0:T(8,128)(2,1)S(1)}, bf16[32,512]{1,0:T(8,128)(2,1)S(1)}, u32[]{:S(2)}, u32[]{:S(2)}) collective-permute-start(bf16[32,512]{1,0:T(8,128)(2,1)S(1)} %copy-done.4), channel_id=1, source_target_pairs={{0,1},{1,0},{2,3},{3,2},{4,5},{5,4},{6,7},{7,6},{8,9},{9,8},{10,11... | collective-permute-start | bytes 98312 | tf_op jit(solution)/shard_map/ppermute | solution.py:26
  5.1 0.0 copy-done.3
  5.1 0.0 copy-done.5
  5.1 0.0 copy-start.2
  5.1 0.0 copy-start.6
  5.1 0.0 copy-start.7
  5.1 0.6 %far_by_cluster.1.refs_0_ = bf16[128,512]{1,0:T(8,128)(2,1)S(1)} custom-call(s32[4,3]{1,0:T(4,128)S(1)} %copy-done.5, s32[1]{0:T(128)} %bitcast.1.own_cluster_ref, bf16[4,3,32,128]{3,2,1,0:T(8,128)(2,1)S(1)} %copy-done.3), custom_call_target="tpu_custom_call" | custom-call | flops 1000000000 | bytes 1 | tf_op jit(solution)/shard_map/far_by_cluster/pallas_call | solution.py:150
  5.7 2.6 %collective-permute-done.refs_1_ = bf16[32,512]{1,0:T(8,128)(2,1)S(1)} collective-permute-done((bf16[32,512]{1,0:T(8,128)(2,1)S(1)}, bf16[32,512]{1,0:T(8,128)(2,1)S(1)}, u32[]{:S(2)}, u32[]{:S(2)}) %collective-permute-start) | collective-permute-done | bytes 32800 | tf_op jit(solution)/shard_map/ppermute | solution.py:26
  8.3 0.0 copy-start.11
  8.3 0.0 copy-start.12
  8.4 0.1 partial.1
  8.5 0.0 collective-permute-start.1
  8.5 0.7 %collective-permute-start.8 = (bf16[128,512]{1,0:T(8,128)(2,1)S(1)}, bf16[128,512]{1,0:T(8,128)(2,1)S(1)}, u32[]{:S(2)}, u32[]{:S(2)}) collective-permute-start(bf16[128,512]{1,0:T(8,128)(2,1)S(1)} %far_by_cluster.1.refs_0_), channel_id=1, source_target_pairs={{0,1},{1,0},{2,3},{3,2},{4,5},{5,4},{6,7},{7,6},{8,9},{9,8},{10,11... | collective-permute-start | bytes 393224 | tf_op jit(solution)/shard_map/ppermute | solution.py:26
  9.2 0.5 %collective-permute-done.1 = f32[4,32]{1,0:T(4,128)S(1)} collective-permute-done((f32[4,32]{1,0:T(4,128)S(1)}, f32[4,32]{1,0:T(4,128)S(1)}, u32[]{:S(2)}, u32[]{:S(2)}) %collective-permute-start.1) | collective-permute-done | bytes 544 | tf_op jit(solution)/shard_map/ppermute | solution.py:26
  9.7 1.5 %collective-permute-start.2 = (f32[4,32]{1,0:T(4,128)S(1)}, f32[4,32]{1,0:T(4,128)S(1)}, u32[]{:S(2)}, u32[]{:S(2)}) collective-permute-start(f32[4,32]{1,0:T(4,128)S(1)} %add.13), channel_id=1, source_target_pairs={{0,4},{2,6},{4,0},{6,2},{8,12},{10,14},{12,8},{14,10},{16,20},{18,... | collective-permute-start | bytes 1544 | tf_op jit(solution)/shard_map/ppermute | solution.py:26
  11.2 0.0 collective-permute-done.3
  11.2 0.1 collective-permute-start.5
  11.2 3.7 %collective-permute-start.4 = (bf16[8,1024]{1,0:T(8,128)(2,1)S(1)}, bf16[8,1024]{1,0:T(8,128)(2,1)S(1)}, u32[]{:S(2)}, u32[]{:S(2)}) collective-permute-start(bf16[8,1024]{1,0:T(8,128)(2,1)S(1)} %pad_maximum_fusion.own_ref), channel_id=1, source_target_pairs={{0,30},{2,4},{4,2},{6,8},{8,6},{10,12},{12,10},{14,16},{16,14},{18... | collective-permute-start | bytes 49160 | tf_op jit(solution)/shard_map/ppermute | solution.py:26
  14.9 0.0 collective-permute-done.2
  14.9 0.0 collective-permute-done.5.near_ref
  14.9 2.2 %collective-permute-done.4.far_ref = bf16[8,1024]{1,0:T(8,128)(2,1)S(1)} collective-permute-done((bf16[8,1024]{1,0:T(8,128)(2,1)S(1)}, bf16[8,1024]{1,0:T(8,128)(2,1)S(1)}, u32[]{:S(2)}, u32[]{:S(2)}) %collective-permute-start.4) | collective-permute-done | bytes 16416 | tf_op jit(solution)/shard_map/ppermute | solution.py:26
  17.2 0.0 collective-permute-start.6
  17.2 0.0 copy-done.2
  17.2 0.0 copy-done.6
  17.2 0.0 copy-done.7
  17.2 1.2 %near.1 = f32[8,512]{1,0:T(8,128)S(1)} custom-call(s32[4,24]{1,0:T(4,128)S(1)} %copy-done.6, s32[4]{0:T(128)S(1)} %copy-done.7, s32[1]{0:T(128)} %bitcast.2.pos_ref, bf16[8,1024]{1,0:T(8,128)(2,1)S(1)} %pad_maximum_fusion.own_ref, bf16[8,1024]{1,0:T(8,128)(2,1)S(1)} %collective-permute-done.5.near_ref, bf16[8,1024]{1,0:T(8,128)(2,1)S(1)} %collective-permute-done.4.far_ref, ...), custom_call_target="tpu_custom_call" | custom-call | flops 1000000000 | bytes 1 | tf_op jit(solution)/shard_map/near/pallas_call | solution.py:169
  18.4 2.4 %collective-permute-done.6 = bf16[4,32]{1,0:T(4,128)(2,1)S(1)} collective-permute-done((bf16[4,32]{1,0:T(4,128)(2,1)S(1)}, bf16[4,32]{1,0:T(4,128)(2,1)S(1)}, u32[]{:S(2)}, u32[]{:S(2)}) %collective-permute-start.6) | collective-permute-done | bytes 288 | tf_op jit(solution)/shard_map/ppermute | solution.py:26
  20.7 0.1 pad_maximum_fusion.1.low_ref
  20.8 0.8 %collective-permute-start.7 = (bf16[4,64]{1,0:T(4,128)(2,1)S(1)}, bf16[4,64]{1,0:T(4,128)(2,1)S(1)}, u32[]{:S(2)}, u32[]{:S(2)}) collective-permute-start(bf16[4,64]{1,0:T(4,128)(2,1)S(1)} %pad_maximum_fusion.1.low_ref), channel_id=1, source_target_pairs={{0,16},{2,18},{4,20},{6,22},{8,24},{10,26},{12,28},{14,30},{16,0},... | collective-permute-start | bytes 1544 | tf_op jit(solution)/shard_map/ppermute | solution.py:26
  21.6 0.9 %collective-permute-start.9 = (f32[4,512]{1,0:T(4,128)S(1)}, f32[4,512]{1,0:T(4,128)S(1)}, u32[]{:S(2)}, u32[]{:S(2)}) collective-permute-start(f32[4,512]{1,0:T(4,128)S(1)} %get-tuple-element.17), channel_id=1, source_target_pairs={{0,1},{1,0},{2,3},{3,2},{4,5},{5,4},{6,7},{7,6},{8,9},{9,8},{10,11... | collective-permute-start | bytes 24584 | tf_op jit(solution)/shard_map/ppermute | solution.py:26
  22.5 0.0 copy-done.1
  22.5 0.0 copy-done.8
  22.5 0.0 copy-done.9
  22.5 0.0 copy-done.10
  22.5 0.0 copy-done.11
  22.6 0.0 copy-done.12
  22.6 0.6 %multiply_add_fusion = (f32[4,1024]{1,0:T(4,128)}, f32[4,1024]{1,0:T(4,128)S(1)}, f32[4,1024]{1,0:T(4,128)S(1)}) fusion(f32[4,1024]{1,0:T(4,128)S(1)} %copy-done.8, f32[4,1024]{1,0:T(4,128)S(1)} %copy-done.9, f32[4,1024]{1,0:T(4,128)S(1)} %copy-done.1, f32[4,1024]{1,0:T(4,128)S(1)} %copy-done.10, f32[4,1024]{1,0:T(4,128)S(1)} %copy-done.11, ...), kind=kLoop, calls=%fused_computation.1 | loop fusion | flops 53248 | bytes 135168 | tf_op jit(solution)/shard_map/add | solution.py:203
  23.2 2.1 %collective-permute-done.7.high_ref = bf16[4,64]{1,0:T(4,128)(2,1)S(1)} collective-permute-done((bf16[4,64]{1,0:T(4,128)(2,1)S(1)}, bf16[4,64]{1,0:T(4,128)(2,1)S(1)}, u32[]{:S(2)}, u32[]{:S(2)}) %collective-permute-start.7) | collective-permute-done | bytes 544 | tf_op jit(solution)/shard_map/ppermute | solution.py:26
  25.3 0.0 collective-permute-done.9.refs_3_
  25.3 0.0 collective-permute-done.8.refs_1_
  25.3 0.8 %last.1 = f32[4,1024]{1,0:T(4,128)} custom-call(s32[1]{0:T(128)} %bitcast.pos_ref, bf16[4,64]{1,0:T(4,128)(2,1)S(1)} %pad_maximum_fusion.1.low_ref, bf16[4,64]{1,0:T(4,128)(2,1)S(1)} %collective-permute-done.7.high_ref, bf16[128,512]{1,0:T(8,128)(2,1)S(1)} %far_by_cluster.1.refs_0_, bf16[128,512]{1,0:T(8,128)(2,1)S(1)} %collective-permute-done.8.refs_1_, ...), custom_call_target="tpu_custom_call" | custom-call | flops 1000000000 | bytes 1 | tf_op jit(solution)/shard_map/last/pallas_call | solution.py:204
  (9 shorter events, 0.0 us)
Async XLA Ops:
  0.6 0.7 %copy-start = (f32[4,1024]{1,0:T(4,128)S(1)}, f32[4,1024]{1,0:T(4,128)}, u32[]{:S(2)}) copy-start(f32[4,1024]{1,0:T(4,128)} %rate_ref.1) | copy-start | bytes 49156
  1.4 3.1 %copy-start.4 = (bf16[32,512]{1,0:T(8,128)(2,1)S(1)}, bf16[32,512]{1,0:T(8,128)(2,1)}, u32[]{:S(2)}) copy-start(bf16[32,512]{1,0:T(8,128)(2,1)} %refs_0_.1) | copy-start | bytes 98308
  1.4 3.7 %copy-start.3 = (bf16[4,3,32,128]{3,2,1,0:T(8,128)(2,1)S(1)}, bf16[4,3,32,128]{3,2,1,0:T(8,128)(2,1)}, u32[]{:S(2)}) copy-start(bf16[4,3,32,128]{3,2,1,0:T(8,128)(2,1)} %basis_ref.1) | copy-start | bytes 294916
  1.4 3.7 %copy-start.5 = (s32[4,3]{1,0:T(4,128)S(1)}, s32[4,3]{1,0:T(4,128)}, u32[]{:S(2)}) copy-start(s32[4,3]{1,0:T(4,128)} %cluster_ref.1) | copy-start | bytes 148
  1.4 9.8 %collective-permute-start.3 = (bf16[4,1024]{1,0:T(4,128)(2,1)S(1)}, bf16[4,1024]{1,0:T(4,128)(2,1)S(1)}, u32[]{:S(2)}, u32[]{:S(2)}) collective-permute-start(bf16[4,1024]{1,0:T(4,128)(2,1)S(1)} %deficit.1.deficit_ref), channel_id=1, source_target_pairs={{0,1},{1,0},{2,3},{3,2},{4,5},{5,4},{6,7},{7,6},{8,9},{9,8},{10,11... | collective-permute-start | bytes 24584 | tf_op jit(solution)/shard_map/ppermute | solution.py:26
  4.4 3.9 %collective-permute-start = (bf16[32,512]{1,0:T(8,128)(2,1)S(1)}, bf16[32,512]{1,0:T(8,128)(2,1)S(1)}, u32[]{:S(2)}, u32[]{:S(2)}) collective-permute-start(bf16[32,512]{1,0:T(8,128)(2,1)S(1)} %copy-done.4), channel_id=1, source_target_pairs={{0,1},{1,0},{2,3},{3,2},{4,5},{5,4},{6,7},{7,6},{8,9},{9,8},{10,11... | collective-permute-start | bytes 98312 | tf_op jit(solution)/shard_map/ppermute | solution.py:26
  5.1 12.1 %copy-start.2 = (bf16[4,24,128,128]{3,2,1,0:T(8,128)(2,1)S(1)}, bf16[4,24,128,128]{3,2,1,0:T(8,128)(2,1)}, u32[]{:S(2)}) copy-start(bf16[4,24,128,128]{3,2,1,0:T(8,128)(2,1)} %blocks_ref.1) | copy-start | bytes 9437188
  5.1 12.1 %copy-start.6 = (s32[4,24]{1,0:T(4,128)S(1)}, s32[4,24]{1,0:T(4,128)}, u32[]{:S(2)}) copy-start(s32[4,24]{1,0:T(4,128)} %column_ref.1) | copy-start | bytes 1156
  5.1 12.1 %copy-start.7 = (s32[4]{0:T(128)S(1)}, s32[4]{0:T(128)}, u32[]{:S(2)}) copy-start(s32[4]{0:T(128)} %count_ref.1) | copy-start | bytes 52
  8.3 14.2 %copy-start.1 = (f32[4,1024]{1,0:T(4,128)S(1)}, f32[4,1024]{1,0:T(4,128)}, u32[]{:S(2)}) copy-start(f32[4,1024]{1,0:T(4,128)} %rate_ref.1) | copy-start | bytes 49156
  8.3 14.2 %copy-start.8 = (f32[4,1024]{1,0:T(4,128)S(1)}, f32[4,1024]{1,0:T(4,128)}, u32[]{:S(2)}) copy-start(f32[4,1024]{1,0:T(4,128)} %param.13) | copy-start | bytes 49156
  8.3 14.2 %copy-start.9 = (f32[4,1024]{1,0:T(4,128)S(1)}, f32[4,1024]{1,0:T(4,128)}, u32[]{:S(2)}) copy-start(f32[4,1024]{1,0:T(4,128)} %param.16) | copy-start | bytes 49156
  8.3 14.2 %copy-start.10 = (f32[4,1024]{1,0:T(4,128)S(1)}, f32[4,1024]{1,0:T(4,128)}, u32[]{:S(2)}) copy-start(f32[4,1024]{1,0:T(4,128)} %param.15) | copy-start | bytes 49156
  8.3 14.2 %copy-start.11 = (f32[4,1024]{1,0:T(4,128)S(1)}, f32[4,1024]{1,0:T(4,128)}, u32[]{:S(2)}) copy-start(f32[4,1024]{1,0:T(4,128)} %param.14) | copy-start | bytes 49156
  8.3 14.2 %copy-start.12 = (f32[1024]{0:T(1024)S(1)}, f32[1024]{0:T(1024)}, u32[]{:S(2)}) copy-start(f32[1024]{0:T(1024)} %param.17) | copy-start | bytes 12292
  8.5 1.2 %collective-permute-start.1 = (f32[4,32]{1,0:T(4,128)S(1)}, f32[4,32]{1,0:T(4,128)S(1)}, u32[]{:S(2)}, u32[]{:S(2)}) collective-permute-start(f32[4,32]{1,0:T(4,128)S(1)} %partial.1), channel_id=1, source_target_pairs={{0,2},{2,0},{4,6},{6,4},{8,10},{10,8},{12,14},{14,12},{16,18},{18,... | collective-permute-start | bytes 1544 | tf_op jit(solution)/shard_map/ppermute | solution.py:26
  8.5 16.8 %collective-permute-start.8 = (bf16[128,512]{1,0:T(8,128)(2,1)S(1)}, bf16[128,512]{1,0:T(8,128)(2,1)S(1)}, u32[]{:S(2)}, u32[]{:S(2)}) collective-permute-start(bf16[128,512]{1,0:T(8,128)(2,1)S(1)} %far_by_cluster.1.refs_0_), channel_id=1, source_target_pairs={{0,1},{1,0},{2,3},{3,2},{4,5},{5,4},{6,7},{7,6},{8,9},{9,8},{10,11... | collective-permute-start | bytes 393224 | tf_op jit(solution)/shard_map/ppermute | solution.py:26
  9.7 5.3 %collective-permute-start.2 = (f32[4,32]{1,0:T(4,128)S(1)}, f32[4,32]{1,0:T(4,128)S(1)}, u32[]{:S(2)}, u32[]{:S(2)}) collective-permute-start(f32[4,32]{1,0:T(4,128)S(1)} %add.13), channel_id=1, source_target_pairs={{0,4},{2,6},{4,0},{6,2},{8,12},{10,14},{12,8},{14,10},{16,20},{18,... | collective-permute-start | bytes 1544 | tf_op jit(solution)/shard_map/ppermute | solution.py:26
  11.2 3.8 %collective-permute-start.5 = (bf16[8,1024]{1,0:T(8,128)(2,1)S(1)}, bf16[8,1024]{1,0:T(8,128)(2,1)S(1)}, u32[]{:S(2)}, u32[]{:S(2)}) collective-permute-start(bf16[8,1024]{1,0:T(8,128)(2,1)S(1)} %pad_maximum_fusion.own_ref), channel_id=1, source_target_pairs={{0,2},{2,0},{4,6},{6,4},{8,10},{10,8},{12,14},{14,12},{16,18},{18,... | collective-permute-start | bytes 49160 | tf_op jit(solution)/shard_map/ppermute | solution.py:26
  11.2 5.9 %collective-permute-start.4 = (bf16[8,1024]{1,0:T(8,128)(2,1)S(1)}, bf16[8,1024]{1,0:T(8,128)(2,1)S(1)}, u32[]{:S(2)}, u32[]{:S(2)}) collective-permute-start(bf16[8,1024]{1,0:T(8,128)(2,1)S(1)} %pad_maximum_fusion.own_ref), channel_id=1, source_target_pairs={{0,30},{2,4},{4,2},{6,8},{8,6},{10,12},{12,10},{14,16},{16,14},{18... | collective-permute-start | bytes 49160 | tf_op jit(solution)/shard_map/ppermute | solution.py:26
  17.2 3.6 %collective-permute-start.6 = (bf16[4,32]{1,0:T(4,128)(2,1)S(1)}, bf16[4,32]{1,0:T(4,128)(2,1)S(1)}, u32[]{:S(2)}, u32[]{:S(2)}) collective-permute-start(bf16[4,32]{1,0:T(4,128)(2,1)S(1)} %add_convert_fusion), channel_id=1, source_target_pairs={{0,8},{2,10},{4,12},{6,14},{8,0},{10,2},{12,4},{14,6},{16,24},{18,... | collective-permute-start | bytes 776 | tf_op jit(solution)/shard_map/ppermute | solution.py:26
  20.8 4.5 %collective-permute-start.7 = (bf16[4,64]{1,0:T(4,128)(2,1)S(1)}, bf16[4,64]{1,0:T(4,128)(2,1)S(1)}, u32[]{:S(2)}, u32[]{:S(2)}) collective-permute-start(bf16[4,64]{1,0:T(4,128)(2,1)S(1)} %pad_maximum_fusion.1.low_ref), channel_id=1, source_target_pairs={{0,16},{2,18},{4,20},{6,22},{8,24},{10,26},{12,28},{14,30},{16,0},... | collective-permute-start | bytes 1544 | tf_op jit(solution)/shard_map/ppermute | solution.py:26
  21.6 3.7 %collective-permute-start.9 = (f32[4,512]{1,0:T(4,128)S(1)}, f32[4,512]{1,0:T(4,128)S(1)}, u32[]{:S(2)}, u32[]{:S(2)}) collective-permute-start(f32[4,512]{1,0:T(4,128)S(1)} %get-tuple-element.17), channel_id=1, source_target_pairs={{0,1},{1,0},{2,3},{3,2},{4,5},{5,4},{6,7},{7,6},{8,9},{9,8},{10,11... | collective-permute-start | bytes 24584 | tf_op jit(solution)/shard_map/ppermute | solution.py:26

commit v3 on v2

--- a/solution.py
+++ b/solution.py
@@ -16,6 +16,7 @@
 time_step = 0.25
 
 IN_SMEM = pl.BlockSpec(memory_space=pltpu.SMEM)
+IN_HBM = pl.BlockSpec(memory_space=pltpu.HBM)
 IN_VMEM = pl.BlockSpec(memory_space=pltpu.VMEM)
 f32 = jnp.float32
 bf16 = jnp.bfloat16
@@ -26,6 +27,10 @@
     return lax.ppermute(block, axis, [(i, partner(i) % count) for i in range(count)])
 
 
+def in_hbm(block):
+    return pltpu.with_memory_space_constraint(block, pltpu.HBM)
+
+
 def place_of(parts, pos, h):
     return pos ^ h if parts == 2 else h
 
@@ -34,23 +39,40 @@
     return pl.ds(pl.multiple_of(start, PANEL), width)
 
 
-def deficit_kernel(rate_ref, out_ref):
-    out_ref[...] = (1.0 - jnp.exp(rate_ref[...])).astype(bf16)
-
-
-def partial_kernel(parts, pos_ref, deficit_ref, *refs):
-    column_refs, out_ref = refs[:parts], refs[parts]
+def pack_kernel(rate_hbm, column_hbm, deficit_ref, message_ref, rate_ref, sems):
+    rank, width = column_hbm.shape
+    rate_copy = pltpu.make_async_copy(rate_hbm, rate_ref, sems.at[0])
+    column_copy = pltpu.make_async_copy(column_hbm, message_ref.at[pl.ds(0, rank)], sems.at[1])
+    rate_copy.start()
+    column_copy.start()
+    rate_copy.wait()
+    deficit = (1.0 - jnp.exp(rate_ref[...])).astype(bf16)
+    deficit_ref[...] = deficit
+    wide = deficit.astype(f32)
+    pieces = [wide[:, k : k + width] for k in range(0, wide.shape[1], width)]
+    message_ref[rank:] = jnp.concatenate(pieces, axis=0).astype(bf16)
+    column_copy.wait()
+
+
+def partial_kernel(parts, rank, pos_ref, deficit_ref, *refs):
+    messages, (all_ref, out_ref) = refs[:parts], refs[parts:]
+    local_members = deficit_ref.shape[0]
     total = None
+    every = []
     for h in range(parts):
-        width = column_refs[h].shape[1]
+        width = messages[h].shape[1]
         piece = lax.dot_general(
             deficit_ref[:, span(place_of(parts, pos_ref[0], h) * width, width)],
-            column_refs[h][...],
+            messages[h][:rank],
             (((1,), (1,)), ((), ())),
             preferred_element_type=f32,
         )
         total = piece if total is None else total + piece
+        tail = messages[h][rank:].astype(f32)
+        cut = [tail[k : k + local_members] for k in range(0, tail.shape[0], local_members)]
+        every.append(jnp.concatenate(cut, axis=1))
     out_ref[...] = total
+    all_ref[...] = jnp.concatenate(every, axis=0).astype(bf16)
 
 
 def far_kernel(cluster_ref, own_cluster_ref, basis_ref, out_ref):
@@ -135,41 +157,55 @@
     def call(body, name, out_shape, specs, mib=2, flops=10**6, scratch=()):
         return pl.pallas_call(
             body,
-            out_shape=jax.ShapeDtypeStruct(*out_shape),
+            out_shape=[jax.ShapeDtypeStruct(*o) for o in out_shape],
             in_specs=specs,
-            out_specs=IN_VMEM,
+            out_specs=[IN_VMEM] * len(out_shape),
             scratch_shapes=scratch,
             compiler_params=pltpu.CompilerParams(vmem_limit_bytes=mib << 20),
             cost_estimate=pl.CostEstimate(flops=flops, bytes_accessed=1, transcendentals=0),
             name=name,
         )
 
-    columns = gathered(column_basis)
-    deficit = call(deficit_kernel, "deficit", ((local_members, elements), bf16), [IN_VMEM], flops=COST)(log_rate)
-    deficits = gathered(deficit)
-    far_by_cluster = call(
-        far_kernel, "far_by_cluster", ((cluster_total * rank_size, row_width), bf16), [IN_SMEM, IN_SMEM, IN_VMEM], flops=COST
+    width = column_basis.shape[1]
+    deficit, message = call(
+        pack_kernel,
+        "pack",
+        [((local_members, elements), bf16), ((rank_size + members, width), bf16)],
+        [IN_HBM] * 2,
+        flops=COST,
+        scratch=[pltpu.VMEM(log_rate.shape, f32), pltpu.SemaphoreType.DMA((2,))],
+    )(in_hbm(log_rate), in_hbm(column_basis))
+    messages = gathered(message)
+    (far_by_cluster,) = call(
+        far_kernel,
+        "far_by_cluster",
+        [((cluster_total * rank_size, row_width), bf16)],
+        [IN_SMEM, IN_SMEM, IN_VMEM],
+        flops=COST,
     )(far_clusters, (fault_pos // GROUP)[None], far_basis)
     far_all = gathered(far_by_cluster)
     deficit, far_by_cluster = lax.optimization_barrier((deficit, far_by_cluster))
-    partial_value = call(
-        functools.partial(partial_kernel, parts), "partial", ((local_members, rank_size), f32), [IN_SMEM] + [IN_VMEM] * (1 + parts), flops=COST
-    )(member_pos[None], deficit, *columns)
-    deficit_all = jnp.concatenate(deficits, axis=0)
+    deficit_all, partial_value = call(
+        functools.partial(partial_kernel, parts, rank_size),
+        "partial",
+        [((members, elements), bf16), ((local_members, rank_size), f32)],
+        [IN_SMEM] + [IN_VMEM] * (1 + parts),
+        flops=COST,
+    )(member_pos[None], deficit, *messages)
 
     total = partial_value + swapped(partial_value, "fault", lambda i: i ^ 1)
     near_side = swapped(deficit_all, "fault", lambda i: i ^ 1)
     far_side = swapped(deficit_all, "fault", lambda i: i + 1 if i % 2 else i - 1)
     bit = 2
     while bit < GROUP:
-        total = total + swapped(total, "fault", lambda i: i ^ bit)
+        total = total + swapped(total, "fault", lambda i: i ^ bit ^ 1)
         bit *= 2
-    low, far_side, near_side = lax.optimization_barrier((total.astype(bf16), far_side, near_side))
-
-    near_field = call(
+    low, near_side = lax.optimization_barrier((total.astype(bf16), near_side))
+
+    (near_field,) = call(
         functools.partial(near_kernel, own_panels, total_panels),
         "near",
-        ((members, row_width), f32),
+        [((members, row_width), f32)],
         [IN_SMEM] * 3 + [IN_VMEM] * 4,
         mib=8,
         flops=COST,
@@ -185,7 +221,7 @@
             low = jnp.concatenate([low, high], axis=1)
         if 2 * bit == fault_count:
             low, near_field = lax.optimization_barrier((low, near_field))
-        high = swapped(low, "fault", lambda i: i ^ bit)
+        high = swapped(low, "fault", lambda i: i ^ bit ^ 1)
         bit *= 2
 
     near_field = near_field.reshape(parts, local_members, row_width)
@@ -201,10 +237,10 @@
     scale = time_step / resistance
     base = log_rate - scale * (normal_stress[None, :] * evolution_effect * state_rate)
     state_next = log_state + time_step * state_rate
-    rate_next = call(
+    (rate_next,) = call(
         functools.partial(last_kernel, parts),
         "last",
-        ((local_members, elements), f32),
+        [((local_members, elements), f32)],
         [IN_SMEM] + [IN_VMEM] * (4 + 2 * parts),
         flops=COST,
     )(member_pos[None], low, high, *far_all, *near_rows, base, scale)

time: 26.3 us -> 23.5 us (0.89)
  waiting for transfers between devices: 9.77 us -> 8.12 us
  starting transfers between devices: 11.4 us -> 10.1 us
  Pallas kernels: 2.7 us -> 3.51 us
  local copies, waits for them, and re-layouts: 0.77 us -> 0.05 us
    ppermute x10 -> x9, waiting for transfers between devices: 9.77 us -> 8.12 us  [swapped(): lax.ppermute(block, axis, [(i, partner(i) % count) for i in range(count)])]
    ppermute x10 -> x9, starting transfers between devices: 11.4 us -> 10.1 us  [swapped(): lax.ppermute(block, axis, [(i, partner(i) % count) for i in range(count)])]
    pallas_call x5, Pallas kernels: 2.7 us -> 3.51 us  [the longest x1 1.15 us: per_device(): call(functools.partial(near_kernel, own_panels, total_panels), 'near', [(...]
    unnamed x26 -> x22, local copies, waits for them, and re-layouts: 0.76 us -> 0.05 us
  transfers between devices with their start and end apart: 10 -> 9, of which waited for: 5 -> 6; matrix products, arithmetic and copies ran while one was open for 3% -> 3% of each run, Pallas kernels for 7% -> 8%
where the time goes in v3:
time: 23.5 us; the launch traced here: 23.3 us
  starting transfers between devices  10.1 us (43%)
  waiting for transfers between devices  8.12 us (35%)
  Pallas kernels  3.51 us (15%)
  between operations  0.75 us (3%)
  other arithmetic  0.72 us (3%)
    ppermute x9, starting transfers between devices, swapped(): lax.ppermute(block, axis, [(i, partner(i) % count) for i in range(count)])  10.1 us
    ppermute x9, waiting for transfers between devices, swapped(): lax.ppermute(block, axis, [(i, partner(i) % count) for i in range(count)])  8.12 us
    pallas_call x1, Pallas kernels, per_device(): call(functools.partial(near_kernel, own_panels, total_panels), 'near', [(...  1.15 us
    pallas_call x1, Pallas kernels, per_device(): call(pack_kernel, 'pack', [((local_members, elements), bf16), ((rank_size...  0.83 us
    pallas_call x1, Pallas kernels, per_device(): call(functools.partial(last_kernel, parts), 'last', [((local_members, ele...  0.77 us
    add x1, other arithmetic, per_device(): state_next = log_state + time_step * state_rate  0.63 us
    pallas_call x1, Pallas kernels, per_device(): call(far_kernel, 'far_by_cluster', [((cluster_total * rank_size, row_widt...  0.62 us
  transfers between devices with their start and end apart: 9, of which 6 were waited for; matrix products, arithmetic and copies ran while one was open for 3% of the time, Pallas kernels for 8%

profile of v3, /device:TPU:0, one launch (start us, length us, event | category | flops | bytes accessed | tf_op | source)
XLA Modules:
  0.0 23.3 jit_solution(15803152908006647114)
XLA Ops:
  0.6 0.0 copy-start.1
  0.6 0.0 copy-start.2
  0.7 0.8 %pack.1 = (bf16[4,1024]{1,0:T(4,128)(2,1)S(1)}, bf16[40,512]{1,0:T(8,128)(2,1)S(1)}) custom-call(f32[4,1024]{1,0:T(4,128)} %rate_hbm.1, bf16[32,512]{1,0:T(8,128)(2,1)} %column_hbm.1), custom_call_target="tpu_custom_call" | custom-call | flops 1000000000 | bytes 1 | tf_op jit(solution)/shard_map/pack/pallas_call | solution.py:170
  1.5 3.0 %collective-permute-start = (bf16[40,512]{1,0:T(8,128)(2,1)S(1)}, bf16[40,512]{1,0:T(8,128)(2,1)S(1)}, u32[]{:S(2)}, u32[]{:S(2)}) collective-permute-start(bf16[40,512]{1,0:T(8,128)(2,1)S(1)} %get-tuple-element.13.refs_0_), channel_id=1, source_target_pairs={{0,1},{1,0},{2,3},{3,2},{4,5},{5,4},{6,7},{7,6},{8,9},{9,8},{10,11... | collective-permute-start | bytes 122888 | tf_op jit(solution)/shard_map/ppermute | solution.py:27
  4.5 0.0 copy-done.1
  4.5 0.0 copy-done.2
  4.5 0.0 copy-start
  4.5 0.0 copy-start.3
  4.5 0.0 copy-start.4
  4.6 0.6 %far_by_cluster.1.refs_0_ = bf16[128,512]{1,0:T(8,128)(2,1)S(1)} custom-call(s32[4,3]{1,0:T(4,128)S(1)} %copy-done.2, s32[1]{0:T(128)} %bitcast.1.own_cluster_ref, bf16[4,3,32,128]{3,2,1,0:T(8,128)(2,1)S(1)} %copy-done.1), custom_call_target="tpu_custom_call" | custom-call | flops 1000000000 | bytes 1 | tf_op jit(solution)/shard_map/far_by_cluster/pallas_call | solution.py:179
  5.2 1.3 %collective-permute-done.refs_1_ = bf16[40,512]{1,0:T(8,128)(2,1)S(1)} collective-permute-done((bf16[40,512]{1,0:T(8,128)(2,1)S(1)}, bf16[40,512]{1,0:T(8,128)(2,1)S(1)}, u32[]{:S(2)}, u32[]{:S(2)}) %collective-permute-start) | collective-permute-done | bytes 40992 | tf_op jit(solution)/shard_map/ppermute | solution.py:27
  6.5 0.0 copy-start.5
  6.5 0.0 copy-start.6
  6.5 0.0 copy-start.7
  6.5 0.0 copy-start.8
  6.5 0.0 copy-start.9
  6.5 0.0 copy-start.10
  6.5 0.1 partial.1
  6.7 0.0 collective-permute-start.1
  6.7 1.2 %collective-permute-done.1 = f32[4,32]{1,0:T(4,128)S(1)} collective-permute-done((f32[4,32]{1,0:T(4,128)S(1)}, f32[4,32]{1,0:T(4,128)S(1)}, u32[]{:S(2)}, u32[]{:S(2)}) %collective-permute-start.1) | collective-permute-done | bytes 544 | tf_op jit(solution)/shard_map/ppermute | solution.py:27
  7.8 1.8 %collective-permute-start.2 = (f32[4,32]{1,0:T(4,128)S(1)}, f32[4,32]{1,0:T(4,128)S(1)}, u32[]{:S(2)}, u32[]{:S(2)}) collective-permute-start(f32[4,32]{1,0:T(4,128)S(1)} %add.13), channel_id=1, source_target_pairs={{0,6},{2,4},{4,2},{6,0},{8,14},{10,12},{12,10},{14,8},{16,22},{18,... | collective-permute-start | bytes 1544 | tf_op jit(solution)/shard_map/ppermute | solution.py:27
  9.6 1.5 %collective-permute-start.7 = (bf16[128,512]{1,0:T(8,128)(2,1)S(1)}, bf16[128,512]{1,0:T(8,128)(2,1)S(1)}, u32[]{:S(2)}, u32[]{:S(2)}) collective-permute-start(bf16[128,512]{1,0:T(8,128)(2,1)S(1)} %far_by_cluster.1.refs_0_), channel_id=1, source_target_pairs={{0,1},{1,0},{2,3},{3,2},{4,5},{5,4},{6,7},{7,6},{8,9},{9,8},{10,11... | collective-permute-start | bytes 393224 | tf_op jit(solution)/shard_map/ppermute | solution.py:27
  11.1 3.2 %collective-permute-start.5 = (bf16[8,1024]{1,0:T(8,128)(2,1)S(1)}, bf16[8,1024]{1,0:T(8,128)(2,1)S(1)}, u32[]{:S(2)}, u32[]{:S(2)}) collective-permute-start(bf16[8,1024]{1,0:T(8,128)(2,1)S(1)} %get-tuple-element.15.own_ref), channel_id=1, source_target_pairs={{0,30},{2,4},{4,2},{6,8},{8,6},{10,12},{12,10},{14,16},{16,14},{18... | collective-permute-start | bytes 49160 | tf_op jit(solution)/shard_map/ppermute | solution.py:27
  14.4 0.0 collective-permute-start.3
  14.4 0.0 collective-permute-done.2
  14.4 1.2 %collective-permute-done.3.near_ref = bf16[8,1024]{1,0:T(8,128)(2,1)S(1)} collective-permute-done((bf16[8,1024]{1,0:T(8,128)(2,1)S(1)}, bf16[8,1024]{1,0:T(8,128)(2,1)S(1)}, u32[]{:S(2)}, u32[]{:S(2)}) %collective-permute-start.3) | collective-permute-done | bytes 16416 | tf_op jit(solution)/shard_map/ppermute | solution.py:27
  15.6 0.0 collective-permute-start.4
  15.6 1.4 %collective-permute-done.5.far_ref = bf16[8,1024]{1,0:T(8,128)(2,1)S(1)} collective-permute-done((bf16[8,1024]{1,0:T(8,128)(2,1)S(1)}, bf16[8,1024]{1,0:T(8,128)(2,1)S(1)}, u32[]{:S(2)}, u32[]{:S(2)}) %collective-permute-start.5) | collective-permute-done | bytes 16416 | tf_op jit(solution)/shard_map/ppermute | solution.py:27
  17.0 0.0 copy-done
  17.0 0.0 copy-done.3
  17.0 0.0 copy-done.4
  17.0 1.2 %near.1 = f32[8,512]{1,0:T(8,128)S(1)} custom-call(s32[4,24]{1,0:T(4,128)S(1)} %copy-done.3, s32[4]{0:T(128)S(1)} %copy-done.4, s32[1]{0:T(128)} %bitcast.2.pos_ref, bf16[8,1024]{1,0:T(8,128)(2,1)S(1)} %get-tuple-element.15.own_ref, bf16[8,1024]{1,0:T(8,128)(2,1)S(1)} %collective-permute-done.3.near_ref, bf16[8,1024]{1,0:T(8,128)(2,1)S(1)} %collective-permute-done.5.far_ref, ...), custom_call_target="tpu_custom_call" | custom-call | flops 1000000000 | bytes 1 | tf_op jit(solution)/shard_map/near/pallas_call | solution.py:205
  18.2 0.4 %collective-permute-done.4 = bf16[4,32]{1,0:T(4,128)(2,1)S(1)} collective-permute-done((bf16[4,32]{1,0:T(4,128)(2,1)S(1)}, bf16[4,32]{1,0:T(4,128)(2,1)S(1)}, u32[]{:S(2)}, u32[]{:S(2)}) %collective-permute-start.4) | collective-permute-done | bytes 288 | tf_op jit(solution)/shard_map/ppermute | solution.py:27
  18.5 0.1 pad_maximum_fusion.low_ref
  18.6 0.0 collective-permute-start.6
  18.7 0.6 %collective-permute-start.8 = (f32[4,512]{1,0:T(4,128)S(1)}, f32[4,512]{1,0:T(4,128)S(1)}, u32[]{:S(2)}, u32[]{:S(2)}) collective-permute-start(f32[4,512]{1,0:T(4,128)S(1)} %get-tuple-element.23), channel_id=1, source_target_pairs={{0,1},{1,0},{2,3},{3,2},{4,5},{5,4},{6,7},{7,6},{8,9},{9,8},{10,11... | collective-permute-start | bytes 24584 | tf_op jit(solution)/shard_map/ppermute | solution.py:27
  19.2 0.0 copy-done.5
  19.2 0.0 copy-done.6
  19.2 0.0 copy-done.7
  19.2 0.0 copy-done.8
  19.2 0.0 copy-done.9
  19.2 0.0 copy-done.10
  19.3 0.6 %multiply_add_fusion = (f32[4,1024]{1,0:T(4,128)}, f32[4,1024]{1,0:T(4,128)S(1)}, f32[4,1024]{1,0:T(4,128)S(1)}) fusion(f32[4,1024]{1,0:T(4,128)S(1)} %copy-done.6, f32[4,1024]{1,0:T(4,128)S(1)} %copy-done.7, f32[4,1024]{1,0:T(4,128)S(1)} %copy-done.5, f32[4,1024]{1,0:T(4,128)S(1)} %copy-done.8, f32[4,1024]{1,0:T(4,128)S(1)} %copy-done.9, f32[1024]{0:T(1024)S(1)} %copy-done.10), kind=kLoop, calls=%fused_computation | loop fusion | flops 53248 | bytes 135168 | tf_op jit(solution)/shard_map/add | solution.py:239
  19.9 2.6 %collective-permute-done.6.high_ref = bf16[4,64]{1,0:T(4,128)(2,1)S(1)} collective-permute-done((bf16[4,64]{1,0:T(4,128)(2,1)S(1)}, bf16[4,64]{1,0:T(4,128)(2,1)S(1)}, u32[]{:S(2)}, u32[]{:S(2)}) %collective-permute-start.6) | collective-permute-done | bytes 544 | tf_op jit(solution)/shard_map/ppermute | solution.py:27
  22.5 0.0 collective-permute-done.8.refs_3_
  22.5 0.0 collective-permute-done.7.refs_1_
  22.5 0.8 %last.1 = f32[4,1024]{1,0:T(4,128)} custom-call(s32[1]{0:T(128)} %bitcast.pos_ref, bf16[4,64]{1,0:T(4,128)(2,1)S(1)} %pad_maximum_fusion.low_ref, bf16[4,64]{1,0:T(4,128)(2,1)S(1)} %collective-permute-done.6.high_ref, bf16[128,512]{1,0:T(8,128)(2,1)S(1)} %far_by_cluster.1.refs_0_, bf16[128,512]{1,0:T(8,128)(2,1)S(1)} %collective-permute-done.7.refs_1_, ...), custom_call_target="tpu_custom_call" | custom-call | flops 1000000000 | bytes 1 | tf_op jit(solution)/shard_map/last/pallas_call | solution.py:240
  (3 shorter events, 0.0 us)
Async XLA Ops:
  0.6 3.9 %copy-start.1 = (bf16[4,3,32,128]{3,2,1,0:T(8,128)(2,1)S(1)}, bf16[4,3,32,128]{3,2,1,0:T(8,128)(2,1)}, u32[]{:S(2)}) copy-start(bf16[4,3,32,128]{3,2,1,0:T(8,128)(2,1)} %basis_ref.1) | copy-start | bytes 294916
  0.6 3.9 %copy-start.2 = (s32[4,3]{1,0:T(4,128)S(1)}, s32[4,3]{1,0:T(4,128)}, u32[]{:S(2)}) copy-start(s32[4,3]{1,0:T(4,128)} %cluster_ref.1) | copy-start | bytes 148
  1.5 5.0 %collective-permute-start = (bf16[40,512]{1,0:T(8,128)(2,1)S(1)}, bf16[40,512]{1,0:T(8,128)(2,1)S(1)}, u32[]{:S(2)}, u32[]{:S(2)}) collective-permute-start(bf16[40,512]{1,0:T(8,128)(2,1)S(1)} %get-tuple-element.13.refs_0_), channel_id=1, source_target_pairs={{0,1},{1,0},{2,3},{3,2},{4,5},{5,4},{6,7},{7,6},{8,9},{9,8},{10,11... | collective-permute-start | bytes 122888 | tf_op jit(solution)/shard_map/ppermute | solution.py:27
  4.5 12.5 %copy-start = (bf16[4,24,128,128]{3,2,1,0:T(8,128)(2,1)S(1)}, bf16[4,24,128,128]{3,2,1,0:T(8,128)(2,1)}, u32[]{:S(2)}) copy-start(bf16[4,24,128,128]{3,2,1,0:T(8,128)(2,1)} %blocks_ref.1) | copy-start | bytes 9437188
  4.5 12.5 %copy-start.3 = (s32[4,24]{1,0:T(4,128)S(1)}, s32[4,24]{1,0:T(4,128)}, u32[]{:S(2)}) copy-start(s32[4,24]{1,0:T(4,128)} %column_ref.1) | copy-start | bytes 1156
  4.5 12.5 %copy-start.4 = (s32[4]{0:T(128)S(1)}, s32[4]{0:T(128)}, u32[]{:S(2)}) copy-start(s32[4]{0:T(128)} %count_ref.1) | copy-start | bytes 52
  6.5 12.7 %copy-start.5 = (f32[4,1024]{1,0:T(4,128)S(1)}, f32[4,1024]{1,0:T(4,128)}, u32[]{:S(2)}) copy-start(f32[4,1024]{1,0:T(4,128)} %rate_hbm.1) | copy-start | bytes 49156
  6.5 12.7 %copy-start.6 = (f32[4,1024]{1,0:T(4,128)S(1)}, f32[4,1024]{1,0:T(4,128)}, u32[]{:S(2)}) copy-start(f32[4,1024]{1,0:T(4,128)} %param.13) | copy-start | bytes 49156
  6.5 12.7 %copy-start.7 = (f32[4,1024]{1,0:T(4,128)S(1)}, f32[4,1024]{1,0:T(4,128)}, u32[]{:S(2)}) copy-start(f32[4,1024]{1,0:T(4,128)} %param.16) | copy-start | bytes 49156
  6.5 12.7 %copy-start.8 = (f32[4,1024]{1,0:T(4,128)S(1)}, f32[4,1024]{1,0:T(4,128)}, u32[]{:S(2)}) copy-start(f32[4,1024]{1,0:T(4,128)} %param.15) | copy-start | bytes 49156
  6.5 12.7 %copy-start.9 = (f32[4,1024]{1,0:T(4,128)S(1)}, f32[4,1024]{1,0:T(4,128)}, u32[]{:S(2)}) copy-start(f32[4,1024]{1,0:T(4,128)} %param.14) | copy-start | bytes 49156
  6.5 12.7 %copy-start.10 = (f32[1024]{0:T(1024)S(1)}, f32[1024]{0:T(1024)}, u32[]{:S(2)}) copy-start(f32[1024]{0:T(1024)} %param.17) | copy-start | bytes 12292
  6.7 1.2 %collective-permute-start.1 = (f32[4,32]{1,0:T(4,128)S(1)}, f32[4,32]{1,0:T(4,128)S(1)}, u32[]{:S(2)}, u32[]{:S(2)}) collective-permute-start(f32[4,32]{1,0:T(4,128)S(1)} %get-tuple-element.14), channel_id=1, source_target_pairs={{0,2},{2,0},{4,6},{6,4},{8,10},{10,8},{12,14},{14,12},{16,18},{18,... | collective-permute-start | bytes 1544 | tf_op jit(solution)/shard_map/ppermute | solution.py:27
  7.8 6.5 %collective-permute-start.2 = (f32[4,32]{1,0:T(4,128)S(1)}, f32[4,32]{1,0:T(4,128)S(1)}, u32[]{:S(2)}, u32[]{:S(2)}) collective-permute-start(f32[4,32]{1,0:T(4,128)S(1)} %add.13), channel_id=1, source_target_pairs={{0,6},{2,4},{4,2},{6,0},{8,14},{10,12},{12,10},{14,8},{16,22},{18,... | collective-permute-start | bytes 1544 | tf_op jit(solution)/shard_map/ppermute | solution.py:27
  9.6 12.9 %collective-permute-start.7 = (bf16[128,512]{1,0:T(8,128)(2,1)S(1)}, bf16[128,512]{1,0:T(8,128)(2,1)S(1)}, u32[]{:S(2)}, u32[]{:S(2)}) collective-permute-start(bf16[128,512]{1,0:T(8,128)(2,1)S(1)} %far_by_cluster.1.refs_0_), channel_id=1, source_target_pairs={{0,1},{1,0},{2,3},{3,2},{4,5},{5,4},{6,7},{7,6},{8,9},{9,8},{10,11... | collective-permute-start | bytes 393224 | tf_op jit(solution)/shard_map/ppermute | solution.py:27
  11.1 5.9 %collective-permute-start.5 = (bf16[8,1024]{1,0:T(8,128)(2,1)S(1)}, bf16[8,1024]{1,0:T(8,128)(2,1)S(1)}, u32[]{:S(2)}, u32[]{:S(2)}) collective-permute-start(bf16[8,1024]{1,0:T(8,128)(2,1)S(1)} %get-tuple-element.15.own_ref), channel_id=1, source_target_pairs={{0,30},{2,4},{4,2},{6,8},{8,6},{10,12},{12,10},{14,16},{16,14},{18... | collective-permute-start | bytes 49160 | tf_op jit(solution)/shard_map/ppermute | solution.py:27
  14.4 1.2 %collective-permute-start.3 = (bf16[8,1024]{1,0:T(8,128)(2,1)S(1)}, bf16[8,1024]{1,0:T(8,128)(2,1)S(1)}, u32[]{:S(2)}, u32[]{:S(2)}) collective-permute-start(bf16[8,1024]{1,0:T(8,128)(2,1)S(1)} %get-tuple-element.15.own_ref), channel_id=1, source_target_pairs={{0,2},{2,0},{4,6},{6,4},{8,10},{10,8},{12,14},{14,12},{16,18},{18,... | collective-permute-start | bytes 49160 | tf_op jit(solution)/shard_map/ppermute | solution.py:27
  15.6 3.0 %collective-permute-start.4 = (bf16[4,32]{1,0:T(4,128)(2,1)S(1)}, bf16[4,32]{1,0:T(4,128)(2,1)S(1)}, u32[]{:S(2)}, u32[]{:S(2)}) collective-permute-start(bf16[4,32]{1,0:T(4,128)(2,1)S(1)} %add_convert_fusion), channel_id=1, source_target_pairs={{0,10},{2,8},{4,14},{6,12},{8,2},{10,0},{12,6},{14,4},{16,26},{18,... | collective-permute-start | bytes 776 | tf_op jit(solution)/shard_map/ppermute | solution.py:27
  18.6 3.9 %collective-permute-start.6 = (bf16[4,64]{1,0:T(4,128)(2,1)S(1)}, bf16[4,64]{1,0:T(4,128)(2,1)S(1)}, u32[]{:S(2)}, u32[]{:S(2)}) collective-permute-start(bf16[4,64]{1,0:T(4,128)(2,1)S(1)} %pad_maximum_fusion.low_ref), channel_id=1, source_target_pairs={{0,18},{2,16},{4,22},{6,20},{8,26},{10,24},{12,30},{14,28},{16,2},... | collective-permute-start | bytes 1544 | tf_op jit(solution)/shard_map/ppermute | solution.py:27
  18.7 3.9 %collective-permute-start.8 = (f32[4,512]{1,0:T(4,128)S(1)}, f32[4,512]{1,0:T(4,128)S(1)}, u32[]{:S(2)}, u32[]{:S(2)}) collective-permute-start(f32[4,512]{1,0:T(4,128)S(1)} %get-tuple-element.23), channel_id=1, source_target_pairs={{0,1},{1,0},{2,3},{3,2},{4,5},{5,4},{6,7},{7,6},{8,9},{9,8},{10,11... | collective-permute-start | bytes 24584 | tf_op jit(solution)/shard_map/ppermute | solution.py:27

commit v4 on v2

--- a/solution.py
+++ b/solution.py
@@ -16,6 +16,7 @@
 time_step = 0.25
 
 IN_SMEM = pl.BlockSpec(memory_space=pltpu.SMEM)
+IN_HBM = pl.BlockSpec(memory_space=pltpu.HBM)
 IN_VMEM = pl.BlockSpec(memory_space=pltpu.VMEM)
 f32 = jnp.float32
 bf16 = jnp.bfloat16
@@ -24,6 +25,10 @@
 def swapped(block, axis, partner):
     count = lax.axis_size(axis)
     return lax.ppermute(block, axis, [(i, partner(i) % count) for i in range(count)])
+
+
+def in_hbm(block):
+    return pltpu.with_memory_space_constraint(block, pltpu.HBM)
 
 
 def place_of(parts, pos, h):
@@ -135,41 +140,54 @@
     def call(body, name, out_shape, specs, mib=2, flops=10**6, scratch=()):
         return pl.pallas_call(
             body,
-            out_shape=jax.ShapeDtypeStruct(*out_shape),
+            out_shape=[jax.ShapeDtypeStruct(*o) for o in out_shape],
             in_specs=specs,
-            out_specs=IN_VMEM,
+            out_specs=[IN_VMEM] * len(out_shape),
             scratch_shapes=scratch,
             compiler_params=pltpu.CompilerParams(vmem_limit_bytes=mib << 20),
             cost_estimate=pl.CostEstimate(flops=flops, bytes_accessed=1, transcendentals=0),
             name=name,
         )
 
-    columns = gathered(column_basis)
-    deficit = call(deficit_kernel, "deficit", ((local_members, elements), bf16), [IN_VMEM], flops=COST)(log_rate)
-    deficits = gathered(deficit)
-    far_by_cluster = call(
-        far_kernel, "far_by_cluster", ((cluster_total * rank_size, row_width), bf16), [IN_SMEM, IN_SMEM, IN_VMEM], flops=COST
-    )(far_clusters, (fault_pos // GROUP)[None], far_basis)
+    if parts == 2:
+        other = swapped(in_hbm(column_basis), "member", lambda i: i ^ 1)
+        columns = [column_basis, pltpu.with_memory_space_constraint(other, pltpu.VMEM)]
+    else:
+        columns = gathered(column_basis)
+    (far_by_cluster,) = call(
+        far_kernel,
+        "far_by_cluster",
+        [((cluster_total * rank_size, row_width), bf16)],
+        [IN_SMEM, IN_SMEM, IN_VMEM],
+        flops=COST,
+    )(in_hbm(far_clusters), (fault_pos // GROUP)[None], in_hbm(far_basis))
     far_all = gathered(far_by_cluster)
-    deficit, far_by_cluster = lax.optimization_barrier((deficit, far_by_cluster))
-    partial_value = call(
-        functools.partial(partial_kernel, parts), "partial", ((local_members, rank_size), f32), [IN_SMEM] + [IN_VMEM] * (1 + parts), flops=COST
+    log_rate_later, far_by_cluster = lax.optimization_barrier((log_rate, far_by_cluster))
+    (deficit,) = call(
+        deficit_kernel, "deficit", [((local_members, elements), bf16)], [IN_VMEM], flops=COST
+    )(log_rate_later)
+    deficit_all = jnp.concatenate(gathered(deficit), axis=0)
+    (partial_value,) = call(
+        functools.partial(partial_kernel, parts),
+        "partial",
+        [((local_members, rank_size), f32)],
+        [IN_SMEM] + [IN_VMEM] * (1 + parts),
+        flops=COST,
     )(member_pos[None], deficit, *columns)
-    deficit_all = jnp.concatenate(deficits, axis=0)
 
     total = partial_value + swapped(partial_value, "fault", lambda i: i ^ 1)
     near_side = swapped(deficit_all, "fault", lambda i: i ^ 1)
     far_side = swapped(deficit_all, "fault", lambda i: i + 1 if i % 2 else i - 1)
     bit = 2
     while bit < GROUP:
-        total = total + swapped(total, "fault", lambda i: i ^ bit)
+        total = total + swapped(total, "fault", lambda i: i ^ bit ^ 1)
         bit *= 2
-    low, far_side, near_side = lax.optimization_barrier((total.astype(bf16), far_side, near_side))
-
-    near_field = call(
+    low, near_side = lax.optimization_barrier((total.astype(bf16), near_side))
+
+    (near_field,) = call(
         functools.partial(near_kernel, own_panels, total_panels),
         "near",
-        ((members, row_width), f32),
+        [((members, row_width), f32)],
         [IN_SMEM] * 3 + [IN_VMEM] * 4,
         mib=8,
         flops=COST,
@@ -185,7 +203,7 @@
             low = jnp.concatenate([low, high], axis=1)
         if 2 * bit == fault_count:
             low, near_field = lax.optimization_barrier((low, near_field))
-        high = swapped(low, "fault", lambda i: i ^ bit)
+        high = swapped(low, "fault", lambda i: i ^ bit ^ 1)
         bit *= 2
 
     near_field = near_field.reshape(parts, local_members, row_width)
@@ -201,10 +219,10 @@
     scale = time_step / resistance
     base = log_rate - scale * (normal_stress[None, :] * evolution_effect * state_rate)
     state_next = log_state + time_step * state_rate
-    rate_next = call(
+    (rate_next,) = call(
         functools.partial(last_kernel, parts),
         "last",
-        ((local_members, elements), f32),
+        [((local_members, elements), f32)],
         [IN_SMEM] + [IN_VMEM] * (4 + 2 * parts),
         flops=COST,
     )(member_pos[None], low, high, *far_all, *near_rows, base, scale)

time: 26.3 us -> 22.1 us (0.84)
  waiting for transfers between devices: 9.77 us -> 5.99 us
  local copies, waits for them, and re-layouts: 0.77 us -> 0.06 us
  Pallas kernels: 2.7 us -> 3.04 us
    ppermute x10, waiting for transfers between devices: 9.77 us -> 5.99 us  [swapped(): lax.ppermute(block, axis, [(i, partner(i) % count) for i in range(count)])]
    unnamed x26 -> x20, local copies, waits for them, and re-layouts: 0.76 us -> 0.05 us
    pallas_call x5, Pallas kernels: 2.7 us -> 3.04 us  [the longest x1 1.17 us: per_device(): call(functools.partial(near_kernel, own_panels, total_panels), 'near', [(...]
  transfers between devices with their start and end apart: 10 -> 10, of which waited for: 5 -> 5; matrix products, arithmetic and copies ran while one was open for 3% -> 3% of each run, Pallas kernels for 7% -> 10%
where the time goes in v4:
time: 22.1 us; the launch traced here: 21.9 us
  starting transfers between devices  11.3 us (51%)
  waiting for transfers between devices  5.99 us (27%)
  Pallas kernels  3.04 us (14%)
  between operations  0.76 us (3%)
  other arithmetic  0.73 us (3%)
    ppermute x10, starting transfers between devices, swapped(): lax.ppermute(block, axis, [(i, partner(i) % count) for i in range(count)])  11.3 us
    ppermute x10, waiting for transfers between devices, swapped(): lax.ppermute(block, axis, [(i, partner(i) % count) for i in range(count)])  5.99 us
    pallas_call x1, Pallas kernels, per_device(): call(functools.partial(near_kernel, own_panels, total_panels), 'near', [(...  1.17 us
    pallas_call x1, Pallas kernels, per_device(): call(far_kernel, 'far_by_cluster', [((cluster_total * rank_size, row_widt...  0.96 us
    pallas_call x1, Pallas kernels, per_device(): call(functools.partial(last_kernel, parts), 'last', [((local_members, ele...  0.77 us
    add x1, other arithmetic, per_device(): state_next = log_state + time_step * state_rate  0.64 us
  transfers between devices with their start and end apart: 10, of which 5 were waited for; matrix products, arithmetic and copies ran while one was open for 3% of the time, Pallas kernels for 10%

profile of v4, /device:TPU:0, one launch (start us, length us, event | category | flops | bytes accessed | tf_op | source)
XLA Modules:
  0.0 21.9 jit_solution(6444854657515005487)
XLA Ops:
  0.6 0.0 copy-start
  0.6 3.0 %collective-permute-start = (bf16[32,512]{1,0:T(8,128)(2,1)}, bf16[32,512]{1,0:T(8,128)(2,1)S(1)}, u32[]{:S(2)}, u32[]{:S(2)}) collective-permute-start(bf16[32,512]{1,0:T(8,128)(2,1)} %refs_0_.1), channel_id=1, source_target_pairs={{0,1},{1,0},{2,3},{3,2},{4,5},{5,4},{6,7},{7,6},{8,9},{9,8},{10,11... | collective-permute-start | bytes 98312 | tf_op jit(solution)/shard_map/ppermute | solution.py:27
  3.7 0.0 copy-start.2
  3.7 1.0 %far_by_cluster.1.refs_0_ = bf16[128,512]{1,0:T(8,128)(2,1)S(1)} custom-call(s32[4,3]{1,0:T(4,128)} %cluster_ref.1, s32[1]{0:T(128)} %bitcast.1.own_cluster_ref, bf16[4,3,32,128]{3,2,1,0:T(8,128)(2,1)} %basis_ref.1), custom_call_target="tpu_custom_call" | custom-call | flops 1000000000 | bytes 1 | tf_op jit(solution)/shard_map/far_by_cluster/pallas_call | solution.py:157
  4.6 0.0 copy-done
  4.7 0.0 copy-start.1
  4.7 0.0 copy-start.3
  4.7 0.0 copy-start.4
  4.7 0.1 collective-permute-start.3
  4.8 1.0 %collective-permute-done.refs_1_ = bf16[32,512]{1,0:T(8,128)(2,1)S(1)} collective-permute-done((bf16[32,512]{1,0:T(8,128)(2,1)}, bf16[32,512]{1,0:T(8,128)(2,1)S(1)}, u32[]{:S(2)}, u32[]{:S(2)}) %collective-permute-start) | collective-permute-done | bytes 32800 | tf_op jit(solution)/shard_map/ppermute | solution.py:27
  5.8 0.0 copy-done.2
  5.8 0.0 copy-start.5
  5.8 0.0 copy-start.6
  5.8 0.0 copy-start.7
  5.8 0.0 copy-start.8
  5.8 0.0 copy-start.9
  5.8 0.1 partial.1
  5.9 0.0 collective-permute-start.1
  6.0 2.1 %collective-permute-start.8 = (bf16[128,512]{1,0:T(8,128)(2,1)S(1)}, bf16[128,512]{1,0:T(8,128)(2,1)S(1)}, u32[]{:S(2)}, u32[]{:S(2)}) collective-permute-start(bf16[128,512]{1,0:T(8,128)(2,1)S(1)} %far_by_cluster.1.refs_0_), channel_id=1, source_target_pairs={{0,1},{1,0},{2,3},{3,2},{4,5},{5,4},{6,7},{7,6},{8,9},{9,8},{10,11... | collective-permute-start | bytes 393224 | tf_op jit(solution)/shard_map/ppermute | solution.py:27
  8.0 0.0 collective-permute-done.1
  8.0 1.4 %collective-permute-start.2 = (f32[4,32]{1,0:T(4,128)S(1)}, f32[4,32]{1,0:T(4,128)S(1)}, u32[]{:S(2)}, u32[]{:S(2)}) collective-permute-start(f32[4,32]{1,0:T(4,128)S(1)} %add.13), channel_id=1, source_target_pairs={{0,6},{2,4},{4,2},{6,0},{8,14},{10,12},{12,10},{14,8},{16,22},{18,... | collective-permute-start | bytes 1544 | tf_op jit(solution)/shard_map/ppermute | solution.py:27
  9.4 0.0 collective-permute-done.3
  9.4 3.6 %collective-permute-start.6 = (bf16[8,1024]{1,0:T(8,128)(2,1)S(1)}, bf16[8,1024]{1,0:T(8,128)(2,1)S(1)}, u32[]{:S(2)}, u32[]{:S(2)}) collective-permute-start(bf16[8,1024]{1,0:T(8,128)(2,1)S(1)} %pad_maximum_fusion.own_ref), channel_id=1, source_target_pairs={{0,30},{2,4},{4,2},{6,8},{8,6},{10,12},{12,10},{14,16},{16,14},{18... | collective-permute-start | bytes 49160 | tf_op jit(solution)/shard_map/ppermute | solution.py:27
  13.0 0.0 collective-permute-start.4
  13.0 0.0 collective-permute-done.2
  13.0 1.2 %collective-permute-done.4.near_ref = bf16[8,1024]{1,0:T(8,128)(2,1)S(1)} collective-permute-done((bf16[8,1024]{1,0:T(8,128)(2,1)S(1)}, bf16[8,1024]{1,0:T(8,128)(2,1)S(1)}, u32[]{:S(2)}, u32[]{:S(2)}) %collective-permute-start.4) | collective-permute-done | bytes 16416 | tf_op jit(solution)/shard_map/ppermute | solution.py:27
  14.1 0.0 collective-permute-start.5
  14.1 1.2 %collective-permute-done.6.far_ref = bf16[8,1024]{1,0:T(8,128)(2,1)S(1)} collective-permute-done((bf16[8,1024]{1,0:T(8,128)(2,1)S(1)}, bf16[8,1024]{1,0:T(8,128)(2,1)S(1)}, u32[]{:S(2)}, u32[]{:S(2)}) %collective-permute-start.6) | collective-permute-done | bytes 16416 | tf_op jit(solution)/shard_map/ppermute | solution.py:27
  15.3 0.0 copy-done.1
  15.3 0.0 copy-done.3
  15.3 0.0 copy-done.4
  15.3 1.2 %near.1 = f32[8,512]{1,0:T(8,128)S(1)} custom-call(s32[4,24]{1,0:T(4,128)S(1)} %copy-done.3, s32[4]{0:T(128)S(1)} %copy-done.4, s32[1]{0:T(128)} %bitcast.2.pos_ref, bf16[8,1024]{1,0:T(8,128)(2,1)S(1)} %pad_maximum_fusion.own_ref, bf16[8,1024]{1,0:T(8,128)(2,1)S(1)} %collective-permute-done.4.near_ref, bf16[8,1024]{1,0:T(8,128)(2,1)S(1)} %collective-permute-done.6.far_ref, ...), custom_call_target="tpu_custom_call" | custom-call | flops 1000000000 | bytes 1 | tf_op jit(solution)/shard_map/near/pallas_call | solution.py:187
  16.5 0.6 %collective-permute-done.5 = bf16[4,32]{1,0:T(4,128)(2,1)S(1)} collective-permute-done((bf16[4,32]{1,0:T(4,128)(2,1)S(1)}, bf16[4,32]{1,0:T(4,128)(2,1)S(1)}, u32[]{:S(2)}, u32[]{:S(2)}) %collective-permute-start.5) | collective-permute-done | bytes 288 | tf_op jit(solution)/shard_map/ppermute | solution.py:27
  17.1 0.1 pad_maximum_fusion.1.low_ref
  17.2 0.0 collective-permute-start.7
  17.2 1.2 %collective-permute-start.9 = (f32[4,512]{1,0:T(4,128)S(1)}, f32[4,512]{1,0:T(4,128)S(1)}, u32[]{:S(2)}, u32[]{:S(2)}) collective-permute-start(f32[4,512]{1,0:T(4,128)S(1)} %get-tuple-element.15), channel_id=1, source_target_pairs={{0,1},{1,0},{2,3},{3,2},{4,5},{5,4},{6,7},{7,6},{8,9},{9,8},{10,11... | collective-permute-start | bytes 24584 | tf_op jit(solution)/shard_map/ppermute | solution.py:27
  18.4 0.0 copy-done.5
  18.4 0.0 copy-done.6
  18.4 0.0 copy-done.7
  18.4 0.0 copy-done.8
  18.4 0.0 copy-done.9
  18.5 0.6 %multiply_add_fusion = (f32[4,1024]{1,0:T(4,128)}, f32[4,1024]{1,0:T(4,128)S(1)}, f32[4,1024]{1,0:T(4,128)S(1)}) fusion(f32[4,1024]{1,0:T(4,128)S(1)} %copy-done.5, f32[4,1024]{1,0:T(4,128)S(1)} %copy-done.6, f32[4,1024]{1,0:T(4,128)S(1)} %copy-done, f32[4,1024]{1,0:T(4,128)S(1)} %copy-done.7, f32[4,1024]{1,0:T(4,128)S(1)} %copy-done.8, f32[1024]{0:T(1024)S(1)} %copy-done.9), kind=kLoop, calls=%fused_computation.1 | loop fusion | flops 53248 | bytes 135168 | tf_op jit(solution)/shard_map/add | solution.py:221
  19.1 2.0 %collective-permute-done.7.high_ref = bf16[4,64]{1,0:T(4,128)(2,1)S(1)} collective-permute-done((bf16[4,64]{1,0:T(4,128)(2,1)S(1)}, bf16[4,64]{1,0:T(4,128)(2,1)S(1)}, u32[]{:S(2)}, u32[]{:S(2)}) %collective-permute-start.7) | collective-permute-done | bytes 544 | tf_op jit(solution)/shard_map/ppermute | solution.py:27
  21.1 0.0 collective-permute-done.9.refs_3_
  21.1 0.0 collective-permute-done.8.refs_1_
  21.1 0.8 %last.1 = f32[4,1024]{1,0:T(4,128)} custom-call(s32[1]{0:T(128)} %bitcast.pos_ref, bf16[4,64]{1,0:T(4,128)(2,1)S(1)} %pad_maximum_fusion.1.low_ref, bf16[4,64]{1,0:T(4,128)(2,1)S(1)} %collective-permute-done.7.high_ref, bf16[128,512]{1,0:T(8,128)(2,1)S(1)} %far_by_cluster.1.refs_0_, bf16[128,512]{1,0:T(8,128)(2,1)S(1)} %collective-permute-done.8.refs_1_, ...), custom_call_target="tpu_custom_call" | custom-call | flops 1000000000 | bytes 1 | tf_op jit(solution)/shard_map/last/pallas_call | solution.py:222
  (5 shorter events, 0.0 us)
Async XLA Ops:
  0.6 4.0 %copy-start = (f32[4,1024]{1,0:T(4,128)S(1)}, f32[4,1024]{1,0:T(4,128)}, u32[]{:S(2)}) copy-start(f32[4,1024]{1,0:T(4,128)} %rate_ref) | copy-start | bytes 49156
  0.6 5.1 %collective-permute-start = (bf16[32,512]{1,0:T(8,128)(2,1)}, bf16[32,512]{1,0:T(8,128)(2,1)S(1)}, u32[]{:S(2)}, u32[]{:S(2)}) collective-permute-start(bf16[32,512]{1,0:T(8,128)(2,1)} %refs_0_.1), channel_id=1, source_target_pairs={{0,1},{1,0},{2,3},{3,2},{4,5},{5,4},{6,7},{7,6},{8,9},{9,8},{10,11... | collective-permute-start | bytes 98312 | tf_op jit(solution)/shard_map/ppermute | solution.py:27
  3.7 2.1 %copy-start.2 = (bf16[32,512]{1,0:T(8,128)(2,1)S(1)}, bf16[32,512]{1,0:T(8,128)(2,1)}, u32[]{:S(2)}) copy-start(bf16[32,512]{1,0:T(8,128)(2,1)} %refs_0_.1) | copy-start | bytes 98308
  4.7 10.7 %copy-start.1 = (bf16[4,24,128,128]{3,2,1,0:T(8,128)(2,1)S(1)}, bf16[4,24,128,128]{3,2,1,0:T(8,128)(2,1)}, u32[]{:S(2)}) copy-start(bf16[4,24,128,128]{3,2,1,0:T(8,128)(2,1)} %blocks_ref.1) | copy-start | bytes 9437188
  4.7 10.7 %copy-start.3 = (s32[4,24]{1,0:T(4,128)S(1)}, s32[4,24]{1,0:T(4,128)}, u32[]{:S(2)}) copy-start(s32[4,24]{1,0:T(4,128)} %column_ref.1) | copy-start | bytes 1156
  4.7 10.7 %copy-start.4 = (s32[4]{0:T(128)S(1)}, s32[4]{0:T(128)}, u32[]{:S(2)}) copy-start(s32[4]{0:T(128)} %count_ref.1) | copy-start | bytes 52
  4.7 4.7 %collective-permute-start.3 = (bf16[4,1024]{1,0:T(4,128)(2,1)S(1)}, bf16[4,1024]{1,0:T(4,128)(2,1)S(1)}, u32[]{:S(2)}, u32[]{:S(2)}) collective-permute-start(bf16[4,1024]{1,0:T(4,128)(2,1)S(1)} %deficit.1.deficit_ref), channel_id=1, source_target_pairs={{0,1},{1,0},{2,3},{3,2},{4,5},{5,4},{6,7},{7,6},{8,9},{9,8},{10,11... | collective-permute-start | bytes 24584 | tf_op jit(solution)/shard_map/ppermute | solution.py:27
  5.8 12.6 %copy-start.5 = (f32[4,1024]{1,0:T(4,128)S(1)}, f32[4,1024]{1,0:T(4,128)}, u32[]{:S(2)}) copy-start(f32[4,1024]{1,0:T(4,128)} %param.13) | copy-start | bytes 49156
  5.8 12.7 %copy-start.6 = (f32[4,1024]{1,0:T(4,128)S(1)}, f32[4,1024]{1,0:T(4,128)}, u32[]{:S(2)}) copy-start(f32[4,1024]{1,0:T(4,128)} %param.16) | copy-start | bytes 49156
  5.8 12.7 %copy-start.7 = (f32[4,1024]{1,0:T(4,128)S(1)}, f32[4,1024]{1,0:T(4,128)}, u32[]{:S(2)}) copy-start(f32[4,1024]{1,0:T(4,128)} %param.15) | copy-start | bytes 49156
  5.8 12.6 %copy-start.8 = (f32[4,1024]{1,0:T(4,128)S(1)}, f32[4,1024]{1,0:T(4,128)}, u32[]{:S(2)}) copy-start(f32[4,1024]{1,0:T(4,128)} %param.14) | copy-start | bytes 49156
  5.8 12.6 %copy-start.9 = (f32[1024]{0:T(1024)S(1)}, f32[1024]{0:T(1024)}, u32[]{:S(2)}) copy-start(f32[1024]{0:T(1024)} %param.17) | copy-start | bytes 12292
  5.9 2.1 %collective-permute-start.1 = (f32[4,32]{1,0:T(4,128)S(1)}, f32[4,32]{1,0:T(4,128)S(1)}, u32[]{:S(2)}, u32[]{:S(2)}) collective-permute-start(f32[4,32]{1,0:T(4,128)S(1)} %partial.1), channel_id=1, source_target_pairs={{0,2},{2,0},{4,6},{6,4},{8,10},{10,8},{12,14},{14,12},{16,18},{18,... | collective-permute-start | bytes 1544 | tf_op jit(solution)/shard_map/ppermute | solution.py:27
  6.0 15.2 %collective-permute-start.8 = (bf16[128,512]{1,0:T(8,128)(2,1)S(1)}, bf16[128,512]{1,0:T(8,128)(2,1)S(1)}, u32[]{:S(2)}, u32[]{:S(2)}) collective-permute-start(bf16[128,512]{1,0:T(8,128)(2,1)S(1)} %far_by_cluster.1.refs_0_), channel_id=1, source_target_pairs={{0,1},{1,0},{2,3},{3,2},{4,5},{5,4},{6,7},{7,6},{8,9},{9,8},{10,11... | collective-permute-start | bytes 393224 | tf_op jit(solution)/shard_map/ppermute | solution.py:27
  8.0 4.9 %collective-permute-start.2 = (f32[4,32]{1,0:T(4,128)S(1)}, f32[4,32]{1,0:T(4,128)S(1)}, u32[]{:S(2)}, u32[]{:S(2)}) collective-permute-start(f32[4,32]{1,0:T(4,128)S(1)} %add.13), channel_id=1, source_target_pairs={{0,6},{2,4},{4,2},{6,0},{8,14},{10,12},{12,10},{14,8},{16,22},{18,... | collective-permute-start | bytes 1544 | tf_op jit(solution)/shard_map/ppermute | solution.py:27
  9.4 5.9 %collective-permute-start.6 = (bf16[8,1024]{1,0:T(8,128)(2,1)S(1)}, bf16[8,1024]{1,0:T(8,128)(2,1)S(1)}, u32[]{:S(2)}, u32[]{:S(2)}) collective-permute-start(bf16[8,1024]{1,0:T(8,128)(2,1)S(1)} %pad_maximum_fusion.own_ref), channel_id=1, source_target_pairs={{0,30},{2,4},{4,2},{6,8},{8,6},{10,12},{12,10},{14,16},{16,14},{18... | collective-permute-start | bytes 49160 | tf_op jit(solution)/shard_map/ppermute | solution.py:27
  13.0 1.2 %collective-permute-start.4 = (bf16[8,1024]{1,0:T(8,128)(2,1)S(1)}, bf16[8,1024]{1,0:T(8,128)(2,1)S(1)}, u32[]{:S(2)}, u32[]{:S(2)}) collective-permute-start(bf16[8,1024]{1,0:T(8,128)(2,1)S(1)} %pad_maximum_fusion.own_ref), channel_id=1, source_target_pairs={{0,2},{2,0},{4,6},{6,4},{8,10},{10,8},{12,14},{14,12},{16,18},{18,... | collective-permute-start | bytes 49160 | tf_op jit(solution)/shard_map/ppermute | solution.py:27
  14.1 3.0 %collective-permute-start.5 = (bf16[4,32]{1,0:T(4,128)(2,1)S(1)}, bf16[4,32]{1,0:T(4,128)(2,1)S(1)}, u32[]{:S(2)}, u32[]{:S(2)}) collective-permute-start(bf16[4,32]{1,0:T(4,128)(2,1)S(1)} %add_convert_fusion), channel_id=1, source_target_pairs={{0,10},{2,8},{4,14},{6,12},{8,2},{10,0},{12,6},{14,4},{16,26},{18,... | collective-permute-start | bytes 776 | tf_op jit(solution)/shard_map/ppermute | solution.py:27
  17.2 3.9 %collective-permute-start.7 = (bf16[4,64]{1,0:T(4,128)(2,1)S(1)}, bf16[4,64]{1,0:T(4,128)(2,1)S(1)}, u32[]{:S(2)}, u32[]{:S(2)}) collective-permute-start(bf16[4,64]{1,0:T(4,128)(2,1)S(1)} %pad_maximum_fusion.1.low_ref), channel_id=1, source_target_pairs={{0,18},{2,16},{4,22},{6,20},{8,26},{10,24},{12,30},{14,28},{16,2},... | collective-permute-start | bytes 1544 | tf_op jit(solution)/shard_map/ppermute | solution.py:27
  17.2 3.9 %collective-permute-start.9 = (f32[4,512]{1,0:T(4,128)S(1)}, f32[4,512]{1,0:T(4,128)S(1)}, u32[]{:S(2)}, u32[]{:S(2)}) collective-permute-start(f32[4,512]{1,0:T(4,128)S(1)} %get-tuple-element.15), channel_id=1, source_target_pairs={{0,1},{1,0},{2,3},{3,2},{4,5},{5,4},{6,7},{7,6},{8,9},{9,8},{10,11... | collective-permute-start | bytes 24584 | tf_op jit(solution)/shard_map/ppermute | solution.py:27

commit v5 on v4

--- a/solution.py
+++ b/solution.py
@@ -71,7 +71,7 @@
             out_ref[j * rank : (j + 1) * rank, r * panel : (r + 1) * panel] = block.astype(bf16)
 
 
-def near_kernel(own_panels, total_panels, column_ref, count_ref, pos_ref, own_ref, near_ref, far_ref, blocks_ref, out_ref, window, picked):
+def near_kernel(own_panels, total_panels, column_ref, count_ref, pos_ref, own_ref, near_ref, far_ref, blocks_ref, out_ref, window):
     rows, slots = column_ref.shape
     members = own_ref.shape[0]
     odd = pos_ref[0] % 2
@@ -81,12 +81,14 @@
     window[3 * own_panels] = jnp.zeros((members, PANEL), f32)
     base = (pos_ref[0] - 1) * own_panels
     for r in range(rows):
+        tiles = []
         for s in range(slots):
             place = lax.rem(column_ref[r, s] - base + total_panels, total_panels)
-            place = jnp.where(s < count_ref[r], place, 3 * own_panels)
-            picked[r, :, s * PANEL : (s + 1) * PANEL] = window[place].astype(bf16)
+            tiles.append(window[jnp.where(s < count_ref[r], place, 3 * own_panels)])
         out_ref[:, r * PANEL : (r + 1) * PANEL] = jnp.dot(
-            picked[r], blocks_ref[r].reshape(slots * PANEL, PANEL), preferred_element_type=f32
+            jnp.concatenate(tiles, axis=1).astype(bf16),
+            blocks_ref[r].reshape(slots * PANEL, PANEL),
+            preferred_element_type=f32,
         )
 
 
@@ -161,7 +163,6 @@
         [IN_SMEM, IN_SMEM, IN_VMEM],
         flops=COST,
     )(in_hbm(far_clusters), (fault_pos // GROUP)[None], in_hbm(far_basis))
-    far_all = gathered(far_by_cluster)
     log_rate_later, far_by_cluster = lax.optimization_barrier((log_rate, far_by_cluster))
     (deficit,) = call(
         deficit_kernel, "deficit", [((local_members, elements), bf16)], [IN_VMEM], flops=COST
@@ -182,7 +183,8 @@
     while bit < GROUP:
         total = total + swapped(total, "fault", lambda i: i ^ bit ^ 1)
         bit *= 2
-    low, near_side = lax.optimization_barrier((total.astype(bf16), near_side))
+    low, near_side, far_by_cluster = lax.optimization_barrier((total.astype(bf16), near_side, far_by_cluster))
+    far_all = gathered(far_by_cluster)
 
     (near_field,) = call(
         functools.partial(near_kernel, own_panels, total_panels),
@@ -191,10 +193,7 @@
         [IN_SMEM] * 3 + [IN_VMEM] * 4,
         mib=8,
         flops=COST,
-        scratch=[
-            pltpu.VMEM((3 * own_panels + 1, members, PANEL), f32),
-            pltpu.VMEM((row_count, members, slots * PANEL), bf16),
-        ],
+        scratch=[pltpu.VMEM((3 * own_panels + 1, members, PANEL), f32)],
     )(near_columns, near_count, fault_pos[None], deficit_all, near_side, far_side, near_blocks)
 
     high = None

time: 22.1 us -> 21.7 us (0.982)
  waiting for transfers between devices: 5.99 us -> 5.28 us
  starting transfers between devices: 11.3 us -> 11.8 us
    ppermute x10, waiting for transfers between devices: 5.99 us -> 5.28 us  [swapped(): lax.ppermute(block, axis, [(i, partner(i) % count) for i in range(count)])]
    ppermute x10, starting transfers between devices: 11.3 us -> 11.8 us  [swapped(): lax.ppermute(block, axis, [(i, partner(i) % count) for i in range(count)])]
  transfers between devices with their start and end apart: 10 -> 10, of which waited for: 5 -> 6; matrix products, arithmetic and copies ran while one was open for 3% -> 3% of each run, Pallas kernels for 10% -> 10%
where the time goes in v5:
time: 21.7 us; the launch traced here: 21.6 us
  starting transfers between devices  11.8 us (54%)
  waiting for transfers between devices  5.28 us (24%)
  Pallas kernels  2.97 us (14%)
  between operations  0.76 us (4%)
  other arithmetic  0.73 us (3%)
    ppermute x10, starting transfers between devices, swapped(): lax.ppermute(block, axis, [(i, partner(i) % count) for i in range(count)])  11.8 us
    ppermute x10, waiting for transfers between devices, swapped(): lax.ppermute(block, axis, [(i, partner(i) % count) for i in range(count)])  5.28 us
    pallas_call x1, Pallas kernels, per_device(): call(functools.partial(near_kernel, own_panels, total_panels), 'near', [(...  1.1 us
    pallas_call x1, Pallas kernels, per_device(): call(far_kernel, 'far_by_cluster', [((cluster_total * rank_size, row_widt...  0.96 us
    pallas_call x1, Pallas kernels, per_device(): call(functools.partial(last_kernel, parts), 'last', [((local_members, ele...  0.77 us
    add x1, other arithmetic, per_device(): state_next = log_state + time_step * state_rate  0.64 us
  transfers between devices with their start and end apart: 10, of which 6 were waited for; matrix products, arithmetic and copies ran while one was open for 3% of the time, Pallas kernels for 10%

profile of v5, /device:TPU:0, one launch (start us, length us, event | category | flops | bytes accessed | tf_op | source)
XLA Modules:
  0.0 21.6 jit_solution(16778871374345630645)
XLA Ops:
  0.6 0.0 copy-start
  0.6 3.0 %collective-permute-start = (bf16[32,512]{1,0:T(8,128)(2,1)}, bf16[32,512]{1,0:T(8,128)(2,1)S(1)}, u32[]{:S(2)}, u32[]{:S(2)}) collective-permute-start(bf16[32,512]{1,0:T(8,128)(2,1)} %refs_0_.1), channel_id=1, source_target_pairs={{0,1},{1,0},{2,3},{3,2},{4,5},{5,4},{6,7},{7,6},{8,9},{9,8},{10,11... | collective-permute-start | bytes 98312 | tf_op jit(solution)/shard_map/ppermute | solution.py:27
  3.7 0.0 copy-start.2
  3.7 1.0 %far_by_cluster.1.refs_0_ = bf16[128,512]{1,0:T(8,128)(2,1)S(1)} custom-call(s32[4,3]{1,0:T(4,128)} %cluster_ref.1, s32[1]{0:T(128)} %bitcast.1.own_cluster_ref, bf16[4,3,32,128]{3,2,1,0:T(8,128)(2,1)} %basis_ref.1), custom_call_target="tpu_custom_call" | custom-call | flops 1000000000 | bytes 1 | tf_op jit(solution)/shard_map/far_by_cluster/pallas_call | solution.py:159
  4.6 0.0 copy-done
  4.7 0.0 copy-start.1
  4.7 0.0 copy-start.3
  4.7 0.0 copy-start.4
  4.7 0.1 collective-permute-start.3
  4.8 1.0 %collective-permute-done.refs_1_ = bf16[32,512]{1,0:T(8,128)(2,1)S(1)} collective-permute-done((bf16[32,512]{1,0:T(8,128)(2,1)}, bf16[32,512]{1,0:T(8,128)(2,1)S(1)}, u32[]{:S(2)}, u32[]{:S(2)}) %collective-permute-start) | collective-permute-done | bytes 32800 | tf_op jit(solution)/shard_map/ppermute | solution.py:27
  5.8 0.0 copy-done.2
  5.8 0.0 copy-start.5
  5.8 0.0 copy-start.6
  5.8 0.0 copy-start.7
  5.8 0.0 copy-start.8
  5.8 0.0 copy-start.9
  5.8 0.1 partial.1
  5.9 0.0 collective-permute-start.1
  6.0 1.2 %collective-permute-done.1 = f32[4,32]{1,0:T(4,128)S(1)} collective-permute-done((f32[4,32]{1,0:T(4,128)S(1)}, f32[4,32]{1,0:T(4,128)S(1)}, u32[]{:S(2)}, u32[]{:S(2)}) %collective-permute-start.1) | collective-permute-done | bytes 544 | tf_op jit(solution)/shard_map/ppermute | solution.py:27
  7.1 1.8 %collective-permute-start.2 = (f32[4,32]{1,0:T(4,128)S(1)}, f32[4,32]{1,0:T(4,128)S(1)}, u32[]{:S(2)}, u32[]{:S(2)}) collective-permute-start(f32[4,32]{1,0:T(4,128)S(1)} %add.13), channel_id=1, source_target_pairs={{0,6},{2,4},{4,2},{6,0},{8,14},{10,12},{12,10},{14,8},{16,22},{18,... | collective-permute-start | bytes 1544 | tf_op jit(solution)/shard_map/ppermute | solution.py:27
  8.9 0.0 collective-permute-done.3
  8.9 3.6 %collective-permute-start.6 = (bf16[8,1024]{1,0:T(8,128)(2,1)S(1)}, bf16[8,1024]{1,0:T(8,128)(2,1)S(1)}, u32[]{:S(2)}, u32[]{:S(2)}) collective-permute-start(bf16[8,1024]{1,0:T(8,128)(2,1)S(1)} %pad_maximum_fusion.own_ref), channel_id=1, source_target_pairs={{0,30},{2,4},{4,2},{6,8},{8,6},{10,12},{12,10},{14,16},{16,14},{18... | collective-permute-start | bytes 49160 | tf_op jit(solution)/shard_map/ppermute | solution.py:27
  12.5 0.0 collective-permute-start.4
  12.5 0.0 collective-permute-done.2
  12.5 1.2 %collective-permute-done.4.near_ref = bf16[8,1024]{1,0:T(8,128)(2,1)S(1)} collective-permute-done((bf16[8,1024]{1,0:T(8,128)(2,1)S(1)}, bf16[8,1024]{1,0:T(8,128)(2,1)S(1)}, u32[]{:S(2)}, u32[]{:S(2)}) %collective-permute-start.4) | collective-permute-done | bytes 16416 | tf_op jit(solution)/shard_map/ppermute | solution.py:27
  13.7 0.0 collective-permute-start.5
  13.7 1.6 %collective-permute-start.8 = (bf16[128,512]{1,0:T(8,128)(2,1)S(1)}, bf16[128,512]{1,0:T(8,128)(2,1)S(1)}, u32[]{:S(2)}, u32[]{:S(2)}) collective-permute-start(bf16[128,512]{1,0:T(8,128)(2,1)S(1)} %far_by_cluster.1.refs_0_), channel_id=1, source_target_pairs={{0,1},{1,0},{2,3},{3,2},{4,5},{5,4},{6,7},{7,6},{8,9},{9,8},{10,11... | collective-permute-start | bytes 393224 | tf_op jit(solution)/shard_map/ppermute | solution.py:27
  15.3 0.0 collective-permute-done.6.far_ref
  15.3 0.0 copy-done.1
  15.3 0.0 copy-done.3
  15.3 0.0 copy-done.4
  15.3 1.1 %near.1 = f32[8,512]{1,0:T(8,128)S(1)} custom-call(s32[4,24]{1,0:T(4,128)S(1)} %copy-done.3, s32[4]{0:T(128)S(1)} %copy-done.4, s32[1]{0:T(128)} %bitcast.2.pos_ref, bf16[8,1024]{1,0:T(8,128)(2,1)S(1)} %pad_maximum_fusion.own_ref, bf16[8,1024]{1,0:T(8,128)(2,1)S(1)} %collective-permute-done.4.near_ref, bf16[8,1024]{1,0:T(8,128)(2,1)S(1)} %collective-permute-done.6.far_ref, ...), custom_call_target="tpu_custom_call" | custom-call | flops 1000000000 | bytes 1 | tf_op jit(solution)/shard_map/near/pallas_call | solution.py:189
  16.4 0.3 %collective-permute-done.5 = bf16[4,32]{1,0:T(4,128)(2,1)S(1)} collective-permute-done((bf16[4,32]{1,0:T(4,128)(2,1)S(1)}, bf16[4,32]{1,0:T(4,128)(2,1)S(1)}, u32[]{:S(2)}, u32[]{:S(2)}) %collective-permute-start.5) | collective-permute-done | bytes 288 | tf_op jit(solution)/shard_map/ppermute | solution.py:27
  16.7 0.1 pad_maximum_fusion.1.low_ref
  16.7 0.4 %collective-permute-start.7 = (bf16[4,64]{1,0:T(4,128)(2,1)S(1)}, bf16[4,64]{1,0:T(4,128)(2,1)S(1)}, u32[]{:S(2)}, u32[]{:S(2)}) collective-permute-start(bf16[4,64]{1,0:T(4,128)(2,1)S(1)} %pad_maximum_fusion.1.low_ref), channel_id=1, source_target_pairs={{0,18},{2,16},{4,22},{6,20},{8,26},{10,24},{12,30},{14,28},{16,2},... | collective-permute-start | bytes 1544 | tf_op jit(solution)/shard_map/ppermute | solution.py:27
  17.1 1.3 %collective-permute-start.9 = (f32[4,512]{1,0:T(4,128)S(1)}, f32[4,512]{1,0:T(4,128)S(1)}, u32[]{:S(2)}, u32[]{:S(2)}) collective-permute-start(f32[4,512]{1,0:T(4,128)S(1)} %get-tuple-element.19), channel_id=1, source_target_pairs={{0,1},{1,0},{2,3},{3,2},{4,5},{5,4},{6,7},{7,6},{8,9},{9,8},{10,11... | collective-permute-start | bytes 24584 | tf_op jit(solution)/shard_map/ppermute | solution.py:27
  18.4 0.0 copy-done.5
  18.4 0.0 copy-done.6
  18.4 0.0 copy-done.7
  18.4 0.0 copy-done.8
  18.4 0.0 copy-done.9
  18.5 0.6 %multiply_add_fusion = (f32[4,1024]{1,0:T(4,128)}, f32[4,1024]{1,0:T(4,128)S(1)}, f32[4,1024]{1,0:T(4,128)S(1)}) fusion(f32[4,1024]{1,0:T(4,128)S(1)} %copy-done.5, f32[4,1024]{1,0:T(4,128)S(1)} %copy-done.6, f32[4,1024]{1,0:T(4,128)S(1)} %copy-done, f32[4,1024]{1,0:T(4,128)S(1)} %copy-done.7, f32[4,1024]{1,0:T(4,128)S(1)} %copy-done.8, f32[1024]{0:T(1024)S(1)} %copy-done.9), kind=kLoop, calls=%fused_computation.1 | loop fusion | flops 53248 | bytes 135168 | tf_op jit(solution)/shard_map/add | solution.py:220
  19.1 1.6 %collective-permute-done.7.high_ref = bf16[4,64]{1,0:T(4,128)(2,1)S(1)} collective-permute-done((bf16[4,64]{1,0:T(4,128)(2,1)S(1)}, bf16[4,64]{1,0:T(4,128)(2,1)S(1)}, u32[]{:S(2)}, u32[]{:S(2)}) %collective-permute-start.7) | collective-permute-done | bytes 544 | tf_op jit(solution)/shard_map/ppermute | solution.py:27
  20.6 0.1 collective-permute-done.9.refs_3_
  20.8 0.0 collective-permute-done.8.refs_1_
  20.8 0.8 %last.1 = f32[4,1024]{1,0:T(4,128)} custom-call(s32[1]{0:T(128)} %bitcast.pos_ref, bf16[4,64]{1,0:T(4,128)(2,1)S(1)} %pad_maximum_fusion.1.low_ref, bf16[4,64]{1,0:T(4,128)(2,1)S(1)} %collective-permute-done.7.high_ref, bf16[128,512]{1,0:T(8,128)(2,1)S(1)} %far_by_cluster.1.refs_0_, bf16[128,512]{1,0:T(8,128)(2,1)S(1)} %collective-permute-done.8.refs_1_, ...), custom_call_target="tpu_custom_call" | custom-call | flops 1000000000 | bytes 1 | tf_op jit(solution)/shard_map/last/pallas_call | solution.py:221
  (5 shorter events, 0.0 us)
Async XLA Ops:
  0.6 4.0 %copy-start = (f32[4,1024]{1,0:T(4,128)S(1)}, f32[4,1024]{1,0:T(4,128)}, u32[]{:S(2)}) copy-start(f32[4,1024]{1,0:T(4,128)} %rate_ref) | copy-start | bytes 49156
  0.6 5.1 %collective-permute-start = (bf16[32,512]{1,0:T(8,128)(2,1)}, bf16[32,512]{1,0:T(8,128)(2,1)S(1)}, u32[]{:S(2)}, u32[]{:S(2)}) collective-permute-start(bf16[32,512]{1,0:T(8,128)(2,1)} %refs_0_.1), channel_id=1, source_target_pairs={{0,1},{1,0},{2,3},{3,2},{4,5},{5,4},{6,7},{7,6},{8,9},{9,8},{10,11... | collective-permute-start | bytes 98312 | tf_op jit(solution)/shard_map/ppermute | solution.py:27
  3.7 2.1 %copy-start.2 = (bf16[32,512]{1,0:T(8,128)(2,1)S(1)}, bf16[32,512]{1,0:T(8,128)(2,1)}, u32[]{:S(2)}) copy-start(bf16[32,512]{1,0:T(8,128)(2,1)} %refs_0_.1) | copy-start | bytes 98308
  4.7 10.6 %copy-start.1 = (bf16[4,24,128,128]{3,2,1,0:T(8,128)(2,1)S(1)}, bf16[4,24,128,128]{3,2,1,0:T(8,128)(2,1)}, u32[]{:S(2)}) copy-start(bf16[4,24,128,128]{3,2,1,0:T(8,128)(2,1)} %blocks_ref.1) | copy-start | bytes 9437188
  4.7 10.6 %copy-start.3 = (s32[4,24]{1,0:T(4,128)S(1)}, s32[4,24]{1,0:T(4,128)}, u32[]{:S(2)}) copy-start(s32[4,24]{1,0:T(4,128)} %column_ref.1) | copy-start | bytes 1156
  4.7 10.6 %copy-start.4 = (s32[4]{0:T(128)S(1)}, s32[4]{0:T(128)}, u32[]{:S(2)}) copy-start(s32[4]{0:T(128)} %count_ref.1) | copy-start | bytes 52
  4.7 4.2 %collective-permute-start.3 = (bf16[4,1024]{1,0:T(4,128)(2,1)S(1)}, bf16[4,1024]{1,0:T(4,128)(2,1)S(1)}, u32[]{:S(2)}, u32[]{:S(2)}) collective-permute-start(bf16[4,1024]{1,0:T(4,128)(2,1)S(1)} %deficit.1.deficit_ref), channel_id=1, source_target_pairs={{0,1},{1,0},{2,3},{3,2},{4,5},{5,4},{6,7},{7,6},{8,9},{9,8},{10,11... | collective-permute-start | bytes 24584 | tf_op jit(solution)/shard_map/ppermute | solution.py:27
  5.8 12.6 %copy-start.5 = (f32[4,1024]{1,0:T(4,128)S(1)}, f32[4,1024]{1,0:T(4,128)}, u32[]{:S(2)}) copy-start(f32[4,1024]{1,0:T(4,128)} %param.13) | copy-start | bytes 49156
  5.8 12.7 %copy-start.6 = (f32[4,1024]{1,0:T(4,128)S(1)}, f32[4,1024]{1,0:T(4,128)}, u32[]{:S(2)}) copy-start(f32[4,1024]{1,0:T(4,128)} %param.16) | copy-start | bytes 49156
  5.8 12.7 %copy-start.7 = (f32[4,1024]{1,0:T(4,128)S(1)}, f32[4,1024]{1,0:T(4,128)}, u32[]{:S(2)}) copy-start(f32[4,1024]{1,0:T(4,128)} %param.15) | copy-start | bytes 49156
  5.8 12.6 %copy-start.8 = (f32[4,1024]{1,0:T(4,128)S(1)}, f32[4,1024]{1,0:T(4,128)}, u32[]{:S(2)}) copy-start(f32[4,1024]{1,0:T(4,128)} %param.14) | copy-start | bytes 49156
  5.8 12.6 %copy-start.9 = (f32[1024]{0:T(1024)S(1)}, f32[1024]{0:T(1024)}, u32[]{:S(2)}) copy-start(f32[1024]{0:T(1024)} %param.17) | copy-start | bytes 12292
  5.9 1.2 %collective-permute-start.1 = (f32[4,32]{1,0:T(4,128)S(1)}, f32[4,32]{1,0:T(4,128)S(1)}, u32[]{:S(2)}, u32[]{:S(2)}) collective-permute-start(f32[4,32]{1,0:T(4,128)S(1)} %partial.1), channel_id=1, source_target_pairs={{0,2},{2,0},{4,6},{6,4},{8,10},{10,8},{12,14},{14,12},{16,18},{18,... | collective-permute-start | bytes 1544 | tf_op jit(solution)/shard_map/ppermute | solution.py:27
  7.1 5.4 %collective-permute-start.2 = (f32[4,32]{1,0:T(4,128)S(1)}, f32[4,32]{1,0:T(4,128)S(1)}, u32[]{:S(2)}, u32[]{:S(2)}) collective-permute-start(f32[4,32]{1,0:T(4,128)S(1)} %add.13), channel_id=1, source_target_pairs={{0,6},{2,4},{4,2},{6,0},{8,14},{10,12},{12,10},{14,8},{16,22},{18,... | collective-permute-start | bytes 1544 | tf_op jit(solution)/shard_map/ppermute | solution.py:27
  8.9 6.4 %collective-permute-start.6 = (bf16[8,1024]{1,0:T(8,128)(2,1)S(1)}, bf16[8,1024]{1,0:T(8,128)(2,1)S(1)}, u32[]{:S(2)}, u32[]{:S(2)}) collective-permute-start(bf16[8,1024]{1,0:T(8,128)(2,1)S(1)} %pad_maximum_fusion.own_ref), channel_id=1, source_target_pairs={{0,30},{2,4},{4,2},{6,8},{8,6},{10,12},{12,10},{14,16},{16,14},{18... | collective-permute-start | bytes 49160 | tf_op jit(solution)/shard_map/ppermute | solution.py:27
  12.5 1.2 %collective-permute-start.4 = (bf16[8,1024]{1,0:T(8,128)(2,1)S(1)}, bf16[8,1024]{1,0:T(8,128)(2,1)S(1)}, u32[]{:S(2)}, u32[]{:S(2)}) collective-permute-start(bf16[8,1024]{1,0:T(8,128)(2,1)S(1)} %pad_maximum_fusion.own_ref), channel_id=1, source_target_pairs={{0,2},{2,0},{4,6},{6,4},{8,10},{10,8},{12,14},{14,12},{16,18},{18,... | collective-permute-start | bytes 49160 | tf_op jit(solution)/shard_map/ppermute | solution.py:27
  13.7 3.0 %collective-permute-start.5 = (bf16[4,32]{1,0:T(4,128)(2,1)S(1)}, bf16[4,32]{1,0:T(4,128)(2,1)S(1)}, u32[]{:S(2)}, u32[]{:S(2)}) collective-permute-start(bf16[4,32]{1,0:T(4,128)(2,1)S(1)} %add_convert_fusion), channel_id=1, source_target_pairs={{0,10},{2,8},{4,14},{6,12},{8,2},{10,0},{12,6},{14,4},{16,26},{18,... | collective-permute-start | bytes 776 | tf_op jit(solution)/shard_map/ppermute | solution.py:27
  13.7 7.1 %collective-permute-start.8 = (bf16[128,512]{1,0:T(8,128)(2,1)S(1)}, bf16[128,512]{1,0:T(8,128)(2,1)S(1)}, u32[]{:S(2)}, u32[]{:S(2)}) collective-permute-start(bf16[128,512]{1,0:T(8,128)(2,1)S(1)} %far_by_cluster.1.refs_0_), channel_id=1, source_target_pairs={{0,1},{1,0},{2,3},{3,2},{4,5},{5,4},{6,7},{7,6},{8,9},{9,8},{10,11... | collective-permute-start | bytes 393224 | tf_op jit(solution)/shard_map/ppermute | solution.py:27
  16.7 3.9 %collective-permute-start.7 = (bf16[4,64]{1,0:T(4,128)(2,1)S(1)}, bf16[4,64]{1,0:T(4,128)(2,1)S(1)}, u32[]{:S(2)}, u32[]{:S(2)}) collective-permute-start(bf16[4,64]{1,0:T(4,128)(2,1)S(1)} %pad_maximum_fusion.1.low_ref), channel_id=1, source_target_pairs={{0,18},{2,16},{4,22},{6,20},{8,26},{10,24},{12,30},{14,28},{16,2},... | collective-permute-start | bytes 1544 | tf_op jit(solution)/shard_map/ppermute | solution.py:27
  17.1 3.7 %collective-permute-start.9 = (f32[4,512]{1,0:T(4,128)S(1)}, f32[4,512]{1,0:T(4,128)S(1)}, u32[]{:S(2)}, u32[]{:S(2)}) collective-permute-start(f32[4,512]{1,0:T(4,128)S(1)} %get-tuple-element.19), channel_id=1, source_target_pairs={{0,1},{1,0},{2,3},{3,2},{4,5},{5,4},{6,7},{7,6},{8,9},{9,8},{10,11... | collective-permute-start | bytes 24584 | tf_op jit(solution)/shard_map/ppermute | solution.py:27

commit v6 on v5

--- a/solution.py
+++ b/solution.py
@@ -163,6 +163,7 @@
         [IN_SMEM, IN_SMEM, IN_VMEM],
         flops=COST,
     )(in_hbm(far_clusters), (fault_pos // GROUP)[None], in_hbm(far_basis))
+    far_all = gathered(far_by_cluster)
     log_rate_later, far_by_cluster = lax.optimization_barrier((log_rate, far_by_cluster))
     (deficit,) = call(
         deficit_kernel, "deficit", [((local_members, elements), bf16)], [IN_VMEM], flops=COST
@@ -183,8 +184,7 @@
     while bit < GROUP:
         total = total + swapped(total, "fault", lambda i: i ^ bit ^ 1)
         bit *= 2
-    low, near_side, far_by_cluster = lax.optimization_barrier((total.astype(bf16), near_side, far_by_cluster))
-    far_all = gathered(far_by_cluster)
+    low = total.astype(bf16)
 
     (near_field,) = call(
         functools.partial(near_kernel, own_panels, total_panels),

time: 21.7 us -> 21.5 us (level)
  transfers between devices with their start and end apart: 10 -> 10, of which waited for: 6 -> 4; matrix products, arithmetic and copies ran while one was open for 3% -> 3% of each run, Pallas kernels for 10% -> 10%
where the time goes in v6:
time: 21.5 us; the launch traced here: 21.3 us
  starting transfers between devices  11.6 us (54%)
  waiting for transfers between devices  5.16 us (24%)
  Pallas kernels  2.97 us (14%)
  between operations  0.77 us (4%)
  other arithmetic  0.73 us (3%)
    ppermute x10, starting transfers between devices, swapped(): lax.ppermute(block, axis, [(i, partner(i) % count) for i in range(count)])  11.6 us
    ppermute x10, waiting for transfers between devices, swapped(): lax.ppermute(block, axis, [(i, partner(i) % count) for i in range(count)])  5.16 us
    pallas_call x1, Pallas kernels, per_device(): call(functools.partial(near_kernel, own_panels, total_panels), 'near', [(...  1.1 us
    pallas_call x1, Pallas kernels, per_device(): call(far_kernel, 'far_by_cluster', [((cluster_total * rank_size, row_widt...  0.96 us
    pallas_call x1, Pallas kernels, per_device(): call(functools.partial(last_kernel, parts), 'last', [((local_members, ele...  0.77 us
    add x1, other arithmetic, per_device(): state_next = log_state + time_step * state_rate  0.64 us
  transfers between devices with their start and end apart: 10, of which 4 were waited for; matrix products, arithmetic and copies ran while one was open for 3% of the time, Pallas kernels for 10%

profile of v6, /device:TPU:0, one launch (start us, length us, event | category | flops | bytes accessed | tf_op | source)
XLA Modules:
  0.0 21.3 jit_solution(2803997616430763399)
XLA Ops:
  0.6 0.0 copy-start
  0.6 3.0 %collective-permute-start = (bf16[32,512]{1,0:T(8,128)(2,1)}, bf16[32,512]{1,0:T(8,128)(2,1)S(1)}, u32[]{:S(2)}, u32[]{:S(2)}) collective-permute-start(bf16[32,512]{1,0:T(8,128)(2,1)} %refs_0_.1), channel_id=1, source_target_pairs={{0,1},{1,0},{2,3},{3,2},{4,5},{5,4},{6,7},{7,6},{8,9},{9,8},{10,11... | collective-permute-start | bytes 98312 | tf_op jit(solution)/shard_map/ppermute | solution.py:27
  3.7 0.0 copy-start.2
  3.7 1.0 %far_by_cluster.1.refs_0_ = bf16[128,512]{1,0:T(8,128)(2,1)S(1)} custom-call(s32[4,3]{1,0:T(4,128)} %cluster_ref.1, s32[1]{0:T(128)} %bitcast.1.own_cluster_ref, bf16[4,3,32,128]{3,2,1,0:T(8,128)(2,1)} %basis_ref.1), custom_call_target="tpu_custom_call" | custom-call | flops 1000000000 | bytes 1 | tf_op jit(solution)/shard_map/far_by_cluster/pallas_call | solution.py:159
  4.6 0.0 copy-done
  4.7 0.0 copy-start.1
  4.7 0.0 copy-start.3
  4.7 0.0 copy-start.4
  4.7 0.1 collective-permute-start.4
  4.8 1.0 %collective-permute-done.refs_1_ = bf16[32,512]{1,0:T(8,128)(2,1)S(1)} collective-permute-done((bf16[32,512]{1,0:T(8,128)(2,1)}, bf16[32,512]{1,0:T(8,128)(2,1)S(1)}, u32[]{:S(2)}, u32[]{:S(2)}) %collective-permute-start) | collective-permute-done | bytes 32800 | tf_op jit(solution)/shard_map/ppermute | solution.py:27
  5.8 0.0 copy-done.2
  5.8 0.0 copy-start.5
  5.8 0.0 copy-start.6
  5.8 0.0 copy-start.7
  5.8 0.0 copy-start.8
  5.8 0.0 copy-start.9
  5.8 0.1 partial.1
  5.9 0.0 collective-permute-start.1
  6.0 2.1 %collective-permute-start.8 = (bf16[128,512]{1,0:T(8,128)(2,1)S(1)}, bf16[128,512]{1,0:T(8,128)(2,1)S(1)}, u32[]{:S(2)}, u32[]{:S(2)}) collective-permute-start(bf16[128,512]{1,0:T(8,128)(2,1)S(1)} %far_by_cluster.1.refs_0_), channel_id=1, source_target_pairs={{0,1},{1,0},{2,3},{3,2},{4,5},{5,4},{6,7},{7,6},{8,9},{9,8},{10,11... | collective-permute-start | bytes 393224 | tf_op jit(solution)/shard_map/ppermute | solution.py:27
  8.0 0.0 collective-permute-done.1
  8.0 1.4 %collective-permute-start.2 = (f32[4,32]{1,0:T(4,128)S(1)}, f32[4,32]{1,0:T(4,128)S(1)}, u32[]{:S(2)}, u32[]{:S(2)}) collective-permute-start(f32[4,32]{1,0:T(4,128)S(1)} %add.13), channel_id=1, source_target_pairs={{0,6},{2,4},{4,2},{6,0},{8,14},{10,12},{12,10},{14,8},{16,22},{18,... | collective-permute-start | bytes 1544 | tf_op jit(solution)/shard_map/ppermute | solution.py:27
  9.4 0.0 collective-permute-done.4
  9.4 3.6 %collective-permute-start.6 = (bf16[8,1024]{1,0:T(8,128)(2,1)S(1)}, bf16[8,1024]{1,0:T(8,128)(2,1)S(1)}, u32[]{:S(2)}, u32[]{:S(2)}) collective-permute-start(bf16[8,1024]{1,0:T(8,128)(2,1)S(1)} %pad_maximum_fusion.own_ref), channel_id=1, source_target_pairs={{0,30},{2,4},{4,2},{6,8},{8,6},{10,12},{12,10},{14,16},{16,14},{18... | collective-permute-start | bytes 49160 | tf_op jit(solution)/shard_map/ppermute | solution.py:27
  13.0 0.0 collective-permute-start.5
  13.0 0.0 collective-permute-done.2
  13.0 0.1 collective-permute-start.3
  13.1 2.3 %collective-permute-done.6.far_ref = bf16[8,1024]{1,0:T(8,128)(2,1)S(1)} collective-permute-done((bf16[8,1024]{1,0:T(8,128)(2,1)S(1)}, bf16[8,1024]{1,0:T(8,128)(2,1)S(1)}, u32[]{:S(2)}, u32[]{:S(2)}) %collective-permute-start.6) | collective-permute-done | bytes 16416 | tf_op jit(solution)/shard_map/ppermute | solution.py:27
  15.3 0.0 collective-permute-done.5.near_ref
  15.3 0.0 copy-done.1
  15.3 0.0 copy-done.3
  15.3 0.0 copy-done.4
  15.3 1.1 %near.1 = f32[8,512]{1,0:T(8,128)S(1)} custom-call(s32[4,24]{1,0:T(4,128)S(1)} %copy-done.3, s32[4]{0:T(128)S(1)} %copy-done.4, s32[1]{0:T(128)} %bitcast.2.pos_ref, bf16[8,1024]{1,0:T(8,128)(2,1)S(1)} %pad_maximum_fusion.own_ref, bf16[8,1024]{1,0:T(8,128)(2,1)S(1)} %collective-permute-done.5.near_ref, bf16[8,1024]{1,0:T(8,128)(2,1)S(1)} %collective-permute-done.6.far_ref, ...), custom_call_target="tpu_custom_call" | custom-call | flops 1000000000 | bytes 1 | tf_op jit(solution)/shard_map/near/pallas_call | solution.py:189
  16.5 0.0 collective-permute-done.3
  16.5 0.1 pad_maximum_fusion.1.low_ref
  16.6 0.3 %collective-permute-start.7 = (bf16[4,64]{1,0:T(4,128)(2,1)S(1)}, bf16[4,64]{1,0:T(4,128)(2,1)S(1)}, u32[]{:S(2)}, u32[]{:S(2)}) collective-permute-start(bf16[4,64]{1,0:T(4,128)(2,1)S(1)} %pad_maximum_fusion.1.low_ref), channel_id=1, source_target_pairs={{0,18},{2,16},{4,22},{6,20},{8,26},{10,24},{12,30},{14,28},{16,2},... | collective-permute-start | bytes 1544 | tf_op jit(solution)/shard_map/ppermute | solution.py:27
  16.9 1.1 %collective-permute-start.9 = (f32[4,512]{1,0:T(4,128)S(1)}, f32[4,512]{1,0:T(4,128)S(1)}, u32[]{:S(2)}, u32[]{:S(2)}) collective-permute-start(f32[4,512]{1,0:T(4,128)S(1)} %get-tuple-element.11), channel_id=1, source_target_pairs={{0,1},{1,0},{2,3},{3,2},{4,5},{5,4},{6,7},{7,6},{8,9},{9,8},{10,11... | collective-permute-start | bytes 24584 | tf_op jit(solution)/shard_map/ppermute | solution.py:27
  18.0 0.0 copy-done.5
  18.0 0.0 copy-done.6
  18.0 0.0 copy-done.7
  18.0 0.0 copy-done.8
  18.0 0.0 copy-done.9
  18.0 0.6 %multiply_add_fusion = (f32[4,1024]{1,0:T(4,128)}, f32[4,1024]{1,0:T(4,128)S(1)}, f32[4,1024]{1,0:T(4,128)S(1)}) fusion(f32[4,1024]{1,0:T(4,128)S(1)} %copy-done.5, f32[4,1024]{1,0:T(4,128)S(1)} %copy-done.6, f32[4,1024]{1,0:T(4,128)S(1)} %copy-done, f32[4,1024]{1,0:T(4,128)S(1)} %copy-done.7, f32[4,1024]{1,0:T(4,128)S(1)} %copy-done.8, f32[1024]{0:T(1024)S(1)} %copy-done.9), kind=kLoop, calls=%fused_computation.1 | loop fusion | flops 53248 | bytes 135168 | tf_op jit(solution)/shard_map/add | solution.py:220
  18.6 1.8 %collective-permute-done.7.high_ref = bf16[4,64]{1,0:T(4,128)(2,1)S(1)} collective-permute-done((bf16[4,64]{1,0:T(4,128)(2,1)S(1)}, bf16[4,64]{1,0:T(4,128)(2,1)S(1)}, u32[]{:S(2)}, u32[]{:S(2)}) %collective-permute-start.7) | collective-permute-done | bytes 544 | tf_op jit(solution)/shard_map/ppermute | solution.py:27
  20.5 0.1 collective-permute-done.9.refs_3_
  20.5 0.0 collective-permute-done.8.refs_1_
  20.5 0.8 %last.1 = f32[4,1024]{1,0:T(4,128)} custom-call(s32[1]{0:T(128)} %bitcast.pos_ref, bf16[4,64]{1,0:T(4,128)(2,1)S(1)} %pad_maximum_fusion.1.low_ref, bf16[4,64]{1,0:T(4,128)(2,1)S(1)} %collective-permute-done.7.high_ref, bf16[128,512]{1,0:T(8,128)(2,1)S(1)} %far_by_cluster.1.refs_0_, bf16[128,512]{1,0:T(8,128)(2,1)S(1)} %collective-permute-done.8.refs_1_, ...), custom_call_target="tpu_custom_call" | custom-call | flops 1000000000 | bytes 1 | tf_op jit(solution)/shard_map/last/pallas_call | solution.py:221
  (5 shorter events, 0.0 us)
Async XLA Ops:
  0.6 4.0 %copy-start = (f32[4,1024]{1,0:T(4,128)S(1)}, f32[4,1024]{1,0:T(4,128)}, u32[]{:S(2)}) copy-start(f32[4,1024]{1,0:T(4,128)} %rate_ref) | copy-start | bytes 49156
  0.6 5.1 %collective-permute-start = (bf16[32,512]{1,0:T(8,128)(2,1)}, bf16[32,512]{1,0:T(8,128)(2,1)S(1)}, u32[]{:S(2)}, u32[]{:S(2)}) collective-permute-start(bf16[32,512]{1,0:T(8,128)(2,1)} %refs_0_.1), channel_id=1, source_target_pairs={{0,1},{1,0},{2,3},{3,2},{4,5},{5,4},{6,7},{7,6},{8,9},{9,8},{10,11... | collective-permute-start | bytes 98312 | tf_op jit(solution)/shard_map/ppermute | solution.py:27
  3.7 2.1 %copy-start.2 = (bf16[32,512]{1,0:T(8,128)(2,1)S(1)}, bf16[32,512]{1,0:T(8,128)(2,1)}, u32[]{:S(2)}) copy-start(bf16[32,512]{1,0:T(8,128)(2,1)} %refs_0_.1) | copy-start | bytes 98308
  4.7 10.7 %copy-start.1 = (bf16[4,24,128,128]{3,2,1,0:T(8,128)(2,1)S(1)}, bf16[4,24,128,128]{3,2,1,0:T(8,128)(2,1)}, u32[]{:S(2)}) copy-start(bf16[4,24,128,128]{3,2,1,0:T(8,128)(2,1)} %blocks_ref.1) | copy-start | bytes 9437188
  4.7 10.7 %copy-start.3 = (s32[4,24]{1,0:T(4,128)S(1)}, s32[4,24]{1,0:T(4,128)}, u32[]{:S(2)}) copy-start(s32[4,24]{1,0:T(4,128)} %column_ref.1) | copy-start | bytes 1156
  4.7 10.7 %copy-start.4 = (s32[4]{0:T(128)S(1)}, s32[4]{0:T(128)}, u32[]{:S(2)}) copy-start(s32[4]{0:T(128)} %count_ref.1) | copy-start | bytes 52
  4.7 4.7 %collective-permute-start.4 = (bf16[4,1024]{1,0:T(4,128)(2,1)S(1)}, bf16[4,1024]{1,0:T(4,128)(2,1)S(1)}, u32[]{:S(2)}, u32[]{:S(2)}) collective-permute-start(bf16[4,1024]{1,0:T(4,128)(2,1)S(1)} %deficit.1.deficit_ref), channel_id=1, source_target_pairs={{0,1},{1,0},{2,3},{3,2},{4,5},{5,4},{6,7},{7,6},{8,9},{9,8},{10,11... | collective-permute-start | bytes 24584 | tf_op jit(solution)/shard_map/ppermute | solution.py:27
  5.8 12.2 %copy-start.5 = (f32[4,1024]{1,0:T(4,128)S(1)}, f32[4,1024]{1,0:T(4,128)}, u32[]{:S(2)}) copy-start(f32[4,1024]{1,0:T(4,128)} %param.13) | copy-start | bytes 49156
  5.8 12.2 %copy-start.6 = (f32[4,1024]{1,0:T(4,128)S(1)}, f32[4,1024]{1,0:T(4,128)}, u32[]{:S(2)}) copy-start(f32[4,1024]{1,0:T(4,128)} %param.16) | copy-start | bytes 49156
  5.8 12.2 %copy-start.7 = (f32[4,1024]{1,0:T(4,128)S(1)}, f32[4,1024]{1,0:T(4,128)}, u32[]{:S(2)}) copy-start(f32[4,1024]{1,0:T(4,128)} %param.15) | copy-start | bytes 49156
  5.8 12.2 %copy-start.8 = (f32[4,1024]{1,0:T(4,128)S(1)}, f32[4,1024]{1,0:T(4,128)}, u32[]{:S(2)}) copy-start(f32[4,1024]{1,0:T(4,128)} %param.14) | copy-start | bytes 49156
  5.8 12.2 %copy-start.9 = (f32[1024]{0:T(1024)S(1)}, f32[1024]{0:T(1024)}, u32[]{:S(2)}) copy-start(f32[1024]{0:T(1024)} %param.17) | copy-start | bytes 12292
  5.9 2.1 %collective-permute-start.1 = (f32[4,32]{1,0:T(4,128)S(1)}, f32[4,32]{1,0:T(4,128)S(1)}, u32[]{:S(2)}, u32[]{:S(2)}) collective-permute-start(f32[4,32]{1,0:T(4,128)S(1)} %partial.1), channel_id=1, source_target_pairs={{0,2},{2,0},{4,6},{6,4},{8,10},{10,8},{12,14},{14,12},{16,18},{18,... | collective-permute-start | bytes 1544 | tf_op jit(solution)/shard_map/ppermute | solution.py:27
  6.0 14.6 %collective-permute-start.8 = (bf16[128,512]{1,0:T(8,128)(2,1)S(1)}, bf16[128,512]{1,0:T(8,128)(2,1)S(1)}, u32[]{:S(2)}, u32[]{:S(2)}) collective-permute-start(bf16[128,512]{1,0:T(8,128)(2,1)S(1)} %far_by_cluster.1.refs_0_), channel_id=1, source_target_pairs={{0,1},{1,0},{2,3},{3,2},{4,5},{5,4},{6,7},{7,6},{8,9},{9,8},{10,11... | collective-permute-start | bytes 393224 | tf_op jit(solution)/shard_map/ppermute | solution.py:27
  8.0 4.9 %collective-permute-start.2 = (f32[4,32]{1,0:T(4,128)S(1)}, f32[4,32]{1,0:T(4,128)S(1)}, u32[]{:S(2)}, u32[]{:S(2)}) collective-permute-start(f32[4,32]{1,0:T(4,128)S(1)} %add.13), channel_id=1, source_target_pairs={{0,6},{2,4},{4,2},{6,0},{8,14},{10,12},{12,10},{14,8},{16,22},{18,... | collective-permute-start | bytes 1544 | tf_op jit(solution)/shard_map/ppermute | solution.py:27
  9.4 5.9 %collective-permute-start.6 = (bf16[8,1024]{1,0:T(8,128)(2,1)S(1)}, bf16[8,1024]{1,0:T(8,128)(2,1)S(1)}, u32[]{:S(2)}, u32[]{:S(2)}) collective-permute-start(bf16[8,1024]{1,0:T(8,128)(2,1)S(1)} %pad_maximum_fusion.own_ref), channel_id=1, source_target_pairs={{0,30},{2,4},{4,2},{6,8},{8,6},{10,12},{12,10},{14,16},{16,14},{18... | collective-permute-start | bytes 49160 | tf_op jit(solution)/shard_map/ppermute | solution.py:27
  13.0 2.4 %collective-permute-start.5 = (bf16[8,1024]{1,0:T(8,128)(2,1)S(1)}, bf16[8,1024]{1,0:T(8,128)(2,1)S(1)}, u32[]{:S(2)}, u32[]{:S(2)}) collective-permute-start(bf16[8,1024]{1,0:T(8,128)(2,1)S(1)} %pad_maximum_fusion.own_ref), channel_id=1, source_target_pairs={{0,2},{2,0},{4,6},{6,4},{8,10},{10,8},{12,14},{14,12},{16,18},{18,... | collective-permute-start | bytes 49160 | tf_op jit(solution)/shard_map/ppermute | solution.py:27
  13.0 3.5 %collective-permute-start.3 = (bf16[4,32]{1,0:T(4,128)(2,1)S(1)}, bf16[4,32]{1,0:T(4,128)(2,1)S(1)}, u32[]{:S(2)}, u32[]{:S(2)}) collective-permute-start(bf16[4,32]{1,0:T(4,128)(2,1)S(1)} %add_convert_fusion), channel_id=1, source_target_pairs={{0,10},{2,8},{4,14},{6,12},{8,2},{10,0},{12,6},{14,4},{16,26},{18,... | collective-permute-start | bytes 776 | tf_op jit(solution)/shard_map/ppermute | solution.py:27
  16.6 3.9 %collective-permute-start.7 = (bf16[4,64]{1,0:T(4,128)(2,1)S(1)}, bf16[4,64]{1,0:T(4,128)(2,1)S(1)}, u32[]{:S(2)}, u32[]{:S(2)}) collective-permute-start(bf16[4,64]{1,0:T(4,128)(2,1)S(1)} %pad_maximum_fusion.1.low_ref), channel_id=1, source_target_pairs={{0,18},{2,16},{4,22},{6,20},{8,26},{10,24},{12,30},{14,28},{16,2},... | collective-permute-start | bytes 1544 | tf_op jit(solution)/shard_map/ppermute | solution.py:27
  16.9 3.7 %collective-permute-start.9 = (f32[4,512]{1,0:T(4,128)S(1)}, f32[4,512]{1,0:T(4,128)S(1)}, u32[]{:S(2)}, u32[]{:S(2)}) collective-permute-start(f32[4,512]{1,0:T(4,128)S(1)} %get-tuple-element.11), channel_id=1, source_target_pairs={{0,1},{1,0},{2,3},{3,2},{4,5},{5,4},{6,7},{7,6},{8,9},{9,8},{10,11... | collective-permute-start | bytes 24584 | tf_op jit(solution)/shard_map/ppermute | solution.py:27

commit v7 on v6

--- a/solution.py
+++ b/solution.py
@@ -81,15 +81,19 @@
     window[3 * own_panels] = jnp.zeros((members, PANEL), f32)
     base = (pos_ref[0] - 1) * own_panels
     for r in range(rows):
-        tiles = []
-        for s in range(slots):
-            place = lax.rem(column_ref[r, s] - base + total_panels, total_panels)
-            tiles.append(window[jnp.where(s < count_ref[r], place, 3 * own_panels)])
-        out_ref[:, r * PANEL : (r + 1) * PANEL] = jnp.dot(
-            jnp.concatenate(tiles, axis=1).astype(bf16),
-            blocks_ref[r].reshape(slots * PANEL, PANEL),
-            preferred_element_type=f32,
-        )
+        total = None
+        for s0 in range(0, slots, 2):
+            tiles = []
+            for s in range(s0, min(s0 + 2, slots)):
+                place = lax.rem(column_ref[r, s] - base + total_panels, total_panels)
+                tiles.append(window[jnp.where(s < count_ref[r], place, 3 * own_panels)])
+            piece = jnp.dot(
+                jnp.concatenate(tiles, axis=1).astype(bf16),
+                blocks_ref[r, s0 : s0 + 2].reshape(len(tiles) * PANEL, PANEL),
+                preferred_element_type=f32,
+            )
+            total = piece if total is None else total + piece
+        out_ref[:, r * PANEL : (r + 1) * PANEL] = total
 
 
 def last_kernel(parts, pos_ref, low_ref, high_ref, *refs):

time: 21.5 us -> 21.5 us (level)
  no operation moved by 1% of the time
where the time goes in v7:
time: 21.5 us; the launch traced here: 21.3 us
  starting transfers between devices  11.6 us (54%)
  waiting for transfers between devices  5.16 us (24%)
  Pallas kernels  2.97 us (14%)
  between operations  0.77 us (4%)
  other arithmetic  0.73 us (3%)
    ppermute x10, starting transfers between devices, swapped(): lax.ppermute(block, axis, [(i, partner(i) % count) for i in range(count)])  11.6 us
    ppermute x10, waiting for transfers between devices, swapped(): lax.ppermute(block, axis, [(i, partner(i) % count) for i in range(count)])  5.16 us
    pallas_call x1, Pallas kernels, per_device(): call(functools.partial(near_kernel, own_panels, total_panels), 'near', [(...  1.09 us
    pallas_call x1, Pallas kernels, per_device(): call(far_kernel, 'far_by_cluster', [((cluster_total * rank_size, row_widt...  0.96 us
    pallas_call x1, Pallas kernels, per_device(): call(functools.partial(last_kernel, parts), 'last', [((local_members, ele...  0.77 us
    add x1, other arithmetic, per_device(): state_next = log_state + time_step * state_rate  0.64 us
  transfers between devices with their start and end apart: 10, of which 4 were waited for; matrix products, arithmetic and copies ran while one was open for 3% of the time, Pallas kernels for 10%

profile of v7, /device:TPU:0, one launch (start us, length us, event | category | flops | bytes accessed | tf_op | source)
XLA Modules:
  0.0 21.3 jit_solution(10312984331489377994)
XLA Ops:
  0.6 0.0 copy-start
  0.6 3.0 %collective-permute-start = (bf16[32,512]{1,0:T(8,128)(2,1)}, bf16[32,512]{1,0:T(8,128)(2,1)S(1)}, u32[]{:S(2)}, u32[]{:S(2)}) collective-permute-start(bf16[32,512]{1,0:T(8,128)(2,1)} %refs_0_.1), channel_id=1, source_target_pairs={{0,1},{1,0},{2,3},{3,2},{4,5},{5,4},{6,7},{7,6},{8,9},{9,8},{10,11... | collective-permute-start | bytes 98312 | tf_op jit(solution)/shard_map/ppermute | solution.py:27
  3.7 0.0 copy-start.2
  3.7 1.0 %far_by_cluster.1.refs_0_ = bf16[128,512]{1,0:T(8,128)(2,1)S(1)} custom-call(s32[4,3]{1,0:T(4,128)} %cluster_ref.1, s32[1]{0:T(128)} %bitcast.1.own_cluster_ref, bf16[4,3,32,128]{3,2,1,0:T(8,128)(2,1)} %basis_ref.1), custom_call_target="tpu_custom_call" | custom-call | flops 1000000000 | bytes 1 | tf_op jit(solution)/shard_map/far_by_cluster/pallas_call | solution.py:163
  4.6 0.0 copy-done
  4.7 0.0 copy-start.1
  4.7 0.0 copy-start.3
  4.7 0.0 copy-start.4
  4.7 0.1 collective-permute-start.4
  4.8 1.0 %collective-permute-done.refs_1_ = bf16[32,512]{1,0:T(8,128)(2,1)S(1)} collective-permute-done((bf16[32,512]{1,0:T(8,128)(2,1)}, bf16[32,512]{1,0:T(8,128)(2,1)S(1)}, u32[]{:S(2)}, u32[]{:S(2)}) %collective-permute-start) | collective-permute-done | bytes 32800 | tf_op jit(solution)/shard_map/ppermute | solution.py:27
  5.8 0.0 copy-done.2
  5.8 0.0 copy-start.5
  5.8 0.0 copy-start.6
  5.8 0.0 copy-start.7
  5.8 0.0 copy-start.8
  5.8 0.0 copy-start.9
  5.8 0.1 partial.1
  5.9 0.0 collective-permute-start.1
  6.0 2.1 %collective-permute-start.8 = (bf16[128,512]{1,0:T(8,128)(2,1)S(1)}, bf16[128,512]{1,0:T(8,128)(2,1)S(1)}, u32[]{:S(2)}, u32[]{:S(2)}) collective-permute-start(bf16[128,512]{1,0:T(8,128)(2,1)S(1)} %far_by_cluster.1.refs_0_), channel_id=1, source_target_pairs={{0,1},{1,0},{2,3},{3,2},{4,5},{5,4},{6,7},{7,6},{8,9},{9,8},{10,11... | collective-permute-start | bytes 393224 | tf_op jit(solution)/shard_map/ppermute | solution.py:27
  8.0 0.0 collective-permute-done.1
  8.0 1.4 %collective-permute-start.2 = (f32[4,32]{1,0:T(4,128)S(1)}, f32[4,32]{1,0:T(4,128)S(1)}, u32[]{:S(2)}, u32[]{:S(2)}) collective-permute-start(f32[4,32]{1,0:T(4,128)S(1)} %add.13), channel_id=1, source_target_pairs={{0,6},{2,4},{4,2},{6,0},{8,14},{10,12},{12,10},{14,8},{16,22},{18,... | collective-permute-start | bytes 1544 | tf_op jit(solution)/shard_map/ppermute | solution.py:27
  9.4 0.0 collective-permute-done.4
  9.4 3.6 %collective-permute-start.6 = (bf16[8,1024]{1,0:T(8,128)(2,1)S(1)}, bf16[8,1024]{1,0:T(8,128)(2,1)S(1)}, u32[]{:S(2)}, u32[]{:S(2)}) collective-permute-start(bf16[8,1024]{1,0:T(8,128)(2,1)S(1)} %pad_maximum_fusion.own_ref), channel_id=1, source_target_pairs={{0,30},{2,4},{4,2},{6,8},{8,6},{10,12},{12,10},{14,16},{16,14},{18... | collective-permute-start | bytes 49160 | tf_op jit(solution)/shard_map/ppermute | solution.py:27
  13.0 0.0 collective-permute-start.5
  13.0 0.0 collective-permute-done.2
  13.0 0.1 collective-permute-start.3
  13.1 2.3 %collective-permute-done.6.far_ref = bf16[8,1024]{1,0:T(8,128)(2,1)S(1)} collective-permute-done((bf16[8,1024]{1,0:T(8,128)(2,1)S(1)}, bf16[8,1024]{1,0:T(8,128)(2,1)S(1)}, u32[]{:S(2)}, u32[]{:S(2)}) %collective-permute-start.6) | collective-permute-done | bytes 16416 | tf_op jit(solution)/shard_map/ppermute | solution.py:27
  15.3 0.0 collective-permute-done.5.near_ref
  15.3 0.0 copy-done.1
  15.3 0.0 copy-done.3
  15.3 0.0 copy-done.4
  15.3 1.1 %near.1 = f32[8,512]{1,0:T(8,128)S(1)} custom-call(s32[4,24]{1,0:T(4,128)S(1)} %copy-done.3, s32[4]{0:T(128)S(1)} %copy-done.4, s32[1]{0:T(128)} %bitcast.2.pos_ref, bf16[8,1024]{1,0:T(8,128)(2,1)S(1)} %pad_maximum_fusion.own_ref, bf16[8,1024]{1,0:T(8,128)(2,1)S(1)} %collective-permute-done.5.near_ref, bf16[8,1024]{1,0:T(8,128)(2,1)S(1)} %collective-permute-done.6.far_ref, ...), custom_call_target="tpu_custom_call" | custom-call | flops 1000000000 | bytes 1 | tf_op jit(solution)/shard_map/near/pallas_call | solution.py:193
  16.5 0.0 collective-permute-done.3
  16.5 0.1 pad_maximum_fusion.1.low_ref
  16.6 0.3 %collective-permute-start.7 = (bf16[4,64]{1,0:T(4,128)(2,1)S(1)}, bf16[4,64]{1,0:T(4,128)(2,1)S(1)}, u32[]{:S(2)}, u32[]{:S(2)}) collective-permute-start(bf16[4,64]{1,0:T(4,128)(2,1)S(1)} %pad_maximum_fusion.1.low_ref), channel_id=1, source_target_pairs={{0,18},{2,16},{4,22},{6,20},{8,26},{10,24},{12,30},{14,28},{16,2},... | collective-permute-start | bytes 1544 | tf_op jit(solution)/shard_map/ppermute | solution.py:27
  16.9 1.1 %collective-permute-start.9 = (f32[4,512]{1,0:T(4,128)S(1)}, f32[4,512]{1,0:T(4,128)S(1)}, u32[]{:S(2)}, u32[]{:S(2)}) collective-permute-start(f32[4,512]{1,0:T(4,128)S(1)} %get-tuple-element.11), channel_id=1, source_target_pairs={{0,1},{1,0},{2,3},{3,2},{4,5},{5,4},{6,7},{7,6},{8,9},{9,8},{10,11... | collective-permute-start | bytes 24584 | tf_op jit(solution)/shard_map/ppermute | solution.py:27
  18.0 0.0 copy-done.5
  18.0 0.0 copy-done.6
  18.0 0.0 copy-done.7
  18.0 0.0 copy-done.8
  18.0 0.0 copy-done.9
  18.0 0.6 %multiply_add_fusion = (f32[4,1024]{1,0:T(4,128)}, f32[4,1024]{1,0:T(4,128)S(1)}, f32[4,1024]{1,0:T(4,128)S(1)}) fusion(f32[4,1024]{1,0:T(4,128)S(1)} %copy-done.5, f32[4,1024]{1,0:T(4,128)S(1)} %copy-done.6, f32[4,1024]{1,0:T(4,128)S(1)} %copy-done, f32[4,1024]{1,0:T(4,128)S(1)} %copy-done.7, f32[4,1024]{1,0:T(4,128)S(1)} %copy-done.8, f32[1024]{0:T(1024)S(1)} %copy-done.9), kind=kLoop, calls=%fused_computation.1 | loop fusion | flops 53248 | bytes 135168 | tf_op jit(solution)/shard_map/add | solution.py:224
  18.6 1.8 %collective-permute-done.7.high_ref = bf16[4,64]{1,0:T(4,128)(2,1)S(1)} collective-permute-done((bf16[4,64]{1,0:T(4,128)(2,1)S(1)}, bf16[4,64]{1,0:T(4,128)(2,1)S(1)}, u32[]{:S(2)}, u32[]{:S(2)}) %collective-permute-start.7) | collective-permute-done | bytes 544 | tf_op jit(solution)/shard_map/ppermute | solution.py:27
  20.5 0.1 collective-permute-done.9.refs_3_
  20.5 0.0 collective-permute-done.8.refs_1_
  20.5 0.8 %last.1 = f32[4,1024]{1,0:T(4,128)} custom-call(s32[1]{0:T(128)} %bitcast.pos_ref, bf16[4,64]{1,0:T(4,128)(2,1)S(1)} %pad_maximum_fusion.1.low_ref, bf16[4,64]{1,0:T(4,128)(2,1)S(1)} %collective-permute-done.7.high_ref, bf16[128,512]{1,0:T(8,128)(2,1)S(1)} %far_by_cluster.1.refs_0_, bf16[128,512]{1,0:T(8,128)(2,1)S(1)} %collective-permute-done.8.refs_1_, ...), custom_call_target="tpu_custom_call" | custom-call | flops 1000000000 | bytes 1 | tf_op jit(solution)/shard_map/last/pallas_call | solution.py:225
  (5 shorter events, 0.0 us)
Async XLA Ops:
  0.6 4.0 %copy-start = (f32[4,1024]{1,0:T(4,128)S(1)}, f32[4,1024]{1,0:T(4,128)}, u32[]{:S(2)}) copy-start(f32[4,1024]{1,0:T(4,128)} %rate_ref) | copy-start | bytes 49156
  0.6 5.1 %collective-permute-start = (bf16[32,512]{1,0:T(8,128)(2,1)}, bf16[32,512]{1,0:T(8,128)(2,1)S(1)}, u32[]{:S(2)}, u32[]{:S(2)}) collective-permute-start(bf16[32,512]{1,0:T(8,128)(2,1)} %refs_0_.1), channel_id=1, source_target_pairs={{0,1},{1,0},{2,3},{3,2},{4,5},{5,4},{6,7},{7,6},{8,9},{9,8},{10,11... | collective-permute-start | bytes 98312 | tf_op jit(solution)/shard_map/ppermute | solution.py:27
  3.7 2.1 %copy-start.2 = (bf16[32,512]{1,0:T(8,128)(2,1)S(1)}, bf16[32,512]{1,0:T(8,128)(2,1)}, u32[]{:S(2)}) copy-start(bf16[32,512]{1,0:T(8,128)(2,1)} %refs_0_.1) | copy-start | bytes 98308
  4.7 10.7 %copy-start.1 = (bf16[4,24,128,128]{3,2,1,0:T(8,128)(2,1)S(1)}, bf16[4,24,128,128]{3,2,1,0:T(8,128)(2,1)}, u32[]{:S(2)}) copy-start(bf16[4,24,128,128]{3,2,1,0:T(8,128)(2,1)} %blocks_ref.1) | copy-start | bytes 9437188
  4.7 10.7 %copy-start.3 = (s32[4,24]{1,0:T(4,128)S(1)}, s32[4,24]{1,0:T(4,128)}, u32[]{:S(2)}) copy-start(s32[4,24]{1,0:T(4,128)} %column_ref.1) | copy-start | bytes 1156
  4.7 10.7 %copy-start.4 = (s32[4]{0:T(128)S(1)}, s32[4]{0:T(128)}, u32[]{:S(2)}) copy-start(s32[4]{0:T(128)} %count_ref.1) | copy-start | bytes 52
  4.7 4.7 %collective-permute-start.4 = (bf16[4,1024]{1,0:T(4,128)(2,1)S(1)}, bf16[4,1024]{1,0:T(4,128)(2,1)S(1)}, u32[]{:S(2)}, u32[]{:S(2)}) collective-permute-start(bf16[4,1024]{1,0:T(4,128)(2,1)S(1)} %deficit.1.deficit_ref), channel_id=1, source_target_pairs={{0,1},{1,0},{2,3},{3,2},{4,5},{5,4},{6,7},{7,6},{8,9},{9,8},{10,11... | collective-permute-start | bytes 24584 | tf_op jit(solution)/shard_map/ppermute | solution.py:27
  5.8 12.2 %copy-start.5 = (f32[4,1024]{1,0:T(4,128)S(1)}, f32[4,1024]{1,0:T(4,128)}, u32[]{:S(2)}) copy-start(f32[4,1024]{1,0:T(4,128)} %param.13) | copy-start | bytes 49156
  5.8 12.2 %copy-start.6 = (f32[4,1024]{1,0:T(4,128)S(1)}, f32[4,1024]{1,0:T(4,128)}, u32[]{:S(2)}) copy-start(f32[4,1024]{1,0:T(4,128)} %param.16) | copy-start | bytes 49156
  5.8 12.2 %copy-start.7 = (f32[4,1024]{1,0:T(4,128)S(1)}, f32[4,1024]{1,0:T(4,128)}, u32[]{:S(2)}) copy-start(f32[4,1024]{1,0:T(4,128)} %param.15) | copy-start | bytes 49156
  5.8 12.2 %copy-start.8 = (f32[4,1024]{1,0:T(4,128)S(1)}, f32[4,1024]{1,0:T(4,128)}, u32[]{:S(2)}) copy-start(f32[4,1024]{1,0:T(4,128)} %param.14) | copy-start | bytes 49156
  5.8 12.2 %copy-start.9 = (f32[1024]{0:T(1024)S(1)}, f32[1024]{0:T(1024)}, u32[]{:S(2)}) copy-start(f32[1024]{0:T(1024)} %param.17) | copy-start | bytes 12292
  5.9 2.1 %collective-permute-start.1 = (f32[4,32]{1,0:T(4,128)S(1)}, f32[4,32]{1,0:T(4,128)S(1)}, u32[]{:S(2)}, u32[]{:S(2)}) collective-permute-start(f32[4,32]{1,0:T(4,128)S(1)} %partial.1), channel_id=1, source_target_pairs={{0,2},{2,0},{4,6},{6,4},{8,10},{10,8},{12,14},{14,12},{16,18},{18,... | collective-permute-start | bytes 1544 | tf_op jit(solution)/shard_map/ppermute | solution.py:27
  6.0 14.6 %collective-permute-start.8 = (bf16[128,512]{1,0:T(8,128)(2,1)S(1)}, bf16[128,512]{1,0:T(8,128)(2,1)S(1)}, u32[]{:S(2)}, u32[]{:S(2)}) collective-permute-start(bf16[128,512]{1,0:T(8,128)(2,1)S(1)} %far_by_cluster.1.refs_0_), channel_id=1, source_target_pairs={{0,1},{1,0},{2,3},{3,2},{4,5},{5,4},{6,7},{7,6},{8,9},{9,8},{10,11... | collective-permute-start | bytes 393224 | tf_op jit(solution)/shard_map/ppermute | solution.py:27
  8.0 4.9 %collective-permute-start.2 = (f32[4,32]{1,0:T(4,128)S(1)}, f32[4,32]{1,0:T(4,128)S(1)}, u32[]{:S(2)}, u32[]{:S(2)}) collective-permute-start(f32[4,32]{1,0:T(4,128)S(1)} %add.13), channel_id=1, source_target_pairs={{0,6},{2,4},{4,2},{6,0},{8,14},{10,12},{12,10},{14,8},{16,22},{18,... | collective-permute-start | bytes 1544 | tf_op jit(solution)/shard_map/ppermute | solution.py:27
  9.4 5.9 %collective-permute-start.6 = (bf16[8,1024]{1,0:T(8,128)(2,1)S(1)}, bf16[8,1024]{1,0:T(8,128)(2,1)S(1)}, u32[]{:S(2)}, u32[]{:S(2)}) collective-permute-start(bf16[8,1024]{1,0:T(8,128)(2,1)S(1)} %pad_maximum_fusion.own_ref), channel_id=1, source_target_pairs={{0,30},{2,4},{4,2},{6,8},{8,6},{10,12},{12,10},{14,16},{16,14},{18... | collective-permute-start | bytes 49160 | tf_op jit(solution)/shard_map/ppermute | solution.py:27
  13.0 2.4 %collective-permute-start.5 = (bf16[8,1024]{1,0:T(8,128)(2,1)S(1)}, bf16[8,1024]{1,0:T(8,128)(2,1)S(1)}, u32[]{:S(2)}, u32[]{:S(2)}) collective-permute-start(bf16[8,1024]{1,0:T(8,128)(2,1)S(1)} %pad_maximum_fusion.own_ref), channel_id=1, source_target_pairs={{0,2},{2,0},{4,6},{6,4},{8,10},{10,8},{12,14},{14,12},{16,18},{18,... | collective-permute-start | bytes 49160 | tf_op jit(solution)/shard_map/ppermute | solution.py:27
  13.0 3.5 %collective-permute-start.3 = (bf16[4,32]{1,0:T(4,128)(2,1)S(1)}, bf16[4,32]{1,0:T(4,128)(2,1)S(1)}, u32[]{:S(2)}, u32[]{:S(2)}) collective-permute-start(bf16[4,32]{1,0:T(4,128)(2,1)S(1)} %add_convert_fusion), channel_id=1, source_target_pairs={{0,10},{2,8},{4,14},{6,12},{8,2},{10,0},{12,6},{14,4},{16,26},{18,... | collective-permute-start | bytes 776 | tf_op jit(solution)/shard_map/ppermute | solution.py:27
  16.6 3.9 %collective-permute-start.7 = (bf16[4,64]{1,0:T(4,128)(2,1)S(1)}, bf16[4,64]{1,0:T(4,128)(2,1)S(1)}, u32[]{:S(2)}, u32[]{:S(2)}) collective-permute-start(bf16[4,64]{1,0:T(4,128)(2,1)S(1)} %pad_maximum_fusion.1.low_ref), channel_id=1, source_target_pairs={{0,18},{2,16},{4,22},{6,20},{8,26},{10,24},{12,30},{14,28},{16,2},... | collective-permute-start | bytes 1544 | tf_op jit(solution)/shard_map/ppermute | solution.py:27
  16.9 3.7 %collective-permute-start.9 = (f32[4,512]{1,0:T(4,128)S(1)}, f32[4,512]{1,0:T(4,128)S(1)}, u32[]{:S(2)}, u32[]{:S(2)}) collective-permute-start(f32[4,512]{1,0:T(4,128)S(1)} %get-tuple-element.11), channel_id=1, source_target_pairs={{0,1},{1,0},{2,3},{3,2},{4,5},{5,4},{6,7},{7,6},{8,9},{9,8},{10,11... | collective-permute-start | bytes 24584 | tf_op jit(solution)/shard_map/ppermute | solution.py:27

commit v8 on v7

--- a/solution.py
+++ b/solution.py
@@ -82,14 +82,14 @@
     base = (pos_ref[0] - 1) * own_panels
     for r in range(rows):
         total = None
-        for s0 in range(0, slots, 2):
+        for s0 in range(0, slots, 4):
             tiles = []
-            for s in range(s0, min(s0 + 2, slots)):
+            for s in range(s0, min(s0 + 4, slots)):
                 place = lax.rem(column_ref[r, s] - base + total_panels, total_panels)
                 tiles.append(window[jnp.where(s < count_ref[r], place, 3 * own_panels)])
             piece = jnp.dot(
                 jnp.concatenate(tiles, axis=1).astype(bf16),
-                blocks_ref[r, s0 : s0 + 2].reshape(len(tiles) * PANEL, PANEL),
+                blocks_ref[r, s0 : s0 + 4].reshape(len(tiles) * PANEL, PANEL),
                 preferred_element_type=f32,
             )
             total = piece if total is None else total + piece

time: 21.5 us -> 21.5 us (level)
  no operation moved by 1% of the time
where the time goes in v8:
time: 21.5 us; the launch traced here: 21.3 us
  starting transfers between devices  11.6 us (54%)
  waiting for transfers between devices  5.15 us (24%)
  Pallas kernels  2.98 us (14%)
  between operations  0.77 us (4%)
  other arithmetic  0.73 us (3%)
    ppermute x10, starting transfers between devices, swapped(): lax.ppermute(block, axis, [(i, partner(i) % count) for i in range(count)])  11.6 us
    ppermute x10, waiting for transfers between devices, swapped(): lax.ppermute(block, axis, [(i, partner(i) % count) for i in range(count)])  5.15 us
    pallas_call x1, Pallas kernels, per_device(): call(functools.partial(near_kernel, own_panels, total_panels), 'near', [(...  1.11 us
    pallas_call x1, Pallas kernels, per_device(): call(far_kernel, 'far_by_cluster', [((cluster_total * rank_size, row_widt...  0.96 us
    pallas_call x1, Pallas kernels, per_device(): call(functools.partial(last_kernel, parts), 'last', [((local_members, ele...  0.77 us
    add x1, other arithmetic, per_device(): state_next = log_state + time_step * state_rate  0.64 us
  transfers between devices with their start and end apart: 10, of which 4 were waited for; matrix products, arithmetic and copies ran while one was open for 3% of the time, Pallas kernels for 10%

profile of v8, /device:TPU:0, one launch (start us, length us, event | category | flops | bytes accessed | tf_op | source)
XLA Modules:
  0.0 21.3 jit_solution(2971665906722311003)
XLA Ops:
  0.6 0.0 copy-start
  0.6 3.0 %collective-permute-start = (bf16[32,512]{1,0:T(8,128)(2,1)}, bf16[32,512]{1,0:T(8,128)(2,1)S(1)}, u32[]{:S(2)}, u32[]{:S(2)}) collective-permute-start(bf16[32,512]{1,0:T(8,128)(2,1)} %refs_0_.1), channel_id=1, source_target_pairs={{0,1},{1,0},{2,3},{3,2},{4,5},{5,4},{6,7},{7,6},{8,9},{9,8},{10,11... | collective-permute-start | bytes 98312 | tf_op jit(solution)/shard_map/ppermute | solution.py:27
  3.7 0.0 copy-start.2
  3.7 1.0 %far_by_cluster.1.refs_0_ = bf16[128,512]{1,0:T(8,128)(2,1)S(1)} custom-call(s32[4,3]{1,0:T(4,128)} %cluster_ref.1, s32[1]{0:T(128)} %bitcast.1.own_cluster_ref, bf16[4,3,32,128]{3,2,1,0:T(8,128)(2,1)} %basis_ref.1), custom_call_target="tpu_custom_call" | custom-call | flops 1000000000 | bytes 1 | tf_op jit(solution)/shard_map/far_by_cluster/pallas_call | solution.py:163
  4.6 0.0 copy-done
  4.7 0.0 copy-start.1
  4.7 0.0 copy-start.3
  4.7 0.0 copy-start.4
  4.7 0.1 collective-permute-start.4
  4.8 1.0 %collective-permute-done.refs_1_ = bf16[32,512]{1,0:T(8,128)(2,1)S(1)} collective-permute-done((bf16[32,512]{1,0:T(8,128)(2,1)}, bf16[32,512]{1,0:T(8,128)(2,1)S(1)}, u32[]{:S(2)}, u32[]{:S(2)}) %collective-permute-start) | collective-permute-done | bytes 32800 | tf_op jit(solution)/shard_map/ppermute | solution.py:27
  5.8 0.0 copy-done.2
  5.8 0.0 copy-start.5
  5.8 0.0 copy-start.6
  5.8 0.0 copy-start.7
  5.8 0.0 copy-start.8
  5.8 0.0 copy-start.9
  5.8 0.1 partial.1
  5.9 0.0 collective-permute-start.1
  6.0 2.1 %collective-permute-start.8 = (bf16[128,512]{1,0:T(8,128)(2,1)S(1)}, bf16[128,512]{1,0:T(8,128)(2,1)S(1)}, u32[]{:S(2)}, u32[]{:S(2)}) collective-permute-start(bf16[128,512]{1,0:T(8,128)(2,1)S(1)} %far_by_cluster.1.refs_0_), channel_id=1, source_target_pairs={{0,1},{1,0},{2,3},{3,2},{4,5},{5,4},{6,7},{7,6},{8,9},{9,8},{10,11... | collective-permute-start | bytes 393224 | tf_op jit(solution)/shard_map/ppermute | solution.py:27
  8.0 0.0 collective-permute-done.1
  8.0 1.4 %collective-permute-start.2 = (f32[4,32]{1,0:T(4,128)S(1)}, f32[4,32]{1,0:T(4,128)S(1)}, u32[]{:S(2)}, u32[]{:S(2)}) collective-permute-start(f32[4,32]{1,0:T(4,128)S(1)} %add.13), channel_id=1, source_target_pairs={{0,6},{2,4},{4,2},{6,0},{8,14},{10,12},{12,10},{14,8},{16,22},{18,... | collective-permute-start | bytes 1544 | tf_op jit(solution)/shard_map/ppermute | solution.py:27
  9.4 0.0 collective-permute-done.4
  9.4 3.6 %collective-permute-start.6 = (bf16[8,1024]{1,0:T(8,128)(2,1)S(1)}, bf16[8,1024]{1,0:T(8,128)(2,1)S(1)}, u32[]{:S(2)}, u32[]{:S(2)}) collective-permute-start(bf16[8,1024]{1,0:T(8,128)(2,1)S(1)} %pad_maximum_fusion.own_ref), channel_id=1, source_target_pairs={{0,30},{2,4},{4,2},{6,8},{8,6},{10,12},{12,10},{14,16},{16,14},{18... | collective-permute-start | bytes 49160 | tf_op jit(solution)/shard_map/ppermute | solution.py:27
  13.0 0.0 collective-permute-start.5
  13.0 0.0 collective-permute-done.2
  13.0 0.1 collective-permute-start.3
  13.1 2.3 %collective-permute-done.6.far_ref = bf16[8,1024]{1,0:T(8,128)(2,1)S(1)} collective-permute-done((bf16[8,1024]{1,0:T(8,128)(2,1)S(1)}, bf16[8,1024]{1,0:T(8,128)(2,1)S(1)}, u32[]{:S(2)}, u32[]{:S(2)}) %collective-permute-start.6) | collective-permute-done | bytes 16416 | tf_op jit(solution)/shard_map/ppermute | solution.py:27
  15.3 0.0 collective-permute-done.5.near_ref
  15.3 0.0 copy-done.1
  15.3 0.0 copy-done.3
  15.3 0.0 copy-done.4
  15.3 1.1 %near.1 = f32[8,512]{1,0:T(8,128)S(1)} custom-call(s32[4,24]{1,0:T(4,128)S(1)} %copy-done.3, s32[4]{0:T(128)S(1)} %copy-done.4, s32[1]{0:T(128)} %bitcast.2.pos_ref, bf16[8,1024]{1,0:T(8,128)(2,1)S(1)} %pad_maximum_fusion.own_ref, bf16[8,1024]{1,0:T(8,128)(2,1)S(1)} %collective-permute-done.5.near_ref, bf16[8,1024]{1,0:T(8,128)(2,1)S(1)} %collective-permute-done.6.far_ref, ...), custom_call_target="tpu_custom_call" | custom-call | flops 1000000000 | bytes 1 | tf_op jit(solution)/shard_map/near/pallas_call | solution.py:193
  16.5 0.0 collective-permute-done.3
  16.5 0.1 pad_maximum_fusion.1.low_ref
  16.6 0.3 %collective-permute-start.7 = (bf16[4,64]{1,0:T(4,128)(2,1)S(1)}, bf16[4,64]{1,0:T(4,128)(2,1)S(1)}, u32[]{:S(2)}, u32[]{:S(2)}) collective-permute-start(bf16[4,64]{1,0:T(4,128)(2,1)S(1)} %pad_maximum_fusion.1.low_ref), channel_id=1, source_target_pairs={{0,18},{2,16},{4,22},{6,20},{8,26},{10,24},{12,30},{14,28},{16,2},... | collective-permute-start | bytes 1544 | tf_op jit(solution)/shard_map/ppermute | solution.py:27
  16.9 1.1 %collective-permute-start.9 = (f32[4,512]{1,0:T(4,128)S(1)}, f32[4,512]{1,0:T(4,128)S(1)}, u32[]{:S(2)}, u32[]{:S(2)}) collective-permute-start(f32[4,512]{1,0:T(4,128)S(1)} %get-tuple-element.11), channel_id=1, source_target_pairs={{0,1},{1,0},{2,3},{3,2},{4,5},{5,4},{6,7},{7,6},{8,9},{9,8},{10,11... | collective-permute-start | bytes 24584 | tf_op jit(solution)/shard_map/ppermute | solution.py:27
  18.0 0.0 copy-done.5
  18.0 0.0 copy-done.6
  18.0 0.0 copy-done.7
  18.0 0.0 copy-done.8
  18.0 0.0 copy-done.9
  18.0 0.6 %multiply_add_fusion = (f32[4,1024]{1,0:T(4,128)}, f32[4,1024]{1,0:T(4,128)S(1)}, f32[4,1024]{1,0:T(4,128)S(1)}) fusion(f32[4,1024]{1,0:T(4,128)S(1)} %copy-done.5, f32[4,1024]{1,0:T(4,128)S(1)} %copy-done.6, f32[4,1024]{1,0:T(4,128)S(1)} %copy-done, f32[4,1024]{1,0:T(4,128)S(1)} %copy-done.7, f32[4,1024]{1,0:T(4,128)S(1)} %copy-done.8, f32[1024]{0:T(1024)S(1)} %copy-done.9), kind=kLoop, calls=%fused_computation.1 | loop fusion | flops 53248 | bytes 135168 | tf_op jit(solution)/shard_map/add | solution.py:224
  18.6 1.8 %collective-permute-done.7.high_ref = bf16[4,64]{1,0:T(4,128)(2,1)S(1)} collective-permute-done((bf16[4,64]{1,0:T(4,128)(2,1)S(1)}, bf16[4,64]{1,0:T(4,128)(2,1)S(1)}, u32[]{:S(2)}, u32[]{:S(2)}) %collective-permute-start.7) | collective-permute-done | bytes 544 | tf_op jit(solution)/shard_map/ppermute | solution.py:27
  20.5 0.1 collective-permute-done.9.refs_3_
  20.5 0.0 collective-permute-done.8.refs_1_
  20.5 0.8 %last.1 = f32[4,1024]{1,0:T(4,128)} custom-call(s32[1]{0:T(128)} %bitcast.pos_ref, bf16[4,64]{1,0:T(4,128)(2,1)S(1)} %pad_maximum_fusion.1.low_ref, bf16[4,64]{1,0:T(4,128)(2,1)S(1)} %collective-permute-done.7.high_ref, bf16[128,512]{1,0:T(8,128)(2,1)S(1)} %far_by_cluster.1.refs_0_, bf16[128,512]{1,0:T(8,128)(2,1)S(1)} %collective-permute-done.8.refs_1_, ...), custom_call_target="tpu_custom_call" | custom-call | flops 1000000000 | bytes 1 | tf_op jit(solution)/shard_map/last/pallas_call | solution.py:225
  (5 shorter events, 0.0 us)
Async XLA Ops:
  0.6 4.0 %copy-start = (f32[4,1024]{1,0:T(4,128)S(1)}, f32[4,1024]{1,0:T(4,128)}, u32[]{:S(2)}) copy-start(f32[4,1024]{1,0:T(4,128)} %rate_ref) | copy-start | bytes 49156
  0.6 5.1 %collective-permute-start = (bf16[32,512]{1,0:T(8,128)(2,1)}, bf16[32,512]{1,0:T(8,128)(2,1)S(1)}, u32[]{:S(2)}, u32[]{:S(2)}) collective-permute-start(bf16[32,512]{1,0:T(8,128)(2,1)} %refs_0_.1), channel_id=1, source_target_pairs={{0,1},{1,0},{2,3},{3,2},{4,5},{5,4},{6,7},{7,6},{8,9},{9,8},{10,11... | collective-permute-start | bytes 98312 | tf_op jit(solution)/shard_map/ppermute | solution.py:27
  3.7 2.1 %copy-start.2 = (bf16[32,512]{1,0:T(8,128)(2,1)S(1)}, bf16[32,512]{1,0:T(8,128)(2,1)}, u32[]{:S(2)}) copy-start(bf16[32,512]{1,0:T(8,128)(2,1)} %refs_0_.1) | copy-start | bytes 98308
  4.7 10.7 %copy-start.1 = (bf16[4,24,128,128]{3,2,1,0:T(8,128)(2,1)S(1)}, bf16[4,24,128,128]{3,2,1,0:T(8,128)(2,1)}, u32[]{:S(2)}) copy-start(bf16[4,24,128,128]{3,2,1,0:T(8,128)(2,1)} %blocks_ref.1) | copy-start | bytes 9437188
  4.7 10.7 %copy-start.3 = (s32[4,24]{1,0:T(4,128)S(1)}, s32[4,24]{1,0:T(4,128)}, u32[]{:S(2)}) copy-start(s32[4,24]{1,0:T(4,128)} %column_ref.1) | copy-start | bytes 1156
  4.7 10.7 %copy-start.4 = (s32[4]{0:T(128)S(1)}, s32[4]{0:T(128)}, u32[]{:S(2)}) copy-start(s32[4]{0:T(128)} %count_ref.1) | copy-start | bytes 52
  4.7 4.7 %collective-permute-start.4 = (bf16[4,1024]{1,0:T(4,128)(2,1)S(1)}, bf16[4,1024]{1,0:T(4,128)(2,1)S(1)}, u32[]{:S(2)}, u32[]{:S(2)}) collective-permute-start(bf16[4,1024]{1,0:T(4,128)(2,1)S(1)} %deficit.1.deficit_ref), channel_id=1, source_target_pairs={{0,1},{1,0},{2,3},{3,2},{4,5},{5,4},{6,7},{7,6},{8,9},{9,8},{10,11... | collective-permute-start | bytes 24584 | tf_op jit(solution)/shard_map/ppermute | solution.py:27
  5.8 12.2 %copy-start.5 = (f32[4,1024]{1,0:T(4,128)S(1)}, f32[4,1024]{1,0:T(4,128)}, u32[]{:S(2)}) copy-start(f32[4,1024]{1,0:T(4,128)} %param.13) | copy-start | bytes 49156
  5.8 12.2 %copy-start.6 = (f32[4,1024]{1,0:T(4,128)S(1)}, f32[4,1024]{1,0:T(4,128)}, u32[]{:S(2)}) copy-start(f32[4,1024]{1,0:T(4,128)} %param.16) | copy-start | bytes 49156
  5.8 12.2 %copy-start.7 = (f32[4,1024]{1,0:T(4,128)S(1)}, f32[4,1024]{1,0:T(4,128)}, u32[]{:S(2)}) copy-start(f32[4,1024]{1,0:T(4,128)} %param.15) | copy-start | bytes 49156
  5.8 12.2 %copy-start.8 = (f32[4,1024]{1,0:T(4,128)S(1)}, f32[4,1024]{1,0:T(4,128)}, u32[]{:S(2)}) copy-start(f32[4,1024]{1,0:T(4,128)} %param.14) | copy-start | bytes 49156
  5.8 12.2 %copy-start.9 = (f32[1024]{0:T(1024)S(1)}, f32[1024]{0:T(1024)}, u32[]{:S(2)}) copy-start(f32[1024]{0:T(1024)} %param.17) | copy-start | bytes 12292
  5.9 2.1 %collective-permute-start.1 = (f32[4,32]{1,0:T(4,128)S(1)}, f32[4,32]{1,0:T(4,128)S(1)}, u32[]{:S(2)}, u32[]{:S(2)}) collective-permute-start(f32[4,32]{1,0:T(4,128)S(1)} %partial.1), channel_id=1, source_target_pairs={{0,2},{2,0},{4,6},{6,4},{8,10},{10,8},{12,14},{14,12},{16,18},{18,... | collective-permute-start | bytes 1544 | tf_op jit(solution)/shard_map/ppermute | solution.py:27
  6.0 14.6 %collective-permute-start.8 = (bf16[128,512]{1,0:T(8,128)(2,1)S(1)}, bf16[128,512]{1,0:T(8,128)(2,1)S(1)}, u32[]{:S(2)}, u32[]{:S(2)}) collective-permute-start(bf16[128,512]{1,0:T(8,128)(2,1)S(1)} %far_by_cluster.1.refs_0_), channel_id=1, source_target_pairs={{0,1},{1,0},{2,3},{3,2},{4,5},{5,4},{6,7},{7,6},{8,9},{9,8},{10,11... | collective-permute-start | bytes 393224 | tf_op jit(solution)/shard_map/ppermute | solution.py:27
  8.0 4.9 %collective-permute-start.2 = (f32[4,32]{1,0:T(4,128)S(1)}, f32[4,32]{1,0:T(4,128)S(1)}, u32[]{:S(2)}, u32[]{:S(2)}) collective-permute-start(f32[4,32]{1,0:T(4,128)S(1)} %add.13), channel_id=1, source_target_pairs={{0,6},{2,4},{4,2},{6,0},{8,14},{10,12},{12,10},{14,8},{16,22},{18,... | collective-permute-start | bytes 1544 | tf_op jit(solution)/shard_map/ppermute | solution.py:27
  9.4 5.9 %collective-permute-start.6 = (bf16[8,1024]{1,0:T(8,128)(2,1)S(1)}, bf16[8,1024]{1,0:T(8,128)(2,1)S(1)}, u32[]{:S(2)}, u32[]{:S(2)}) collective-permute-start(bf16[8,1024]{1,0:T(8,128)(2,1)S(1)} %pad_maximum_fusion.own_ref), channel_id=1, source_target_pairs={{0,30},{2,4},{4,2},{6,8},{8,6},{10,12},{12,10},{14,16},{16,14},{18... | collective-permute-start | bytes 49160 | tf_op jit(solution)/shard_map/ppermute | solution.py:27
  13.0 2.4 %collective-permute-start.5 = (bf16[8,1024]{1,0:T(8,128)(2,1)S(1)}, bf16[8,1024]{1,0:T(8,128)(2,1)S(1)}, u32[]{:S(2)}, u32[]{:S(2)}) collective-permute-start(bf16[8,1024]{1,0:T(8,128)(2,1)S(1)} %pad_maximum_fusion.own_ref), channel_id=1, source_target_pairs={{0,2},{2,0},{4,6},{6,4},{8,10},{10,8},{12,14},{14,12},{16,18},{18,... | collective-permute-start | bytes 49160 | tf_op jit(solution)/shard_map/ppermute | solution.py:27
  13.0 3.5 %collective-permute-start.3 = (bf16[4,32]{1,0:T(4,128)(2,1)S(1)}, bf16[4,32]{1,0:T(4,128)(2,1)S(1)}, u32[]{:S(2)}, u32[]{:S(2)}) collective-permute-start(bf16[4,32]{1,0:T(4,128)(2,1)S(1)} %add_convert_fusion), channel_id=1, source_target_pairs={{0,10},{2,8},{4,14},{6,12},{8,2},{10,0},{12,6},{14,4},{16,26},{18,... | collective-permute-start | bytes 776 | tf_op jit(solution)/shard_map/ppermute | solution.py:27
  16.6 3.9 %collective-permute-start.7 = (bf16[4,64]{1,0:T(4,128)(2,1)S(1)}, bf16[4,64]{1,0:T(4,128)(2,1)S(1)}, u32[]{:S(2)}, u32[]{:S(2)}) collective-permute-start(bf16[4,64]{1,0:T(4,128)(2,1)S(1)} %pad_maximum_fusion.1.low_ref), channel_id=1, source_target_pairs={{0,18},{2,16},{4,22},{6,20},{8,26},{10,24},{12,30},{14,28},{16,2},... | collective-permute-start | bytes 1544 | tf_op jit(solution)/shard_map/ppermute | solution.py:27
  16.9 3.7 %collective-permute-start.9 = (f32[4,512]{1,0:T(4,128)S(1)}, f32[4,512]{1,0:T(4,128)S(1)}, u32[]{:S(2)}, u32[]{:S(2)}) collective-permute-start(f32[4,512]{1,0:T(4,128)S(1)} %get-tuple-element.11), channel_id=1, source_target_pairs={{0,1},{1,0},{2,3},{3,2},{4,5},{5,4},{6,7},{7,6},{8,9},{9,8},{10,11... | collective-permute-start | bytes 24584 | tf_op jit(solution)/shard_map/ppermute | solution.py:27
